TPU v7x, 128 devices: a whole 4x4x4 slice. The times are simulated.
128 devices in a mesh: grp: 4 (over z), term: 32 (over y, x, core).
Axes of the slice: x: 4, y: 4, z: 4, core: 2. Of those that a mesh axis runs over, the one named last changes fastest.
Arguments:
- hidden_states: bfloat16 [65536, 768], P(('grp', 'term')), may hold values from -8 to 8
- lengths: int32 [512], P(('grp', 'term')), may hold values from 32 to 128, as said below
- block_list: int32 [512, 96], P(('grp', 'term')), may hold values from 0 to 128, as said below
- cluster_ids: int32 [512], P(('grp', 'term')), may hold values from 0 to 65535, as said below
- attn_weight: bfloat16 [768, 2304], replicated, may hold values from -4 to 4
- out_weight: bfloat16 [768, 768], replicated, may hold values from -0.21875 to 0.21875
- up_weight: bfloat16 [768, 3072], replicated, may hold values from -0.21875 to 0.21875
- down_weight: bfloat16 [3072, 768], replicated, may hold values from -0.109375 to 0.109375
- head_weight: bfloat16 [768, 768], replicated, may hold values from -0.21875 to 0.21875
- head_gain: float32 [768], replicated, may hold values from 0.1 to 1.9
- vocab_weight: bfloat16 [16384, 768], P('term'), may hold values from -0.21875 to 0.21875
- vocab_bias: bfloat16 [16384], P('term'), may hold values from 0 to 2
- centroids: bfloat16 [65536, 768], P(('grp', 'term')), may hold values from -6 to 6
Outputs:
- sparse_weights: bfloat16 [512, 16384], P('grp', 'term')
- dense_slots: bfloat16 [128, 16, 768], P(('grp', 'term'))
- slot_passage: int32 [128, 16], P(('grp', 'term'))
Inputs may be any that keep to these rules, and one draw needn't show every extreme that they name: `lengths`: the first token of every passage is live; some passage has all 128 tokens live. `block_list`: the live entries of a row are distinct term blocks and come first; the rest equal 128, which names no block. Every row has at least 48 live entries and at least one padding entry. The 4 passages of one device have distinct owners (cluster_ids // 512). No owner has more than 16 passages, and some owner has exactly 16.
All inputs are finite; a program needn't handle non-finite values.
Results may differ from a plain program's by a relative error of at most 0.007.
Values may be sent and summed in bfloat16 or wider, within the bound.
No kernel may reach another device: no remote copies, remote signals or barrier semaphores. Data moves between devices by JAX's collectives and lax.ppermute only.
A program may use at most 128 MiB of HBM per device.

v0:
```python
import functools
import math

import jax
import jax.numpy as jnp
from jax import lax
from jax.experimental import pallas as pl
from jax.experimental.pallas import tpu as pltpu
from jax.sharding import PartitionSpec as P

HEAD = 64
BLOCK = 128
SEQ = 128
CL_DEV = 512
CAP = 16
NX = 4
NY = 4
FCH = 512
EXTRA = 16
META = 128
STEP = 256
PARTS = 1
FILL = -1e30
F32 = jnp.float32
BF16 = jnp.bfloat16
I32 = jnp.int32
VMEM_BYTES = 62 * 1024 * 1024

TAIL = (
    -0.9999988675117493,
    -1.151123285293579,
    -0.4591154456138611,
    -0.05271419882774353,
    0.007333385292440653,
    -0.0003233428578823805,
    -0.00011446241842349991,
    2.508325815142598e-05,
    -1.6903979940252611e-06,
)


def vmem():
    return pl.BlockSpec(memory_space=pltpu.VMEM)


def smem():
    return pl.BlockSpec(memory_space=pltpu.SMEM)


def hbm():
    return pl.BlockSpec(memory_space=pltpu.HBM)


def gelu(x):
    mag = jnp.abs(x)
    power = jnp.full_like(mag, TAIL[-1])
    for coefficient in TAIL[-2::-1]:
        power = power * mag + coefficient
    return jnp.maximum(x, 0.0) - mag * jnp.exp2(power)


def normalize(values):
    width = values.shape[-1]
    center = values - jnp.sum(values, axis=-1, keepdims=True) * (1.0 / width)
    spread = jnp.sum(center * center, axis=-1, keepdims=True) * (1.0 / width)
    return center * lax.rsqrt(spread + 1e-06)


def encode_kernel(
    offset,
    lengths_ref, hidden_hbm, lists_ref, gain_ref, attn_hbm, out_hbm, up_hbm, down_hbm, head_hbm,
    send_ref, dense_ref,
    hidden, attn_v, out_v, up_v, down_v, head_v, joined, context, first, acc, sems,
):
    rows, width = hidden.shape
    passages = rows // SEQ
    pairs = width // 128
    chunks = up_v.shape[0]

    moves = [(hidden_hbm.at[pl.ds(offset * SEQ, rows), :], hidden)]
    for k in range(3):
        moves.append((attn_hbm.at[:, pl.ds(k * width, width)], attn_v.at[k]))
    moves.append((out_hbm, out_v))
    for c in range(chunks):
        moves.append((up_hbm.at[:, pl.ds(c * FCH, FCH)], up_v.at[c]))
        moves.append((down_hbm.at[pl.ds(c * FCH, FCH), :], down_v.at[c]))
    moves.append((head_hbm, head_v))
    dma = [pltpu.make_async_copy(s, d, sems.at[i]) for i, (s, d) in enumerate(moves)]
    for d in dma:
        d.start()

    dma[0].wait()
    for k in range(3):
        dma[1 + k].wait()
        joined[:, k * width : (k + 1) * width] = jnp.dot(
            hidden[...], attn_v[k], preferred_element_type=F32
        ).astype(BF16)

    low = lax.broadcasted_iota(I32, (SEQ, 128), 1) < HEAD
    lane = lax.broadcasted_iota(I32, (2 * SEQ, 128), 1)
    ones = jnp.ones((SEQ, 128), BF16)
    scale = math.log2(math.e) / math.sqrt(HEAD)

    @pl.loop(0, passages)
    def _(p):
        at = pl.ds(pl.multiple_of(p * SEQ, SEQ), SEQ)
        length = lengths_ref[offset + p]
        for h in range(pairs):
            q = joined[at, h * 128 : (h + 1) * 128]
            k = joined[at, width + h * 128 : width + (h + 1) * 128]
            v = joined[at, 2 * width + h * 128 : 2 * width + (h + 1) * 128]
            zero = jnp.zeros_like(q)
            both = jnp.concatenate([jnp.where(low, q, zero), jnp.where(low, zero, q)], axis=0)
            s = lax.dot_general(both, k, (((1,), (1,)), ((), ())), preferred_element_type=F32)
            s = jnp.where(lane < length, s, FILL)
            top = jnp.max(s, axis=-1, keepdims=True)
            e = jnp.exp2((s - top) * scale).astype(BF16)
            o = jnp.dot(e, jnp.concatenate([v, ones], axis=1), preferred_element_type=F32)
            num = jnp.where(low, o[:SEQ, :128], o[SEQ:, :128])
            den = jnp.where(low, o[:SEQ, 128:], o[SEQ:, 128:])
            context[at, h * 128 : (h + 1) * 128] = (num / den).astype(BF16)

    dma[4].wait()
    mixed = hidden[...].astype(F32) + jnp.dot(context[...], out_v[...], preferred_element_type=F32)
    first[...] = normalize(mixed).astype(BF16)
    acc[...] = first[...].astype(F32)
    for c in range(chunks):
        dma[5 + 2 * c].wait()
        dma[6 + 2 * c].wait()
        inner = gelu(jnp.dot(first[...], up_v[c], preferred_element_type=F32)).astype(BF16)
        acc[...] += jnp.dot(inner, down_v[c], preferred_element_type=F32)
    layer_out = normalize(acc[...]).astype(BF16)
    first[...] = layer_out
    dma[5 + 2 * chunks].wait()
    middle = gelu(jnp.dot(layer_out, head_v[...], preferred_element_type=F32))
    acc[...] = normalize(middle) * gain_ref[...]

    row = lax.broadcasted_iota(I32, (SEQ, 1), 0)
    slots = lists_ref.shape[1]
    block_id = lax.broadcasted_iota(I32, (BLOCK, slots), 0)
    send_ref[rows:, :] = jnp.zeros((EXTRA, width), BF16)
    for p in range(passages):
        base = p * SEQ
        send_ref[base : base + SEQ, :] = jnp.where(
            row < lengths_ref[offset + p], acc[base : base + SEQ, :], acc[base : base + 1, :]
        ).astype(BF16)
        dense_ref[p : p + 1, :] = first[base : base + 1, :].astype(F32)
        hit = (lists_ref[offset + p : offset + p + 1, :] == block_id).astype(F32).astype(BF16)
        count = lax.dot_general(
            jnp.ones((8, slots), BF16), hit, (((1,), (1,)), ((), ())), preferred_element_type=F32
        )
        send_ref[rows + p : rows + p + 1, 0:BLOCK] = count[0:1, :].astype(BF16)


def encode(part, hidden, lengths, block_list, gain, attn_w, out_w, up_w, down_w, head_w):
    width = hidden.shape[1]
    passages = lengths.shape[0] // PARTS
    rows = passages * SEQ
    ff = up_w.shape[1]
    chunks = ff // FCH
    flops = 2 * rows * width * (3 * width + width + 2 * ff + width)
    return pl.pallas_call(
        functools.partial(encode_kernel, part * passages),
        out_shape=(
            jax.ShapeDtypeStruct((rows + EXTRA, width), BF16),
            jax.ShapeDtypeStruct((8, width), F32),
        ),
        in_specs=[smem(), hbm(), vmem(), vmem(), hbm(), hbm(), hbm(), hbm(), hbm()],
        out_specs=(vmem(), vmem()),
        scratch_shapes=[
            pltpu.VMEM((rows, width), BF16),
            pltpu.VMEM((3, width, width), BF16),
            pltpu.VMEM((width, width), BF16),
            pltpu.VMEM((chunks, width, FCH), BF16),
            pltpu.VMEM((chunks, FCH, width), BF16),
            pltpu.VMEM((width, width), BF16),
            pltpu.VMEM((rows, 3 * width), BF16),
            pltpu.VMEM((rows, width), BF16),
            pltpu.VMEM((rows, width), BF16),
            pltpu.VMEM((rows, width), F32),
            pltpu.SemaphoreType.DMA((6 + 2 * chunks,)),
        ],
        compiler_params=pltpu.CompilerParams(vmem_limit_bytes=VMEM_BYTES),
        cost_estimate=pl.CostEstimate(
            flops=flops, transcendentals=0, bytes_accessed=2 * width * (5 * width + 2 * ff)
        ),
        name="encode",
    )(lengths, hidden, block_list, gain, attn_w, out_w, up_w, down_w, head_w)


def route_kernel(parts, info_ref, *refs):
    dense, out_ref = refs[:parts], refs[parts]
    devices = out_ref.shape[0]
    width = dense[0].shape[1]
    passages = (info_ref.shape[0] - 1) // parts
    row = lax.broadcasted_iota(I32, (devices, 1), 0)
    lane = lax.broadcasted_iota(I32, (devices, META), 1)
    rows = jnp.zeros((devices, width), F32)
    meta = jnp.zeros((devices, META), I32)
    device = info_ref[0]
    for part in range(parts):
        for p in range(passages):
            cluster = info_ref[1 + part * passages + p]
            owner = lax.div(cluster, CL_DEV)
            local = cluster - owner * CL_DEV
            mine = row == owner
            rows = jnp.where(mine, dense[part][p : p + 1, :], rows)
            high = lax.div(local, 256)
            word = jnp.where(lane == 0, 1, 0)
            word = jnp.where(lane == 1, device, word)
            word = jnp.where(lane == 2, part * passages + p, word)
            word = jnp.where(lane == 3, high, word)
            word = jnp.where(lane == 4, local - high * 256, word)
            meta = jnp.where(mine, word, meta)
    out_ref[:, :width] = rows.astype(BF16)
    out_ref[:, width:] = meta.astype(F32).astype(BF16)


def route(device, cluster_ids, dense, devices):
    width = dense[0].shape[1]
    info = jnp.concatenate([device.reshape(1).astype(I32), cluster_ids])
    return pl.pallas_call(
        functools.partial(route_kernel, len(dense)),
        out_shape=jax.ShapeDtypeStruct((devices, width + META), BF16),
        in_specs=[smem()] + [vmem()] * len(dense),
        out_specs=vmem(),
        name="route",
    )(info, *dense)


def place_kernel(passages, recv_ref, cent_ref, dense_ref, slot_ref):
    devices = recv_ref.shape[0]
    width = dense_ref.shape[1]
    meta = recv_ref[:, width:]
    source = lax.broadcasted_iota(I32, (devices, devices), 0)
    other = lax.broadcasted_iota(I32, (devices, devices), 1)
    before = (other < source).astype(F32).astype(BF16)
    rank = jnp.dot(before, meta, preferred_element_type=F32)[:, 0:1]
    valid = meta[:, 0:1].astype(F32)
    slot = lax.broadcasted_iota(I32, (devices, META), 1).astype(F32)
    chosen = ((rank == slot) & (valid > 0.5)).astype(F32).astype(BF16)
    over = (((0,), (0,)), ((), ()))
    picked = lax.dot_general(chosen, recv_ref[...], over, preferred_element_type=F32)[:CAP]
    filled = picked[:, width : width + 1] > 0.5
    local = picked[:, width + 3 : width + 4] * 256.0 + picked[:, width + 4 : width + 5]
    ids = lax.broadcasted_iota(I32, (CAP, cent_ref.shape[0]), 1).astype(F32)
    lookup = ((ids == local) & filled).astype(F32).astype(BF16)
    center = jnp.dot(lookup, cent_ref[...], preferred_element_type=F32)
    dense_ref[...] = jnp.where(filled, picked[:, :width] - center, 0.0).astype(BF16)
    words = lax.dot_general(meta, chosen, over, preferred_element_type=F32)
    ident = words[1:2, :] * passages + words[2:3, :]
    slot_ref[...] = jnp.where(words[0:1, :] > 0.5, ident, -1.0).astype(I32)


def place(recv, centroids, passages):
    width = centroids.shape[1]
    return pl.pallas_call(
        functools.partial(place_kernel, passages),
        out_shape=(
            jax.ShapeDtypeStruct((CAP, width), BF16),
            jax.ShapeDtypeStruct((1, META), I32),
        ),
        in_specs=[vmem(), vmem()],
        out_specs=(vmem(), vmem()),
        name="place",
    )(recv, centroids)


def score_kernel(groups, shards, base_row, info_ref, *refs):
    tokens = refs[: 2 * groups]
    weights = refs[2 * groups : 2 * groups + shards]
    outs = refs[2 * groups + shards : 2 * groups + 2 * shards]
    tok_v, w_v, tok_sem, w_sem = refs[2 * groups + 2 * shards :]
    rows = tok_v.shape[1] - EXTRA
    passages = rows // SEQ
    terms = w_v.shape[1]
    per_device = terms // BLOCK
    tok_dma = [pltpu.make_async_copy(t, tok_v.at[g], tok_sem.at[g]) for g, t in enumerate(tokens)]
    w_dma = [pltpu.make_async_copy(w, w_v.at[s], w_sem.at[s]) for s, w in enumerate(weights)]
    tok_dma[0].start()
    w_dma[0].start()
    for d in tok_dma[1:]:
        d.start()
    for d in w_dma[1:]:
        d.start()
    core = info_ref[shards]
    source = lax.broadcasted_iota(I32, (BLOCK, terms), 0)
    target = lax.div(lax.broadcasted_iota(I32, (BLOCK, terms), 1), BLOCK)
    row = lax.broadcasted_iota(I32, (8, 1), 0)
    for s in range(shards):
        w_dma[s].wait()
        spread = (source == target + info_ref[s] * per_device).astype(F32).astype(BF16)
        for g in range(groups):
            listed = []
            for c in range(2):
                if s == 0:
                    tok_dma[2 * g + c].wait()
                listed.append(
                    jnp.dot(
                        tok_v[2 * g + c, rows:, 0:BLOCK], spread, preferred_element_type=F32
                    )
                )
            for n in range(terms // STEP):
                at = slice(n * STEP, (n + 1) * STEP)
                tile = jnp.full((8, STEP), FILL, F32)
                for c in range(2):
                    logits = lax.dot_general(
                        tok_v[2 * g + c, :rows, :], w_v[s, at, :], (((1,), (1,)), ((), ())),
                        preferred_element_type=F32,
                    )
                    best = jnp.max(logits.reshape(passages, SEQ, STEP), axis=1)
                    best = jnp.where(listed[c][:passages, at] > 0.5, best, FILL)
                    position = core if c == 0 else 1 - core
                    for p in range(passages):
                        tile = jnp.where(
                            row == position * 4 + base_row + p, best[p : p + 1, :], tile
                        )
                outs[s][g, :, at] = tile


def score(part, info, tokens, weights):
    groups, shards = len(tokens) // 2, len(weights)
    rows, width = tokens[0].shape
    terms = weights[0].shape[0]
    passages = (rows - EXTRA) // SEQ
    flops = 2 * 2 * groups * rows * width * terms * shards
    return pl.pallas_call(
        functools.partial(score_kernel, groups, shards, part * passages),
        out_shape=tuple(
            jax.ShapeDtypeStruct((groups, 8, terms), F32) for _ in range(shards)
        ),
        in_specs=[smem()] + [hbm()] * (2 * groups + shards),
        out_specs=(vmem(),) * shards,
        scratch_shapes=[
            pltpu.VMEM((2 * groups, rows, width), BF16),
            pltpu.VMEM((shards, terms, width), BF16),
            pltpu.SemaphoreType.DMA((2 * groups,)),
            pltpu.SemaphoreType.DMA((shards,)),
        ],
        compiler_params=pltpu.CompilerParams(vmem_limit_bytes=VMEM_BYTES),
        cost_estimate=pl.CostEstimate(
            flops=flops, transcendentals=0, bytes_accessed=shards * terms * width * 2
        ),
        name="score",
    )(info, *tokens, *weights)


def finish_kernel(plan, info_ref, bias_ref, *refs):
    pieces, (out_ref, best) = refs[: len(plan)], refs[len(plan) :]
    y, x = info_ref[0], info_ref[1]
    bias = bias_ref[...].astype(F32)
    seen = set()
    for (dx, dys), piece in zip(plan, pieces):
        for g, dy in enumerate(dys):
            spot = lax.rem(y + dy, NY) * NX + lax.rem(x + dx, NX)
            at = pl.ds(pl.multiple_of(spot * 8, 8), 8)
            if (dx, dy) in seen:
                best[at, :] = jnp.maximum(best[at, :], piece[g])
            else:
                best[at, :] = piece[g]
            seen.add((dx, dy))
    out_ref[...] = jnp.log1p(jnp.maximum(best[...] + bias, 0.0)).astype(BF16)


def finish(info, bias, plan, pieces):
    terms = bias.shape[1]
    rows = NX * NY * 8
    return pl.pallas_call(
        functools.partial(finish_kernel, tuple(plan)),
        out_shape=jax.ShapeDtypeStruct((rows, terms), BF16),
        in_specs=[smem()] + [vmem()] * (1 + len(pieces)),
        out_specs=vmem(),
        scratch_shapes=[pltpu.VMEM((rows, terms), F32)],
        name="finish",
    )(info, bias, *pieces)


def shift(value, dy, dx, swap=False):
    pairs = []
    for y in range(NY):
        for x in range(NX):
            for c in range(2):
                source = (((y + dy) % NY) * NX + (x + dx) % NX) * 2 + (c ^ int(swap))
                pairs.append((source, (y * NX + x) * 2 + c))
    return lax.ppermute(value, "term", pairs)


def body(
    hidden_states,
    lengths,
    block_list,
    cluster_ids,
    attn_weight,
    out_weight,
    up_weight,
    down_weight,
    head_weight,
    head_gain,
    vocab_weight,
    vocab_bias,
    centroids,
):
    term = lax.axis_index("term").astype(I32)
    core = lax.rem(term, 2)
    x = lax.rem(lax.div(term, 2), NX)
    y = lax.div(term, 2 * NX)
    devices = lax.axis_size("grp") * lax.axis_size("term")
    device = lax.axis_index("grp").astype(I32) * lax.axis_size("term") + term
    passages = lengths.shape[0]
    offsets = (0, 1, 3, 2)

    shards = [vocab_weight] + [shift(vocab_weight, 0, d) for d in offsets[1:]]
    info = jnp.stack([(y * NX + lax.rem(x + d, NX)) * 2 + core for d in offsets] + [core])
    gain = head_gain.reshape(1, -1)

    pieces, plan, dense = [], [], []
    sent = []
    for part in range(PARTS):
        payload, rows = encode(
            part, hidden_states, lengths, block_list, gain,
            attn_weight, out_weight, up_weight, down_weight, head_weight,
        )
        dense.append(rows)
        sent.append(payload)

    received = []
    for part in range(PARTS):
        mine = [sent[part]] + [shift(sent[part], d, 0) for d in offsets[1:]]
        other = [shift(m, 0, 0, swap=True) for m in mine]
        received.append((mine, other))

    recv = lax.all_to_all(
        route(device, cluster_ids, dense, devices), ("grp", "term"),
        split_axis=0, concat_axis=0, tiled=True,
    )
    dense_part, slot_part = place(recv, centroids, passages)

    for part in range(PARTS):
        mine, other = received[part]
        for which in ((0,), (1, 2), (3,)):
            tokens = [t for k in which for t in (mine[k], other[k])]
            results = score(part, info, tokens, shards)
            dys = tuple(offsets[k] for k in which)
            for k, d in enumerate(offsets):
                plan.append((((NX - d) % NX), dys))
                pieces.append(results[k] if d == 0 else shift(results[k], 0, (NX - d) % NX))

    sparse = finish(jnp.stack([y, x]), vocab_bias.reshape(1, -1), plan, pieces)
    return (sparse, dense_part[None], slot_part[:, :CAP])


def solution(mesh):
    placed = (
        P(("grp", "term"), None),
        P(("grp", "term")),
        P(("grp", "term"), None),
        P(("grp", "term")),
        P(),
        P(),
        P(),
        P(),
        P(),
        P(),
        P("term", None),
        P("term"),
        P(("grp", "term"), None),
    )
    return jax.shard_map(
        body,
        mesh=mesh,
        in_specs=placed,
        out_specs=(P("grp", "term"), P(("grp", "term"), None, None), P(("grp", "term"), None)),
        check_vma=False,
    )
```

profile of v0, /device:TPU:1, one launch (start us, length us, event | category | flops | bytes accessed | tf_op | source)
XLA Modules:
  0.0 130.8 jit_solution(10839082699506545498)
XLA Ops:
  0.6 3.4 %collective-permute-start.1 = (bf16[512,768]{1,0:T(8,128)(2,1)}, bf16[512,768]{1,0:T(8,128)(2,1)}, u32[]{:S(2)}, u32[]{:S(2)}) collective-permute-start(bf16[512,768]{1,0:T(8,128)(2,1)} %refs_2_.3), channel_id=1, source_target_pairs={{2,0},{3,1},{4,2},{5,3},{6,4},{7,5},{0,6},{1,7},{10,8},{11,9},{12,... | collective-permute-start | bytes 2359304 | tf_op jit(solution)/shard_map/ppermute | solution.py:385
  4.0 0.0 collective-permute-start.2
  4.0 1.3 reshape.18.gain_ref
  5.3 24.4 %encode.1 = (bf16[528,768]{1,0:T(8,128)(2,1)}, f32[8,768]{1,0:T(8,128)}) custom-call(s32[4]{0:T(128)} %lengths_ref.1, bf16[512,768]{1,0:T(8,128)(2,1)} %hidden_hbm.1, s32[4,96]{1,0:T(4,128)} %lists_ref.1, f32[1,768]{1,0:T(1,128)} %reshape.18.gain_ref, bf16[768,2304]{1,0:T(8,128)(2,1)} %attn_hbm.1, bf16[768,768]{1,0:T(8,128)(2,1)} %out_hbm.1, ...), custom_call_target="tpu_custom_call" | custom-call | flops 7851737088 | bytes 15335424 | tf_op jit(solution)/shard_map/encode/pallas_call | solution.py:162
  29.7 3.0 %collective-permute-start.14 = (bf16[528,768]{1,0:T(8,128)(2,1)}, bf16[528,768]{1,0:T(8,128)(2,1)}, u32[]{:S(2)}, u32[]{:S(2)}) collective-permute-start(bf16[528,768]{1,0:T(8,128)(2,1)} %get-tuple-element.19.refs_0_), channel_id=1, source_target_pairs={{16,0},{17,1},{18,2},{19,3},{20,4},{21,5},{22,6},{23,7},{24,8},{25... | collective-permute-start | bytes 2433032 | tf_op jit(solution)/shard_map/ppermute | solution.py:385
  32.7 0.4 collective-permute-start.9
  33.1 2.3 %collective-permute-start.7 = (bf16[528,768]{1,0:T(8,128)(2,1)}, bf16[528,768]{1,0:T(8,128)(2,1)S(1)}, u32[]{:S(2)}, u32[]{:S(2)}) collective-permute-start(bf16[528,768]{1,0:T(8,128)(2,1)} %get-tuple-element.19.refs_0_), channel_id=1, source_target_pairs={{8,0},{9,1},{10,2},{11,3},{12,4},{13,5},{14,6},{15,7},{16,8},{17,9... | collective-permute-start | bytes 2433032 | tf_op jit(solution)/shard_map/ppermute | solution.py:385
  35.3 0.0 collective-permute-done.1.refs_3_.refs_5_
  35.3 1.8 %collective-permute-start = (bf16[528,768]{1,0:T(8,128)(2,1)}, bf16[528,768]{1,0:T(8,128)(2,1)}, u32[]{:S(2)}, u32[]{:S(2)}) collective-permute-start(bf16[528,768]{1,0:T(8,128)(2,1)} %get-tuple-element.19.refs_0_), channel_id=1, source_target_pairs={{1,0},{0,1},{3,2},{2,3},{5,4},{4,5},{7,6},{6,7},{9,8},{8,9},{11,10... | collective-permute-start | bytes 2433032 | tf_op jit(solution)/shard_map/ppermute | solution.py:385
  37.1 0.0 collective-permute-done.2.refs_4_.refs_6_
  37.1 2.0 %collective-permute-start.3 = (bf16[512,768]{1,0:T(8,128)(2,1)}, bf16[512,768]{1,0:T(8,128)(2,1)}, u32[]{:S(2)}, u32[]{:S(2)}) collective-permute-start(bf16[512,768]{1,0:T(8,128)(2,1)} %refs_2_.3), channel_id=1, source_target_pairs={{4,0},{5,1},{6,2},{7,3},{0,4},{1,5},{2,6},{3,7},{12,8},{13,9},{14,... | collective-permute-start | bytes 2359304 | tf_op jit(solution)/shard_map/ppermute | solution.py:385
  39.2 11.1 %collective-permute-done.14.refs_0_ = bf16[528,768]{1,0:T(8,128)(2,1)} collective-permute-done((bf16[528,768]{1,0:T(8,128)(2,1)}, bf16[528,768]{1,0:T(8,128)(2,1)}, u32[]{:S(2)}, u32[]{:S(2)}) %collective-permute-start.14) | collective-permute-done | bytes 811040 | tf_op jit(solution)/shard_map/ppermute | solution.py:385
  50.2 3.3 %collective-permute-start.15 = (bf16[528,768]{1,0:T(8,128)(2,1)}, bf16[528,768]{1,0:T(8,128)(2,1)}, u32[]{:S(2)}, u32[]{:S(2)}) collective-permute-start(bf16[528,768]{1,0:T(8,128)(2,1)} %collective-permute-done.14.refs_0_), channel_id=1, source_target_pairs={{1,0},{0,1},{3,2},{2,3},{5,4},{4,5},{7,6},{6,7},{9,8},{8,9},{11,10... | collective-permute-start | bytes 2433032 | tf_op jit(solution)/shard_map/ppermute | solution.py:385
  53.6 15.3 %collective-permute-done.9.refs_2_ = bf16[528,768]{1,0:T(8,128)(2,1)S(1)} collective-permute-done((bf16[528,768]{1,0:T(8,128)(2,1)}, bf16[528,768]{1,0:T(8,128)(2,1)S(1)}, u32[]{:S(2)}, u32[]{:S(2)}) %collective-permute-start.9) | collective-permute-done | bytes 811040 | tf_op jit(solution)/shard_map/ppermute | solution.py:385
  68.8 0.5 collective-permute-start.10
  69.3 0.4 collective-permute-start.8
  69.7 0.6 pad_add_fusion.1.info_ref
  70.3 1.5 %route.1 = bf16[128,896]{1,0:T(8,128)(2,1)} custom-call(s32[5]{0:T(128)} %pad_add_fusion.1.info_ref, f32[8,768]{1,0:T(8,128)} %get-tuple-element.32.refs_0_), custom_call_target="tpu_custom_call" | custom-call | tf_op jit(solution)/shard_map/route/pallas_call | solution.py:222
  71.8 0.5 broadcast.6
  72.4 1.7 %reduce = bf16[128,896]{1,0:T(8,128)(2,1)S(1)} reduce(bf16[128,1,896]{2,0,1:T(8,128)(2,1)} %bitcast.14, bf16[]{:T(256)} %broadcast.6), dimensions={1}, to_apply=%copy.17.reduce_sub_computation | reduce | bytes 458754 | tf_op jit(solution)/shard_map/all_to_all | solution.py:432
  74.0 0.9 reshape.20
  75.0 9.5 %all-to-all-start = ((bf16[128,2,448]{2,1,0:T(2,128)(2,1)}), bf16[128,2,448]{2,1,0:T(2,128)(2,1)S(1)}, u32[]{:S(2)}, u32[]{:S(2)}) async-start(bf16[128,2,448]{2,1,0:T(2,128)(2,1)} %reshape.20), calls=%async_computation | async-start | bytes 524288 | tf_op jit(solution)/shard_map/all_to_all | solution.py:432
  84.5 0.7 stack.35.info_ref
  85.2 0.0 collective-permute-done.3.refs_5_.refs_7_
  85.2 7.7 %score.3 = (f32[1,8,512]{2,1,0:T(8,128)}, f32[1,8,512]{2,1,0:T(8,128)}, f32[1,8,512]{2,1,0:T(8,128)}, f32[1,8,512]{2,1,0:T(8,128)}) custom-call(s32[5]{0:T(128)} %stack.35.info_ref, bf16[528,768]{1,0:T(8,128)(2,1)} %get-tuple-element.19.refs_0_, bf16[528,768]{1,0:T(8,128)(2,1)} %collective-permute-done.refs_1_, bf16[512,768]{1,0:T(8,128)(2,1)} %refs_2_.3, ...), custom_call_target="tpu_custom_call" | custom-call | flops 3321888768 | bytes 3145728 | tf_op jit(solution)/shard_map/score/pallas_call | solution.py:327
  92.9 1.5 %collective-permute-start.4 = (f32[1,8,512]{2,1,0:T(8,128)}, f32[1,8,512]{2,1,0:T(8,128)S(1)}, u32[]{:S(2)}, u32[]{:S(2)}) collective-permute-start(f32[1,8,512]{2,1,0:T(8,128)} %get-tuple-element.21), channel_id=1, source_target_pairs={{6,0},{7,1},{0,2},{1,3},{2,4},{3,5},{4,6},{5,7},{14,8},{15,9},{8,1... | collective-permute-start | bytes 49160 | tf_op jit(solution)/shard_map/ppermute | solution.py:385
  94.4 1.3 collective-permute-start.5
  95.7 1.7 %collective-permute-start.6 = (f32[1,8,512]{2,1,0:T(8,128)}, f32[1,8,512]{2,1,0:T(8,128)S(1)}, u32[]{:S(2)}, u32[]{:S(2)}) collective-permute-start(f32[1,8,512]{2,1,0:T(8,128)} %get-tuple-element.23), channel_id=1, source_target_pairs={{4,0},{5,1},{6,2},{7,3},{0,4},{1,5},{2,6},{3,7},{12,8},{13,9},{14,... | collective-permute-start | bytes 49160 | tf_op jit(solution)/shard_map/ppermute | solution.py:385
  97.3 7.7 %score.5 = (f32[1,8,512]{2,1,0:T(8,128)}, f32[1,8,512]{2,1,0:T(8,128)}, f32[1,8,512]{2,1,0:T(8,128)}, f32[1,8,512]{2,1,0:T(8,128)}) custom-call(s32[5]{0:T(128)} %stack.35.info_ref, bf16[528,768]{1,0:T(8,128)(2,1)} %collective-permute-done.14.refs_0_, bf16[528,768]{1,0:T(8,128)(2,1)} %collective-permute-done.15.refs_1_, bf16[512,768]{1,0:T(8,128)(2,1)} %refs_2_.3, ...), custom_call_target="tpu_custom_call" | custom-call | flops 3321888768 | bytes 3145728 | tf_op jit(solution)/shard_map/score/pallas_call | solution.py:327
  105.1 0.0 copy-start.9
  105.1 0.6 collective-permute-start.16
  105.7 11.2 %score.4 = (f32[2,8,512]{2,1,0:T(8,128)}, f32[2,8,512]{2,1,0:T(8,128)}, f32[2,8,512]{2,1,0:T(8,128)}, f32[2,8,512]{2,1,0:T(8,128)}) custom-call(s32[5]{0:T(128)} %stack.35.info_ref, bf16[528,768]{1,0:T(8,128)(2,1)} %copy-done.11, bf16[528,768]{1,0:T(8,128)(2,1)} %collective-permute-done.8.refs_1_, bf16[528,768]{1,0:T(8,128)(2,1)} %copy-done.10, ...), custom_call_target="tpu_custom_call" | custom-call | flops 6643777536 | bytes 3145728 | tf_op jit(solution)/shard_map/score/pallas_call | solution.py:327
  116.9 0.8 collective-permute-start.11
  117.6 2.0 %collective-permute-start.12 = (f32[2,8,512]{2,1,0:T(8,128)}, f32[2,8,512]{2,1,0:T(8,128)S(1)}, u32[]{:S(2)}, u32[]{:S(2)}) collective-permute-start(f32[2,8,512]{2,1,0:T(8,128)} %get-tuple-element.26), channel_id=1, source_target_pairs={{2,0},{3,1},{4,2},{5,3},{6,4},{7,5},{0,6},{1,7},{10,8},{11,9},{12,... | collective-permute-start | bytes 98312 | tf_op jit(solution)/shard_map/ppermute | solution.py:385
  119.6 1.0 collective-permute-start.13
  120.7 0.9 collective-permute-start.17
  121.6 1.8 %collective-permute-start.18 = (f32[1,8,512]{2,1,0:T(8,128)S(1)}, f32[1,8,512]{2,1,0:T(8,128)S(1)}, u32[]{:S(2)}, u32[]{:S(2)}) collective-permute-start(f32[1,8,512]{2,1,0:T(8,128)S(1)} %copy-done.12), channel_id=1, source_target_pairs={{4,0},{5,1},{6,2},{7,3},{0,4},{1,5},{2,6},{3,7},{12,8},{13,9},{14,... | collective-permute-start | bytes 49160 | tf_op jit(solution)/shard_map/ppermute | solution.py:385
  123.4 0.6 pad_add_fusion.info_ref
  123.9 0.6 reshape.17.bias_ref
  124.5 0.5 reshape.21
  125.0 0.7 copy.20
  125.7 2.7 %place.1 = (bf16[16,768]{1,0:T(8,128)(2,1)}, s32[1,128]{1,0:T(1,128)}) custom-call(bf16[128,896]{1,0:T(8,128)(2,1)} %bitcast.15, bf16[512,768]{1,0:T(8,128)(2,1)} %cent_ref.1), custom_call_target="tpu_custom_call" | custom-call | tf_op jit(solution)/shard_map/place/pallas_call | solution.py:257
  128.5 0.5 copy-done.7
  129.0 0.0 copy-done.8
  129.0 0.0 copy-done
  129.1 0.0 copy-done.1
  129.1 0.0 copy-done.2
  129.1 1.7 %finish.1 = bf16[128,512]{1,0:T(8,128)(2,1)} custom-call(s32[2]{0:T(128)} %pad_add_fusion.info_ref, bf16[1,512]{1,0:T(2,128)(2,1)} %reshape.17.bias_ref, f32[1,8,512]{2,1,0:T(8,128)} %get-tuple-element.20.refs_0_, f32[1,8,512]{2,1,0:T(8,128)} %copy-done.3, f32[1,8,512]{2,1,0:T(8,128)} %copy-done.4, f32[1,8,512]{2,1,0:T(8,128)} %copy-done.5, ...), custom_call_target="tpu_custom_call" | custom-call | tf_op jit(solution)/shard_map/finish/pallas_call | solution.py:368
  (39 shorter events, 0.1 us)
Async XLA Ops:
  0.6 34.7 %collective-permute-start.1 = (bf16[512,768]{1,0:T(8,128)(2,1)}, bf16[512,768]{1,0:T(8,128)(2,1)}, u32[]{:S(2)}, u32[]{:S(2)}) collective-permute-start(bf16[512,768]{1,0:T(8,128)(2,1)} %refs_2_.3), channel_id=1, source_target_pairs={{2,0},{3,1},{4,2},{5,3},{6,4},{7,5},{0,6},{1,7},{10,8},{11,9},{12,... | collective-permute-start | bytes 2359304 | tf_op jit(solution)/shard_map/ppermute | solution.py:385
  4.0 33.1 %collective-permute-start.2 = (bf16[512,768]{1,0:T(8,128)(2,1)}, bf16[512,768]{1,0:T(8,128)(2,1)}, u32[]{:S(2)}, u32[]{:S(2)}) collective-permute-start(bf16[512,768]{1,0:T(8,128)(2,1)} %refs_2_.3), channel_id=1, source_target_pairs={{6,0},{7,1},{0,2},{1,3},{2,4},{3,5},{4,6},{5,7},{14,8},{15,9},{8,1... | collective-permute-start | bytes 2359304 | tf_op jit(solution)/shard_map/ppermute | solution.py:385
  5.3 64.4 %copy-start.14 = (s32[4]{0:T(128)S(1)}, s32[4]{0:T(128)}, u32[]{:S(2)}) copy-start(s32[4]{0:T(128)} %param.16) | copy-start | bytes 52
  29.7 20.6 %collective-permute-start.14 = (bf16[528,768]{1,0:T(8,128)(2,1)}, bf16[528,768]{1,0:T(8,128)(2,1)}, u32[]{:S(2)}, u32[]{:S(2)}) collective-permute-start(bf16[528,768]{1,0:T(8,128)(2,1)} %get-tuple-element.19.refs_0_), channel_id=1, source_target_pairs={{16,0},{17,1},{18,2},{19,3},{20,4},{21,5},{22,6},{23,7},{24,8},{25... | collective-permute-start | bytes 2433032 | tf_op jit(solution)/shard_map/ppermute | solution.py:385
  32.7 36.2 %collective-permute-start.9 = (bf16[528,768]{1,0:T(8,128)(2,1)}, bf16[528,768]{1,0:T(8,128)(2,1)S(1)}, u32[]{:S(2)}, u32[]{:S(2)}) collective-permute-start(bf16[528,768]{1,0:T(8,128)(2,1)} %get-tuple-element.19.refs_0_), channel_id=1, source_target_pairs={{24,0},{25,1},{26,2},{27,3},{28,4},{29,5},{30,6},{31,7},{0,8},{1,9... | collective-permute-start | bytes 2433032 | tf_op jit(solution)/shard_map/ppermute | solution.py:385
  33.1 36.3 %collective-permute-start.7 = (bf16[528,768]{1,0:T(8,128)(2,1)}, bf16[528,768]{1,0:T(8,128)(2,1)S(1)}, u32[]{:S(2)}, u32[]{:S(2)}) collective-permute-start(bf16[528,768]{1,0:T(8,128)(2,1)} %get-tuple-element.19.refs_0_), channel_id=1, source_target_pairs={{8,0},{9,1},{10,2},{11,3},{12,4},{13,5},{14,6},{15,7},{16,8},{17,9... | collective-permute-start | bytes 2433032 | tf_op jit(solution)/shard_map/ppermute | solution.py:385
  35.3 49.9 %collective-permute-start = (bf16[528,768]{1,0:T(8,128)(2,1)}, bf16[528,768]{1,0:T(8,128)(2,1)}, u32[]{:S(2)}, u32[]{:S(2)}) collective-permute-start(bf16[528,768]{1,0:T(8,128)(2,1)} %get-tuple-element.19.refs_0_), channel_id=1, source_target_pairs={{1,0},{0,1},{3,2},{2,3},{5,4},{4,5},{7,6},{6,7},{9,8},{8,9},{11,10... | collective-permute-start | bytes 2433032 | tf_op jit(solution)/shard_map/ppermute | solution.py:385
  37.1 48.1 %collective-permute-start.3 = (bf16[512,768]{1,0:T(8,128)(2,1)}, bf16[512,768]{1,0:T(8,128)(2,1)}, u32[]{:S(2)}, u32[]{:S(2)}) collective-permute-start(bf16[512,768]{1,0:T(8,128)(2,1)} %refs_2_.3), channel_id=1, source_target_pairs={{4,0},{5,1},{6,2},{7,3},{0,4},{1,5},{2,6},{3,7},{12,8},{13,9},{14,... | collective-permute-start | bytes 2359304 | tf_op jit(solution)/shard_map/ppermute | solution.py:385
  50.2 45.4 %collective-permute-start.15 = (bf16[528,768]{1,0:T(8,128)(2,1)}, bf16[528,768]{1,0:T(8,128)(2,1)}, u32[]{:S(2)}, u32[]{:S(2)}) collective-permute-start(bf16[528,768]{1,0:T(8,128)(2,1)} %collective-permute-done.14.refs_0_), channel_id=1, source_target_pairs={{1,0},{0,1},{3,2},{2,3},{5,4},{4,5},{7,6},{6,7},{9,8},{8,9},{11,10... | collective-permute-start | bytes 2433032 | tf_op jit(solution)/shard_map/ppermute | solution.py:385
  68.8 24.1 %copy-start.10 = (bf16[528,768]{1,0:T(8,128)(2,1)}, bf16[528,768]{1,0:T(8,128)(2,1)S(1)}, u32[]{:S(2)}) copy-start(bf16[528,768]{1,0:T(8,128)(2,1)S(1)} %collective-permute-done.9.refs_2_) | copy-start | bytes 2433028
  68.8 36.2 %collective-permute-start.10 = (bf16[528,768]{1,0:T(8,128)(2,1)S(1)}, bf16[528,768]{1,0:T(8,128)(2,1)}, u32[]{:S(2)}, u32[]{:S(2)}) collective-permute-start(bf16[528,768]{1,0:T(8,128)(2,1)S(1)} %collective-permute-done.9.refs_2_), channel_id=1, source_target_pairs={{1,0},{0,1},{3,2},{2,3},{5,4},{4,5},{7,6},{6,7},{9,8},{8,9},{11,10... | collective-permute-start | bytes 2433032 | tf_op jit(solution)/shard_map/ppermute | solution.py:385
  69.3 23.6 %copy-start.11 = (bf16[528,768]{1,0:T(8,128)(2,1)}, bf16[528,768]{1,0:T(8,128)(2,1)S(1)}, u32[]{:S(2)}) copy-start(bf16[528,768]{1,0:T(8,128)(2,1)S(1)} %collective-permute-done.7.refs_0_) | copy-start | bytes 2433028
  69.3 36.4 %collective-permute-start.8 = (bf16[528,768]{1,0:T(8,128)(2,1)S(1)}, bf16[528,768]{1,0:T(8,128)(2,1)}, u32[]{:S(2)}, u32[]{:S(2)}) collective-permute-start(bf16[528,768]{1,0:T(8,128)(2,1)S(1)} %collective-permute-done.7.refs_0_), channel_id=1, source_target_pairs={{1,0},{0,1},{3,2},{2,3},{5,4},{4,5},{7,6},{6,7},{9,8},{8,9},{11,10... | collective-permute-start | bytes 2433032 | tf_op jit(solution)/shard_map/ppermute | solution.py:385
  75.0 49.6 %all-to-all-start = ((bf16[128,2,448]{2,1,0:T(2,128)(2,1)}), bf16[128,2,448]{2,1,0:T(2,128)(2,1)S(1)}, u32[]{:S(2)}, u32[]{:S(2)}) async-start(bf16[128,2,448]{2,1,0:T(2,128)(2,1)} %reshape.20), calls=%async_computation | async-start | bytes 524288 | tf_op jit(solution)/shard_map/all_to_all | solution.py:432
  92.9 24.7 %collective-permute-start.4 = (f32[1,8,512]{2,1,0:T(8,128)}, f32[1,8,512]{2,1,0:T(8,128)S(1)}, u32[]{:S(2)}, u32[]{:S(2)}) collective-permute-start(f32[1,8,512]{2,1,0:T(8,128)} %get-tuple-element.21), channel_id=1, source_target_pairs={{6,0},{7,1},{0,2},{1,3},{2,4},{3,5},{4,6},{5,7},{14,8},{15,9},{8,1... | collective-permute-start | bytes 49160 | tf_op jit(solution)/shard_map/ppermute | solution.py:385
  94.4 25.3 %collective-permute-start.5 = (f32[1,8,512]{2,1,0:T(8,128)}, f32[1,8,512]{2,1,0:T(8,128)S(1)}, u32[]{:S(2)}, u32[]{:S(2)}) collective-permute-start(f32[1,8,512]{2,1,0:T(8,128)} %get-tuple-element.22), channel_id=1, source_target_pairs={{2,0},{3,1},{4,2},{5,3},{6,4},{7,5},{0,6},{1,7},{10,8},{11,9},{12,... | collective-permute-start | bytes 49160 | tf_op jit(solution)/shard_map/ppermute | solution.py:385
  95.7 25.0 %collective-permute-start.6 = (f32[1,8,512]{2,1,0:T(8,128)}, f32[1,8,512]{2,1,0:T(8,128)S(1)}, u32[]{:S(2)}, u32[]{:S(2)}) collective-permute-start(f32[1,8,512]{2,1,0:T(8,128)} %get-tuple-element.23), channel_id=1, source_target_pairs={{4,0},{5,1},{6,2},{7,3},{0,4},{1,5},{2,6},{3,7},{12,8},{13,9},{14,... | collective-permute-start | bytes 49160 | tf_op jit(solution)/shard_map/ppermute | solution.py:385
  105.1 15.6 %copy-start.13 = (f32[1,8,512]{2,1,0:T(8,128)S(1)}, f32[1,8,512]{2,1,0:T(8,128)}, u32[]{:S(2)}) copy-start(f32[1,8,512]{2,1,0:T(8,128)} %get-tuple-element.30) | copy-start | bytes 49156
  105.1 16.5 %copy-start.12 = (f32[1,8,512]{2,1,0:T(8,128)S(1)}, f32[1,8,512]{2,1,0:T(8,128)}, u32[]{:S(2)}) copy-start(f32[1,8,512]{2,1,0:T(8,128)} %get-tuple-element.31) | copy-start | bytes 49156
  105.1 18.9 %copy-start.9 = (bf16[512]{0:T(512)(128)(2,1)S(1)}, bf16[512]{0:T(512)(128)(2,1)}, u32[]{:S(2)}) copy-start(bf16[512]{0:T(512)(128)(2,1)} %param.24) | copy-start | bytes 3076
  105.1 16.5 %collective-permute-start.16 = (f32[1,8,512]{2,1,0:T(8,128)}, f32[1,8,512]{2,1,0:T(8,128)S(1)}, u32[]{:S(2)}, u32[]{:S(2)}) collective-permute-start(f32[1,8,512]{2,1,0:T(8,128)} %get-tuple-element.29), channel_id=1, source_target_pairs={{6,0},{7,1},{0,2},{1,3},{2,4},{3,5},{4,6},{5,7},{14,8},{15,9},{8,1... | collective-permute-start | bytes 49160 | tf_op jit(solution)/shard_map/ppermute | solution.py:385
  116.9 11.6 %collective-permute-start.11 = (f32[2,8,512]{2,1,0:T(8,128)}, f32[2,8,512]{2,1,0:T(8,128)S(1)}, u32[]{:S(2)}, u32[]{:S(2)}) collective-permute-start(f32[2,8,512]{2,1,0:T(8,128)} %get-tuple-element.25), channel_id=1, source_target_pairs={{6,0},{7,1},{0,2},{1,3},{2,4},{3,5},{4,6},{5,7},{14,8},{15,9},{8,1... | collective-permute-start | bytes 98312 | tf_op jit(solution)/shard_map/ppermute | solution.py:385
  117.6 10.9 %copy-start.3 = (f32[1,8,512]{2,1,0:T(8,128)}, f32[1,8,512]{2,1,0:T(8,128)S(1)}, u32[]{:S(2)}) copy-start(f32[1,8,512]{2,1,0:T(8,128)S(1)} %collective-permute-done.4.refs_1_) | copy-start | bytes 49156
  117.6 10.8 %collective-permute-start.12 = (f32[2,8,512]{2,1,0:T(8,128)}, f32[2,8,512]{2,1,0:T(8,128)S(1)}, u32[]{:S(2)}, u32[]{:S(2)}) collective-permute-start(f32[2,8,512]{2,1,0:T(8,128)} %get-tuple-element.26), channel_id=1, source_target_pairs={{2,0},{3,1},{4,2},{5,3},{6,4},{7,5},{0,6},{1,7},{10,8},{11,9},{12,... | collective-permute-start | bytes 98312 | tf_op jit(solution)/shard_map/ppermute | solution.py:385
  119.6 8.9 %copy-start.4 = (f32[1,8,512]{2,1,0:T(8,128)}, f32[1,8,512]{2,1,0:T(8,128)S(1)}, u32[]{:S(2)}) copy-start(f32[1,8,512]{2,1,0:T(8,128)S(1)} %collective-permute-done.5.refs_2_) | copy-start | bytes 49156
  119.6 8.8 %collective-permute-start.13 = (f32[2,8,512]{2,1,0:T(8,128)}, f32[2,8,512]{2,1,0:T(8,128)S(1)}, u32[]{:S(2)}, u32[]{:S(2)}) collective-permute-start(f32[2,8,512]{2,1,0:T(8,128)} %get-tuple-element.27), channel_id=1, source_target_pairs={{4,0},{5,1},{6,2},{7,3},{0,4},{1,5},{2,6},{3,7},{12,8},{13,9},{14,... | collective-permute-start | bytes 98312 | tf_op jit(solution)/shard_map/ppermute | solution.py:385
  120.6 7.9 %copy-start.5 = (f32[1,8,512]{2,1,0:T(8,128)}, f32[1,8,512]{2,1,0:T(8,128)S(1)}, u32[]{:S(2)}) copy-start(f32[1,8,512]{2,1,0:T(8,128)S(1)} %collective-permute-done.6.refs_3_) | copy-start | bytes 49156
  120.7 7.8 %collective-permute-start.17 = (f32[1,8,512]{2,1,0:T(8,128)S(1)}, f32[1,8,512]{2,1,0:T(8,128)S(1)}, u32[]{:S(2)}, u32[]{:S(2)}) collective-permute-start(f32[1,8,512]{2,1,0:T(8,128)S(1)} %copy-done.13), channel_id=1, source_target_pairs={{2,0},{3,1},{4,2},{5,3},{6,4},{7,5},{0,6},{1,7},{10,8},{11,9},{12,... | collective-permute-start | bytes 49160 | tf_op jit(solution)/shard_map/ppermute | solution.py:385
  121.6 6.9 %copy-start.6 = (f32[1,8,512]{2,1,0:T(8,128)}, f32[1,8,512]{2,1,0:T(8,128)S(1)}, u32[]{:S(2)}) copy-start(f32[1,8,512]{2,1,0:T(8,128)S(1)} %collective-permute-done.16.refs_9_) | copy-start | bytes 49156
  121.6 6.8 %collective-permute-start.18 = (f32[1,8,512]{2,1,0:T(8,128)S(1)}, f32[1,8,512]{2,1,0:T(8,128)S(1)}, u32[]{:S(2)}, u32[]{:S(2)}) collective-permute-start(f32[1,8,512]{2,1,0:T(8,128)S(1)} %copy-done.12), channel_id=1, source_target_pairs={{4,0},{5,1},{6,2},{7,3},{0,4},{1,5},{2,6},{3,7},{12,8},{13,9},{14,... | collective-permute-start | bytes 49160 | tf_op jit(solution)/shard_map/ppermute | solution.py:385
  128.4 0.6 copy-start.7
  128.4 0.6 copy-start.8
  128.4 0.6 copy-start
  128.5 0.6 copy-start.1
  128.5 0.6 copy-start.2
where the time goes:
time: 133 us; the launch traced here: 131 us
  Pallas kernels  56.9 us (43%)
  starting transfers between devices  38.1 us (29%)
  waiting for transfers between devices  26.4 us (20%)
  local copies, waits for them, and re-layouts  5.78 us (4%)
  other arithmetic  2.84 us (2%)
    ppermute x19, starting transfers between devices, shift(): return lax.ppermute(value, 'term', pairs)  28.6 us
    pallas_call x3, Pallas kernels, score(): pl.pallas_call(functools.partial(score_kernel, groups, shards, part * pas...  26.6 us
    ppermute x19, waiting for transfers between devices, shift(): return lax.ppermute(value, 'term', pairs)  26.4 us
    pallas_call x1, Pallas kernels, encode(): pl.pallas_call(functools.partial(encode_kernel, part * passages), out_sha...  24.4 us
    all_to_all x1, starting transfers between devices, body(): lax.all_to_all(route(device, cluster_ids, dense, devices), ('grp', 'term'...  9.5 us
    unnamed x33, local copies, waits for them, and re-layouts  2.73 us
    pallas_call x1, Pallas kernels, place(): pl.pallas_call(functools.partial(place_kernel, passages), out_shape=(jax....  2.67 us
  transfers between devices with their start and end apart: 20, of which 2 were waited for; matrix products, arithmetic and copies ran while one was open for 6% of the time, Pallas kernels for 42%

commit v1 on v0

v1 whole, which is shorter than its diff:
```python
import functools
import math

import jax
import jax.numpy as jnp
from jax import lax
from jax.experimental import pallas as pl
from jax.experimental.pallas import tpu as pltpu
from jax.sharding import PartitionSpec as P

HEAD = 64
BLOCK = 128
SEQ = 128
CL_DEV = 512
CAP = 16
NX = 4
NY = 4
FCH = 512
EXTRA = 16
META = 128
STEP = 256
PARTS = 2
OFFSETS = (0, 1, 3, 2)
PEERS = tuple((dx, dc) for dx in OFFSETS for dc in (0, 1))
FILL = -1e30
F32 = jnp.float32
BF16 = jnp.bfloat16
I32 = jnp.int32
VMEM_BYTES = 62 * 1024 * 1024

TAIL = (
    -0.9999988675117493,
    -1.151123285293579,
    -0.4591154456138611,
    -0.05271419882774353,
    0.007333385292440653,
    -0.0003233428578823805,
    -0.00011446241842349991,
    2.508325815142598e-05,
    -1.6903979940252611e-06,
)


def vmem():
    return pl.BlockSpec(memory_space=pltpu.VMEM)


def smem():
    return pl.BlockSpec(memory_space=pltpu.SMEM)


def hbm():
    return pl.BlockSpec(memory_space=pltpu.HBM)


def gelu(x):
    mag = jnp.abs(x)
    power = jnp.full_like(mag, TAIL[-1])
    for coefficient in TAIL[-2::-1]:
        power = power * mag + coefficient
    return jnp.maximum(x, 0.0) - mag * jnp.exp2(power)


def normalize(values):
    width = values.shape[-1]
    center = values - jnp.sum(values, axis=-1, keepdims=True) * (1.0 / width)
    spread = jnp.sum(center * center, axis=-1, keepdims=True) * (1.0 / width)
    return center * lax.rsqrt(spread + 1e-06)


def attend_kernel(
    lengths_ref, hidden_hbm, attn_hbm, out_hbm, first_ref,
    hidden, attn_v, out_v, joined, context, sems,
):
    rows, width = hidden.shape
    passages = rows // SEQ
    pairs = width // 128
    moves = [(hidden_hbm, hidden)]
    for k in range(3):
        moves.append((attn_hbm.at[:, pl.ds(k * width, width)], attn_v.at[k]))
    moves.append((out_hbm, out_v))
    dma = [pltpu.make_async_copy(s, d, sems.at[i]) for i, (s, d) in enumerate(moves)]
    for d in dma:
        d.start()
    dma[0].wait()
    for k in range(3):
        dma[1 + k].wait()
        joined[:, k * width : (k + 1) * width] = jnp.dot(
            hidden[...], attn_v[k], preferred_element_type=F32
        ).astype(BF16)

    low = lax.broadcasted_iota(I32, (SEQ, 128), 1) < HEAD
    lane = lax.broadcasted_iota(I32, (2 * SEQ, 128), 1)
    ones = jnp.ones((SEQ, 128), BF16)
    scale = math.log2(math.e) / math.sqrt(HEAD)

    @pl.loop(0, passages)
    def _(p):
        at = pl.ds(pl.multiple_of(p * SEQ, SEQ), SEQ)
        length = lengths_ref[p]
        for h in range(pairs):
            q = joined[at, h * 128 : (h + 1) * 128]
            k = joined[at, width + h * 128 : width + (h + 1) * 128]
            v = joined[at, 2 * width + h * 128 : 2 * width + (h + 1) * 128]
            zero = jnp.zeros_like(q)
            both = jnp.concatenate([jnp.where(low, q, zero), jnp.where(low, zero, q)], axis=0)
            s = lax.dot_general(both, k, (((1,), (1,)), ((), ())), preferred_element_type=F32)
            s = jnp.where(lane < length, s, FILL)
            top = jnp.max(s, axis=-1, keepdims=True)
            e = jnp.exp2((s - top) * scale).astype(BF16)
            o = jnp.dot(e, jnp.concatenate([v, ones], axis=1), preferred_element_type=F32)
            num = jnp.where(low, o[:SEQ, :128], o[SEQ:, :128])
            den = jnp.where(low, o[:SEQ, 128:], o[SEQ:, 128:])
            context[at, h * 128 : (h + 1) * 128] = (num / den).astype(BF16)

    dma[4].wait()
    mixed = hidden[...].astype(F32) + jnp.dot(context[...], out_v[...], preferred_element_type=F32)
    first_ref[...] = normalize(mixed).astype(BF16)


def attend(hidden, lengths, attn_w, out_w):
    rows, width = hidden.shape
    return pl.pallas_call(
        attend_kernel,
        out_shape=jax.ShapeDtypeStruct((rows, width), BF16),
        in_specs=[smem(), hbm(), hbm(), hbm()],
        out_specs=vmem(),
        scratch_shapes=[
            pltpu.VMEM((rows, width), BF16),
            pltpu.VMEM((3, width, width), BF16),
            pltpu.VMEM((width, width), BF16),
            pltpu.VMEM((rows, 3 * width), BF16),
            pltpu.VMEM((rows, width), BF16),
            pltpu.SemaphoreType.DMA((5,)),
        ],
        compiler_params=pltpu.CompilerParams(vmem_limit_bytes=VMEM_BYTES),
        cost_estimate=pl.CostEstimate(
            flops=2 * rows * width * 4 * width, transcendentals=0, bytes_accessed=8 * width * width
        ),
        name="attend",
    )(lengths, hidden, attn_w, out_w)


def forward_kernel(
    offset,
    lengths_ref, first_hbm, lists_ref, gain_ref, up_hbm, down_hbm, head_hbm,
    send_ref, dense_ref,
    first, up_v, down_v, head_v, wide, acc, sems,
):
    rows, width = first.shape
    passages = rows // SEQ
    chunks = up_v.shape[0]
    moves = [(first_hbm.at[pl.ds(offset * SEQ, rows), :], first)]
    for c in range(chunks):
        moves.append((up_hbm.at[:, pl.ds(c * FCH, FCH)], up_v.at[c]))
    moves.append((down_hbm, down_v))
    moves.append((head_hbm, head_v))
    dma = [pltpu.make_async_copy(s, d, sems.at[i]) for i, (s, d) in enumerate(moves)]
    for d in dma:
        d.start()

    def up(c):
        dma[1 + c].wait()
        return jnp.dot(first[...], up_v[c], preferred_element_type=F32)

    dma[0].wait()
    current = up(0)
    for c in range(chunks):
        following = up(c + 1) if c + 1 < chunks else None
        wide[:, c * FCH : (c + 1) * FCH] = gelu(current).astype(BF16)
        current = following
    dma[1 + chunks].wait()
    second = first[...].astype(F32) + jnp.dot(
        wide[...], down_v[...], preferred_element_type=F32
    )
    layer_out = normalize(second).astype(BF16)
    first[...] = layer_out
    dma[2 + chunks].wait()
    middle = gelu(jnp.dot(layer_out, head_v[...], preferred_element_type=F32))
    acc[...] = normalize(middle) * gain_ref[...].reshape(1, width)

    row = lax.broadcasted_iota(I32, (SEQ, 1), 0)
    slots = lists_ref.shape[1]
    block_id = lax.broadcasted_iota(I32, (BLOCK, slots), 0)
    send_ref[rows:, :] = jnp.zeros((EXTRA, width), BF16)
    for p in range(passages):
        base = p * SEQ
        send_ref[base : base + SEQ, :] = jnp.where(
            row < lengths_ref[offset + p], acc[base : base + SEQ, :], acc[base : base + 1, :]
        ).astype(BF16)
        dense_ref[p : p + 1, :] = first[base : base + 1, :].astype(F32)
        hit = (lists_ref[offset + p : offset + p + 1, :] == block_id).astype(F32).astype(BF16)
        count = lax.dot_general(
            jnp.ones((8, slots), BF16), hit, (((1,), (1,)), ((), ())), preferred_element_type=F32
        )
        send_ref[rows + p : rows + p + 1, 0:BLOCK] = count[0:1, :].astype(BF16)


def forward(part, first, lengths, block_list, gain, up_w, down_w, head_w):
    width = first.shape[1]
    passages = lengths.shape[0] // PARTS
    rows = passages * SEQ
    ff = up_w.shape[1]
    chunks = ff // FCH
    return pl.pallas_call(
        functools.partial(forward_kernel, part * passages),
        out_shape=(
            jax.ShapeDtypeStruct((rows + EXTRA, width), BF16),
            jax.ShapeDtypeStruct((8, width), F32),
        ),
        in_specs=[smem(), hbm(), vmem(), vmem(), hbm(), hbm(), hbm()],
        out_specs=(vmem(), vmem()),
        scratch_shapes=[
            pltpu.VMEM((rows, width), BF16),
            pltpu.VMEM((chunks, width, FCH), BF16),
            pltpu.VMEM((ff, width), BF16),
            pltpu.VMEM((width, width), BF16),
            pltpu.VMEM((rows, ff), BF16),
            pltpu.VMEM((rows, width), F32),
            pltpu.SemaphoreType.DMA((3 + chunks,)),
        ],
        compiler_params=pltpu.CompilerParams(vmem_limit_bytes=VMEM_BYTES),
        cost_estimate=pl.CostEstimate(flops=1, transcendentals=0, bytes_accessed=1),
        name="forward",
    )(lengths, first, block_list, gain, up_w, down_w, head_w)


def here():
    term = lax.axis_index("term").astype(I32)
    chip = lax.div(term, 2)
    return lax.div(chip, NX), lax.rem(chip, NX), lax.rem(term, 2)


def route_kernel(parts, clusters_ref, *refs):
    dense, out_ref = refs[:parts], refs[parts]
    devices = out_ref.shape[0]
    pieces = dense[0].shape[1] // META
    passages = clusters_ref.shape[0] // parts
    row = lax.broadcasted_iota(I32, (devices, 1), 0)
    lane = lax.broadcasted_iota(I32, (devices, META), 1)
    term = lax.axis_index("term").astype(I32)
    device = lax.axis_index("grp").astype(I32) * lax.axis_size("term") + term
    rows = [jnp.zeros((devices, META), F32) for _ in range(pieces)]
    meta = jnp.zeros((devices, META), I32)
    for part in range(parts):
        for p in range(passages):
            cluster = clusters_ref[part * passages + p]
            owner = lax.div(cluster, CL_DEV)
            mine = row == owner
            for k in range(pieces):
                piece = dense[part][p : p + 1, k * META : (k + 1) * META]
                rows[k] = jnp.where(mine, piece, rows[k])
            word = jnp.where(lane == 0, 1, 0)
            word = jnp.where(lane == 1, device, word)
            word = jnp.where(lane == 2, part * passages + p, word)
            word = jnp.where(lane == 3, cluster - owner * CL_DEV, word)
            meta = jnp.where(mine, word, meta)
    for k in range(pieces):
        out_ref[:, k, :] = rows[k]
    out_ref[:, pieces, :] = meta.astype(F32)
    out_ref[:, pieces + 1, :] = jnp.zeros((devices, META), F32)


def route(cluster_ids, dense, devices):
    return pl.pallas_call(
        functools.partial(route_kernel, len(dense)),
        out_shape=jax.ShapeDtypeStruct((devices, 8, META), F32),
        in_specs=[smem()] + [vmem()] * len(dense),
        out_specs=vmem(),
        cost_estimate=pl.CostEstimate(flops=1, transcendentals=0, bytes_accessed=1),
        name="route",
    )(cluster_ids, *dense)


def place_kernel(passages, recv_ref, cent_ref, dense_ref, slot_ref):
    devices = recv_ref.shape[0]
    width = dense_ref.shape[1]
    pieces = width // META
    words = recv_ref[:, pieces, :]
    high = jnp.floor(words * (1.0 / 256.0))
    meta = words.astype(BF16)
    source = lax.broadcasted_iota(I32, (devices, devices), 0)
    other = lax.broadcasted_iota(I32, (devices, devices), 1)
    before = (other < source).astype(F32).astype(BF16)
    valid = words[:, 0:1]
    rank = jnp.dot(before, meta, preferred_element_type=F32)[:, 0:1]
    slot = lax.broadcasted_iota(I32, (devices, META), 1).astype(F32)
    chosen = ((rank == slot) & (valid > 0.5)).astype(F32).astype(BF16)
    over = (((0,), (0,)), ((), ()))

    def pick(values):
        return lax.dot_general(
            chosen, values.astype(BF16), over, preferred_element_type=F32
        )[:CAP]

    small = pick(words - high * 256.0)
    large = pick(high)
    filled = small[:, 0:1] > 0.5
    local = (small + large * 256.0)[:, 3:4]
    ids = lax.broadcasted_iota(I32, (CAP, cent_ref.shape[0]), 1).astype(F32)
    lookup = ((ids == local) & filled).astype(F32).astype(BF16)
    center = jnp.dot(lookup, cent_ref[...], preferred_element_type=F32)
    for k in range(pieces):
        at = slice(k * META, (k + 1) * META)
        dense_ref[:, at] = jnp.where(
            filled, pick(recv_ref[:, k, :]) - center[:, at], 0.0
        ).astype(BF16)
    names = lax.dot_general(meta, chosen, over, preferred_element_type=F32)
    ident = names[1:2, :] * passages + names[2:3, :]
    slot_ref[...] = jnp.where(names[0:1, :] > 0.5, ident, -1.0).astype(I32)


def place(recv, centroids, passages):
    width = centroids.shape[1]
    return pl.pallas_call(
        functools.partial(place_kernel, passages),
        out_shape=(
            jax.ShapeDtypeStruct((CAP, width), BF16),
            jax.ShapeDtypeStruct((1, META), I32),
        ),
        in_specs=[vmem(), vmem()],
        out_specs=(vmem(), vmem()),
        name="place",
    )(recv, centroids)


def score_kernel(base_row, tokens, vocab_hbm, earlier, res, outs, tok_v, side_v, w_v, tok_sem, side_sem, w_sem):
    groups, rows, width = tok_v.shape
    passages = rows // SEQ
    shards, terms = w_v.shape[:2]
    per_device = terms // BLOCK
    span = 2 * rows
    tok_dma, side_dma, w_dma = [], [], []
    for g, t in enumerate(tokens):
        tok_dma.append(
            pltpu.make_async_copy(t.at[pl.ds(0, rows), :], tok_v.at[g], tok_sem.at[g])
        )
        side_dma.append(
            pltpu.make_async_copy(
                t.at[pl.ds(rows, EXTRA), pl.ds(0, BLOCK)], side_v.at[g], side_sem.at[g]
            )
        )
    for s in range(shards):
        w_dma.append(
            pltpu.make_async_copy(
                vocab_hbm.at[pl.ds(s * terms, terms), :], w_v.at[s], w_sem.at[s]
            )
        )
    for d in tok_dma[:2] + w_dma[:1] + tok_dma[2:] + side_dma + w_dma[1:]:
        d.start()
    y, x, core = here()
    source = lax.broadcasted_iota(I32, (BLOCK, terms), 0)
    target = lax.div(lax.broadcasted_iota(I32, (BLOCK, terms), 1), BLOCK)
    row = lax.broadcasted_iota(I32, (8, 1), 0)
    for d in tok_dma + side_dma:
        d.wait()

    @pl.loop(0, shards)
    def _(s):
        pltpu.make_async_copy(
            vocab_hbm.at[pl.ds(pl.multiple_of(s * terms, terms), terms), :], w_v.at[s], w_sem.at[s]
        ).wait()
        owner = y * (2 * NX) + s
        spread = (source == target + owner * per_device).astype(F32).astype(BF16)
        for j in range(groups // 2):
            listed = [
                jnp.dot(side_v[2 * j + k], spread, preferred_element_type=F32) for k in range(2)
            ]
            both = tok_v[2 * j : 2 * j + 2].reshape(span, width)
            for n in range(terms // STEP):
                at = slice(n * STEP, (n + 1) * STEP)
                logits = lax.dot_general(
                    both, w_v[s, at, :], (((1,), (1,)), ((), ())), preferred_element_type=F32
                )
                best = jnp.max(logits.reshape(2 * passages, SEQ, STEP), axis=1)
                if earlier is None:
                    tile = jnp.full((8, STEP), FILL, F32)
                else:
                    tile = earlier[s, 8 * j : 8 * j + 8, at]
                for g in range(2):
                    for p in range(passages):
                        k = g * passages + p
                        value = jnp.where(
                            listed[g][p : p + 1, at] > 0.5, best[k : k + 1, :], FILL
                        )
                        tile = jnp.where(row == g * 4 + base_row + p, value, tile)
                res[s, 8 * j : 8 * j + 8, at] = tile

    for k, (dx, dc) in enumerate(PEERS if outs else ()):
        spot = lax.rem(x + dx, NX) * 2 + lax.rem(core + dc, 2)
        outs[k][...] = res[spot]


def score(part, tokens, vocab, earlier):
    groups = len(tokens)
    rows, width = tokens[0].shape
    rows -= EXTRA
    shards = 2 * NX
    terms = vocab.shape[0] // shards
    passages = rows // SEQ
    whole = jax.ShapeDtypeStruct((shards, groups * 4, terms), F32)
    last = earlier is not None

    def kernel(*refs):
        refs = list(refs)
        toks, refs = refs[:groups], refs[groups:]
        voc = refs.pop(0)
        before = refs.pop(0) if last else None
        if last:
            outs, refs = refs[:shards], refs[shards:]
            res = refs.pop(0)
        else:
            outs, res = None, refs.pop(0)
        score_kernel(part * passages, toks, voc, before, res, outs, *refs)

    flops = 2 * groups * rows * width * terms * shards
    piece = jax.ShapeDtypeStruct((groups * 4, terms), F32)
    return pl.pallas_call(
        kernel,
        out_shape=(piece,) * shards if last else whole,
        in_specs=[hbm()] * (groups + 1) + [vmem()] * last,
        out_specs=(vmem(),) * shards if last else vmem(),
        scratch_shapes=[pltpu.VMEM(whole.shape, F32)] * last + [
            pltpu.VMEM((groups, rows, width), BF16),
            pltpu.VMEM((groups, EXTRA, BLOCK), BF16),
            pltpu.VMEM((shards, terms, width), BF16),
            pltpu.SemaphoreType.DMA((groups,)),
            pltpu.SemaphoreType.DMA((groups,)),
            pltpu.SemaphoreType.DMA((shards,)),
        ],
        compiler_params=pltpu.CompilerParams(vmem_limit_bytes=VMEM_BYTES),
        cost_estimate=pl.CostEstimate(
            flops=flops, transcendentals=0, bytes_accessed=shards * terms * width * 2
        ),
        name="score",
    )(*tokens, vocab, *((earlier,) if last else ()))


def finish_kernel(bias_ref, *refs):
    pieces, (out_ref, best) = refs[: len(PEERS)], refs[len(PEERS) :]
    y, x, core = here()
    bias = bias_ref[...].astype(F32).reshape(1, -1)
    for k in range(0, len(PEERS), 2):
        dx = PEERS[k][0]
        for g, dy in enumerate(OFFSETS):
            same = pieces[k][4 * g : 4 * g + 4, :]
            other = pieces[k + 1][4 * g : 4 * g + 4, :]
            tile = jnp.where(
                core == 0,
                jnp.concatenate([same, other], axis=0),
                jnp.concatenate([other, same], axis=0),
            )
            spot = lax.rem(y + dy, NY) * NX + lax.rem(x + dx, NX)
            best[pl.ds(pl.multiple_of(spot * 8, 8), 8), :] = tile
    out_ref[...] = jnp.log1p(jnp.maximum(best[...] + bias, 0.0)).astype(BF16)


def finish(bias, pieces):
    terms = bias.shape[0]
    rows = NX * NY * 8
    return pl.pallas_call(
        finish_kernel,
        out_shape=jax.ShapeDtypeStruct((rows, terms), BF16),
        in_specs=[vmem()] * (1 + len(pieces)),
        out_specs=vmem(),
        scratch_shapes=[pltpu.VMEM((rows, terms), F32)],
        name="finish",
    )(bias, *pieces)


def shift(value, dy, dx, dc):
    pairs = []
    for y in range(NY):
        for x in range(NX):
            for c in range(2):
                source = (((y + dy) % NY) * NX + (x + dx) % NX) * 2 + (c ^ dc)
                pairs.append((source, (y * NX + x) * 2 + c))
    return lax.ppermute(value, "term", pairs)


def body(
    hidden_states,
    lengths,
    block_list,
    cluster_ids,
    attn_weight,
    out_weight,
    up_weight,
    down_weight,
    head_weight,
    head_gain,
    vocab_weight,
    vocab_bias,
    centroids,
):
    devices = lax.axis_size("grp") * lax.axis_size("term")
    passages = lengths.shape[0]

    side = 2 * NX
    rows_of_chips = [[g * side + k for k in range(side)] for g in range(NY)]
    vocab = lax.all_gather(
        vocab_weight, "term", axis=0, tiled=True, axis_index_groups=rows_of_chips
    )
    first = attend(hidden_states, lengths, attn_weight, out_weight)
    dense, received = [], []
    for part in range(PARTS):
        payload, rows = forward(
            part, first, lengths, block_list, head_gain, up_weight, down_weight, head_weight
        )
        dense.append(rows)
        received.append([payload] + [shift(payload, d, 0, 0) for d in OFFSETS[1:]])

    recv = lax.all_to_all(
        route(cluster_ids, dense, devices), ("grp", "term"), split_axis=0, concat_axis=0, tiled=True
    )


    scored = score(0, received[0], vocab, None)
    sent = score(1, received[1], vocab, scored)
    pieces = []
    for dx, dc in PEERS:
        back = sent[PEERS.index(((NX - dx) % NX, dc))]
        pieces.append(back if (dx, dc) == (0, 0) else shift(back, 0, dx, dc))
    sparse = finish(vocab_bias, pieces)
    dense_part, slot_part = place(recv, centroids, passages)
    return (sparse, dense_part[None], slot_part[:, :CAP])


def solution(mesh):
    placed = (
        P(("grp", "term"), None),
        P(("grp", "term")),
        P(("grp", "term"), None),
        P(("grp", "term")),
        P(),
        P(),
        P(),
        P(),
        P(),
        P(),
        P("term", None),
        P("term"),
        P(("grp", "term"), None),
    )
    return jax.shard_map(
        body,
        mesh=mesh,
        in_specs=placed,
        out_specs=(P("grp", "term"), P(("grp", "term"), None, None), P(("grp", "term"), None)),
        check_vma=False,
    )
```

time: 133 us -> 116 us (0.87); the launches traced: 131 us -> 116 us
  waiting for transfers between devices: 26.4 us -> 1.59 us
  between operations: 0.9 us -> 14.2 us
  Pallas kernels: 56.9 us -> 67.9 us
  starting transfers between devices: 38.1 us -> 29.9 us
  local copies, waits for them, and re-layouts: 5.78 us -> 2.23 us
  other arithmetic: 2.84 us -> 0 us
    ppermute x19 -> x13, waiting for transfers between devices: 26.4 us -> 0.9 us  [shift(): return lax.ppermute(value, 'term', pairs)]
    pallas_call x5 -> x6, Pallas kernels: 52.6 us -> 62.9 us  [the longest x2 27.4 us: score(): pl.pallas_call(kernel, out_shape=(piece,) * shards if last else whole, in...]
    ppermute x19 -> x13, starting transfers between devices: 28.6 us -> 18.4 us  [shift(): return lax.ppermute(value, 'term', pairs)]
    all_to_all x1, starting transfers between devices: 9.5 us -> 11.5 us  [body(): lax.all_to_all(route(cluster_ids, dense, devices), ('grp', 'term'), split...]
    reshape x2 -> x0, local copies, waits for them, and re-layouts: 1.86 us -> none  [the longest x1 1.27 us: body(): gain = head_gain.reshape(1, -1)]
    all_to_all x1 -> x0, other arithmetic: 1.66 us -> none  [body(): lax.all_to_all(route(device, cluster_ids, dense, devices), ('grp', 'term'...]
    unnamed x33 -> x22, local copies, waits for them, and re-layouts: 2.73 us -> 2.23 us
  transfers between devices with their start and end apart: 20 -> 15, of which waited for: 2 -> 2; matrix products, arithmetic and copies ran while one was open for 6% -> 0% of each run, Pallas kernels for 42% -> 57%
where the time goes in v1:
time: 116 us
  Pallas kernels  67.9 us (59%)
  starting transfers between devices  29.9 us (26%)
  between operations  14.2 us (12%)
  local copies, waits for them, and re-layouts  2.23 us (2%)
  waiting for transfers between devices  1.59 us (1%)
    pallas_call x2, Pallas kernels, score(): pl.pallas_call(kernel, out_shape=(piece,) * shards if last else whole, in...  27.4 us
    pallas_call x2, Pallas kernels, forward(): pl.pallas_call(functools.partial(forward_kernel, part * passages), out_sh...  22.7 us
    ppermute x13, starting transfers between devices, shift(): return lax.ppermute(value, 'term', pairs)  18.4 us
    all_to_all x1, starting transfers between devices, body(): lax.all_to_all(route(cluster_ids, dense, devices), ('grp', 'term'), split...  11.5 us
    pallas_call x1, Pallas kernels, attend(): pl.pallas_call(attend_kernel, out_shape=jax.ShapeDtypeStruct((rows, width...  11.2 us
    pallas_call x1, Pallas kernels, place(): pl.pallas_call(functools.partial(place_kernel, passages), out_shape=(jax....  3.01 us
  transfers between devices with their start and end apart: 15, of which 2 were waited for; matrix products, arithmetic and copies ran while one was open for 0% of the time, Pallas kernels for 57%

profile of v1, /device:TPU:1, one launch (start us, length us, event | category | flops | bytes accessed | tf_op | source)
XLA Modules:
  0.0 115.8 jit_solution(1311788835826135614)
XLA Ops:
  7.2 0.0 all-gather.2.cloned.1.call-start
  7.2 0.7 all-gather.2.cloned.1.call-update
  7.9 11.2 %attend.1.first_hbm = bf16[512,768]{1,0:T(8,128)(2,1)} custom-call(s32[4]{0:T(128)} %lengths_ref.5, bf16[512,768]{1,0:T(8,128)(2,1)} %hidden_hbm.1, bf16[768,2304]{1,0:T(8,128)(2,1)} %attn_hbm.1, bf16[768,768]{1,0:T(8,128)(2,1)} %out_hbm.1), custom_call_target="tpu_custom_call" | custom-call | flops 2415919104 | bytes 4718592 | tf_op jit(solution)/shard_map/attend/pallas_call | solution.py:123
  19.1 11.3 %forward.3 = (bf16[272,768]{1,0:T(8,128)(2,1)}, f32[8,768]{1,0:T(8,128)}) custom-call(s32[4]{0:T(128)} %lengths_ref.5, bf16[512,768]{1,0:T(8,128)(2,1)} %attend.1.first_hbm, s32[4,96]{1,0:T(4,128)} %lists_ref.3, f32[768]{0:T(1024)} %gain_ref.3, bf16[768,3072]{1,0:T(8,128)(2,1)} %up_hbm.3, bf16[3072,768]{1,0:T(8,128)(2,1)} %down_hbm.3, bf16[768,768]{1,0:T(8,128)(2,1)} %head_hbm.3), custom_call_target="tpu_custom_call" | custom-call | flops 1 | bytes 1 | tf_op jit(solution)/shard_map/forward/pallas_call | solution.py:205
  30.4 3.9 %collective-permute-start.5 = (bf16[272,768]{1,0:T(8,128)(2,1)}, bf16[272,768]{1,0:T(8,128)(2,1)S(1)}, u32[]{:S(2)}, u32[]{:S(2)}) collective-permute-start(bf16[272,768]{1,0:T(8,128)(2,1)} %get-tuple-element.18.refs_0_), channel_id=1, source_target_pairs={{16,0},{17,1},{18,2},{19,3},{20,4},{21,5},{22,6},{23,7},{24,8},{25... | collective-permute-start | bytes 1253384 | tf_op jit(solution)/shard_map/ppermute | solution.py:478
  34.3 0.4 collective-permute-start.4
  34.7 2.3 %collective-permute-start.3 = (bf16[272,768]{1,0:T(8,128)(2,1)}, bf16[272,768]{1,0:T(8,128)(2,1)}, u32[]{:S(2)}, u32[]{:S(2)}) collective-permute-start(bf16[272,768]{1,0:T(8,128)(2,1)} %get-tuple-element.18.refs_0_), channel_id=1, source_target_pairs={{8,0},{9,1},{10,2},{11,3},{12,4},{13,5},{14,6},{15,7},{16,8},{17,9... | collective-permute-start | bytes 1253384 | tf_op jit(solution)/shard_map/ppermute | solution.py:478
  37.0 11.4 %forward.2 = (bf16[272,768]{1,0:T(8,128)(2,1)}, f32[8,768]{1,0:T(8,128)}) custom-call(s32[4]{0:T(128)} %lengths_ref.5, bf16[512,768]{1,0:T(8,128)(2,1)} %attend.1.first_hbm, s32[4,96]{1,0:T(4,128)} %lists_ref.3, f32[768]{0:T(1024)} %gain_ref.3, bf16[768,3072]{1,0:T(8,128)(2,1)} %up_hbm.3, bf16[3072,768]{1,0:T(8,128)(2,1)} %down_hbm.3, bf16[768,768]{1,0:T(8,128)(2,1)} %head_hbm.3), custom_call_target="tpu_custom_call" | custom-call | flops 1 | bytes 1 | tf_op jit(solution)/shard_map/forward/pallas_call | solution.py:205
  48.3 0.1 collective-permute-start.2
  48.4 0.5 collective-permute-start.1
  48.9 2.0 %route.1 = f32[128,8,128]{2,1,0:T(8,128)} custom-call(s32[4]{0:T(128)} %clusters_ref.1, f32[8,768]{1,0:T(8,128)} %get-tuple-element.27.refs_0_, f32[8,768]{1,0:T(8,128)} %get-tuple-element.28.refs_1_), custom_call_target="tpu_custom_call" | custom-call | flops 1 | bytes 1 | tf_op jit(solution)/shard_map/route/pallas_call | solution.py:265
  50.8 11.5 %all-to-all-start = ((f32[128,8,128]{2,1,0:T(8,128)}), f32[128,8,128]{2,1,0:T(8,128)S(1)}, u32[]{:S(2)}, u32[]{:S(2)}) async-start(f32[128,8,128]{2,1,0:T(8,128)} %route.1), calls=%async_computation | async-start | bytes 1048576 | tf_op jit(solution)/shard_map/all_to_all | solution.py:513
  62.3 0.0 collective-permute-done.5.refs_3_
  62.3 0.0 copy-start.10
  62.3 2.7 %collective-permute-start = (bf16[272,768]{1,0:T(8,128)(2,1)}, bf16[272,768]{1,0:T(8,128)(2,1)}, u32[]{:S(2)}, u32[]{:S(2)}) collective-permute-start(bf16[272,768]{1,0:T(8,128)(2,1)} %get-tuple-element.17.refs_0_), channel_id=1, source_target_pairs={{8,0},{9,1},{10,2},{11,3},{12,4},{13,5},{14,6},{15,7},{16,8},{17,9... | collective-permute-start | bytes 1253384 | tf_op jit(solution)/shard_map/ppermute | solution.py:478
  65.1 0.0 collective-permute-done.4.refs_2_
  65.1 0.0 collective-permute-done.3.refs_1_
  65.1 0.0 copy-done.10
  65.1 13.2 %score.2.refs_5_ = f32[8,16,512]{2,1,0:T(8,128)} custom-call(bf16[272,768]{1,0:T(8,128)(2,1)} %get-tuple-element.18.refs_0_, bf16[272,768]{1,0:T(8,128)(2,1)} %collective-permute-done.3.refs_1_, bf16[272,768]{1,0:T(8,128)(2,1)} %collective-permute-done.4.refs_2_, bf16[272,768]{1,0:T(8,128)(2,1)} %copy-done.10, ...), custom_call_target="tpu_custom_call" | custom-call | flops 6442450944 | bytes 6291456 | tf_op jit(solution)/shard_map/score/pallas_call | solution.py:418
  78.3 0.0 collective-permute-done.2.refs_3_
  78.3 0.0 copy-start.8
  78.3 0.0 collective-permute-done.1.refs_2_
  78.3 0.0 copy-start.9
  78.3 0.1 collective-permute-done.refs_1_
  78.4 0.7 copy-done.8
  79.1 0.1 copy-done.9
  79.3 14.2 %score.3 = (f32[16,512]{1,0:T(8,128)}, f32[16,512]{1,0:T(8,128)}, f32[16,512]{1,0:T(8,128)}, f32[16,512]{1,0:T(8,128)}, f32[16,512]{1,0:T(8,128)}, /*index=5*/f3...) custom-call(bf16[272,768]{1,0:T(8,128)(2,1)} %get-tuple-element.17.refs_0_, ...), custom_call_target="tpu_custom_call" | custom-call | flops 6442450944 | bytes 6291456 | tf_op jit(solution)/shard_map/score/pallas_call | solution.py:418
  93.5 0.7 collective-permute-start.6
  94.2 2.4 %collective-permute-start.7 = (f32[16,512]{1,0:T(8,128)}, f32[16,512]{1,0:T(8,128)S(1)}, u32[]{:S(2)}, u32[]{:S(2)}) collective-permute-start(f32[16,512]{1,0:T(8,128)} %get-tuple-element.21), channel_id=1, source_target_pairs={{2,0},{3,1},{4,2},{5,3},{6,4},{7,5},{0,6},{1,7},{10,8},{11,9},{12,... | collective-permute-start | bytes 98312 | tf_op jit(solution)/shard_map/ppermute | solution.py:478
  96.6 0.8 collective-permute-start.8
  97.4 0.9 collective-permute-start.9
  98.3 0.1 collective-permute-start.10
  98.4 0.0 collective-permute-done.6.refs_1_
  98.4 3.2 %collective-permute-start.11 = (f32[16,512]{1,0:T(8,128)}, f32[16,512]{1,0:T(8,128)S(1)}, u32[]{:S(2)}, u32[]{:S(2)}) collective-permute-start(f32[16,512]{1,0:T(8,128)} %get-tuple-element.25), channel_id=1, source_target_pairs={{4,0},{5,1},{6,2},{7,3},{0,4},{1,5},{2,6},{3,7},{12,8},{13,9},{14,... | collective-permute-start | bytes 98312 | tf_op jit(solution)/shard_map/ppermute | solution.py:478
  101.6 0.0 collective-permute-done.7.refs_2_
  101.6 0.4 collective-permute-start.12
  102.0 0.0 all-to-all-done.recv_ref
  102.0 0.8 copy-done
  102.8 3.0 %place.1 = (bf16[16,768]{1,0:T(8,128)(2,1)}, s32[1,128]{1,0:T(1,128)}) custom-call(f32[128,8,128]{2,1,0:T(8,128)} %copy-done, bf16[512,768]{1,0:T(8,128)(2,1)} %cent_ref.1), custom_call_target="tpu_custom_call" | custom-call | tf_op jit(solution)/shard_map/place/pallas_call | solution.py:315
  105.8 0.0 collective-permute-done.8.refs_3_
  105.9 0.0 collective-permute-done.9.refs_4_
  105.9 0.0 copy-start.4
  105.9 0.0 collective-permute-done.10.refs_5_
  105.9 0.0 collective-permute-done.11.refs_6_
  105.9 0.8 collective-permute-done.12.refs_7_
  106.7 0.0 copy-done.3
  106.7 0.6 copy-done.7
  107.3 1.7 %finish.1 = bf16[128,512]{1,0:T(8,128)(2,1)} custom-call(bf16[512]{0:T(512)(128)(2,1)} %bias_ref.1, f32[16,512]{1,0:T(8,128)} %get-tuple-element.19.refs_0_, f32[16,512]{1,0:T(8,128)} %copy-done.1, f32[16,512]{1,0:T(8,128)} %copy-done.2, f32[16,512]{1,0:T(8,128)} %copy-done.3, f32[16,512]{1,0:T(8,128)} %copy-done.4, f32[16,512]{1,0:T(8,128)} %copy-done.5, ...), custom_call_target="tpu_custom_call" | custom-call | tf_op jit(solution)/shard_map/finish/pallas_call | solution.py:461
  (13 shorter events, 0.0 us)
Async XLA Ops:
  7.2 57.9 %all-gather.2.cloned.1.call-start = ((), (), s32[]{:S(2)}) async-start(), calls=%async_computation.1 | async-start | bytes 7077888 | tf_op jit(solution)/shard_map/all_gather | solution.py:501
  30.4 31.9 %collective-permute-start.5 = (bf16[272,768]{1,0:T(8,128)(2,1)}, bf16[272,768]{1,0:T(8,128)(2,1)S(1)}, u32[]{:S(2)}, u32[]{:S(2)}) collective-permute-start(bf16[272,768]{1,0:T(8,128)(2,1)} %get-tuple-element.18.refs_0_), channel_id=1, source_target_pairs={{16,0},{17,1},{18,2},{19,3},{20,4},{21,5},{22,6},{23,7},{24,8},{25... | collective-permute-start | bytes 1253384 | tf_op jit(solution)/shard_map/ppermute | solution.py:478
  34.3 30.8 %collective-permute-start.4 = (bf16[272,768]{1,0:T(8,128)(2,1)}, bf16[272,768]{1,0:T(8,128)(2,1)}, u32[]{:S(2)}, u32[]{:S(2)}) collective-permute-start(bf16[272,768]{1,0:T(8,128)(2,1)} %get-tuple-element.18.refs_0_), channel_id=1, source_target_pairs={{24,0},{25,1},{26,2},{27,3},{28,4},{29,5},{30,6},{31,7},{0,8},{1,9... | collective-permute-start | bytes 1253384 | tf_op jit(solution)/shard_map/ppermute | solution.py:478
  34.7 30.4 %collective-permute-start.3 = (bf16[272,768]{1,0:T(8,128)(2,1)}, bf16[272,768]{1,0:T(8,128)(2,1)}, u32[]{:S(2)}, u32[]{:S(2)}) collective-permute-start(bf16[272,768]{1,0:T(8,128)(2,1)} %get-tuple-element.18.refs_0_), channel_id=1, source_target_pairs={{8,0},{9,1},{10,2},{11,3},{12,4},{13,5},{14,6},{15,7},{16,8},{17,9... | collective-permute-start | bytes 1253384 | tf_op jit(solution)/shard_map/ppermute | solution.py:478
  48.3 30.0 %collective-permute-start.2 = (bf16[272,768]{1,0:T(8,128)(2,1)}, bf16[272,768]{1,0:T(8,128)(2,1)S(1)}, u32[]{:S(2)}, u32[]{:S(2)}) collective-permute-start(bf16[272,768]{1,0:T(8,128)(2,1)} %get-tuple-element.17.refs_0_), channel_id=1, source_target_pairs={{16,0},{17,1},{18,2},{19,3},{20,4},{21,5},{22,6},{23,7},{24,8},{25... | collective-permute-start | bytes 1253384 | tf_op jit(solution)/shard_map/ppermute | solution.py:478
  48.4 29.9 %collective-permute-start.1 = (bf16[272,768]{1,0:T(8,128)(2,1)}, bf16[272,768]{1,0:T(8,128)(2,1)S(1)}, u32[]{:S(2)}, u32[]{:S(2)}) collective-permute-start(bf16[272,768]{1,0:T(8,128)(2,1)} %get-tuple-element.17.refs_0_), channel_id=1, source_target_pairs={{24,0},{25,1},{26,2},{27,3},{28,4},{29,5},{30,6},{31,7},{0,8},{1,9... | collective-permute-start | bytes 1253384 | tf_op jit(solution)/shard_map/ppermute | solution.py:478
  50.8 51.2 %all-to-all-start = ((f32[128,8,128]{2,1,0:T(8,128)}), f32[128,8,128]{2,1,0:T(8,128)S(1)}, u32[]{:S(2)}, u32[]{:S(2)}) async-start(f32[128,8,128]{2,1,0:T(8,128)} %route.1), calls=%async_computation | async-start | bytes 1048576 | tf_op jit(solution)/shard_map/all_to_all | solution.py:513
  62.3 2.7 %copy-start.10 = (bf16[272,768]{1,0:T(8,128)(2,1)}, bf16[272,768]{1,0:T(8,128)(2,1)S(1)}, u32[]{:S(2)}) copy-start(bf16[272,768]{1,0:T(8,128)(2,1)S(1)} %collective-permute-done.5.refs_3_) | copy-start | bytes 1253380
  62.3 16.1 %collective-permute-start = (bf16[272,768]{1,0:T(8,128)(2,1)}, bf16[272,768]{1,0:T(8,128)(2,1)}, u32[]{:S(2)}, u32[]{:S(2)}) collective-permute-start(bf16[272,768]{1,0:T(8,128)(2,1)} %get-tuple-element.17.refs_0_), channel_id=1, source_target_pairs={{8,0},{9,1},{10,2},{11,3},{12,4},{13,5},{14,6},{15,7},{16,8},{17,9... | collective-permute-start | bytes 1253384 | tf_op jit(solution)/shard_map/ppermute | solution.py:478
  78.3 0.8 copy-start.8
  78.3 0.9 copy-start.9
  93.5 5.0 %collective-permute-start.6 = (f32[16,512]{1,0:T(8,128)}, f32[16,512]{1,0:T(8,128)S(1)}, u32[]{:S(2)}, u32[]{:S(2)}) collective-permute-start(f32[16,512]{1,0:T(8,128)} %get-tuple-element.20), channel_id=1, source_target_pairs={{1,0},{0,1},{3,2},{2,3},{5,4},{4,5},{7,6},{6,7},{9,8},{8,9},{11,10... | collective-permute-start | bytes 98312 | tf_op jit(solution)/shard_map/ppermute | solution.py:478
  94.2 7.4 %collective-permute-start.7 = (f32[16,512]{1,0:T(8,128)}, f32[16,512]{1,0:T(8,128)S(1)}, u32[]{:S(2)}, u32[]{:S(2)}) collective-permute-start(f32[16,512]{1,0:T(8,128)} %get-tuple-element.21), channel_id=1, source_target_pairs={{2,0},{3,1},{4,2},{5,3},{6,4},{7,5},{0,6},{1,7},{10,8},{11,9},{12,... | collective-permute-start | bytes 98312 | tf_op jit(solution)/shard_map/ppermute | solution.py:478
  96.6 9.2 %collective-permute-start.8 = (f32[16,512]{1,0:T(8,128)}, f32[16,512]{1,0:T(8,128)S(1)}, u32[]{:S(2)}, u32[]{:S(2)}) collective-permute-start(f32[16,512]{1,0:T(8,128)} %get-tuple-element.22), channel_id=1, source_target_pairs={{3,0},{2,1},{5,2},{4,3},{7,4},{6,5},{1,6},{0,7},{11,8},{10,9},{13,... | collective-permute-start | bytes 98312 | tf_op jit(solution)/shard_map/ppermute | solution.py:478
  97.4 8.4 %collective-permute-start.9 = (f32[16,512]{1,0:T(8,128)}, f32[16,512]{1,0:T(8,128)S(1)}, u32[]{:S(2)}, u32[]{:S(2)}) collective-permute-start(f32[16,512]{1,0:T(8,128)} %get-tuple-element.23), channel_id=1, source_target_pairs={{6,0},{7,1},{0,2},{1,3},{2,4},{3,5},{4,6},{5,7},{14,8},{15,9},{8,1... | collective-permute-start | bytes 98312 | tf_op jit(solution)/shard_map/ppermute | solution.py:478
  98.3 7.5 %collective-permute-start.10 = (f32[16,512]{1,0:T(8,128)}, f32[16,512]{1,0:T(8,128)S(1)}, u32[]{:S(2)}, u32[]{:S(2)}) collective-permute-start(f32[16,512]{1,0:T(8,128)} %get-tuple-element.24), channel_id=1, source_target_pairs={{7,0},{6,1},{1,2},{0,3},{3,4},{2,5},{5,6},{4,7},{15,8},{14,9},{9,1... | collective-permute-start | bytes 98312 | tf_op jit(solution)/shard_map/ppermute | solution.py:478
  98.4 8.3 %copy-start.1 = (f32[16,512]{1,0:T(8,128)}, f32[16,512]{1,0:T(8,128)S(1)}, u32[]{:S(2)}) copy-start(f32[16,512]{1,0:T(8,128)S(1)} %collective-permute-done.6.refs_1_) | copy-start | bytes 98308
  98.4 7.5 %collective-permute-start.11 = (f32[16,512]{1,0:T(8,128)}, f32[16,512]{1,0:T(8,128)S(1)}, u32[]{:S(2)}, u32[]{:S(2)}) collective-permute-start(f32[16,512]{1,0:T(8,128)} %get-tuple-element.25), channel_id=1, source_target_pairs={{4,0},{5,1},{6,2},{7,3},{0,4},{1,5},{2,6},{3,7},{12,8},{13,9},{14,... | collective-permute-start | bytes 98312 | tf_op jit(solution)/shard_map/ppermute | solution.py:478
  101.6 5.1 %copy-start.2 = (f32[16,512]{1,0:T(8,128)}, f32[16,512]{1,0:T(8,128)S(1)}, u32[]{:S(2)}) copy-start(f32[16,512]{1,0:T(8,128)S(1)} %collective-permute-done.7.refs_2_) | copy-start | bytes 98308
  101.6 5.1 %collective-permute-start.12 = (f32[16,512]{1,0:T(8,128)}, f32[16,512]{1,0:T(8,128)S(1)}, u32[]{:S(2)}, u32[]{:S(2)}) collective-permute-start(f32[16,512]{1,0:T(8,128)} %get-tuple-element.26), channel_id=1, source_target_pairs={{5,0},{4,1},{7,2},{6,3},{1,4},{0,5},{3,6},{2,7},{13,8},{12,9},{15,... | collective-permute-start | bytes 98312 | tf_op jit(solution)/shard_map/ppermute | solution.py:478
  102.0 0.8 copy-start
  105.8 0.8 copy-start.3
  105.9 0.8 copy-start.4
  105.9 0.8 copy-start.5
  105.9 0.8 copy-start.6
  106.7 0.6 copy-start.7
Sparse Core Ops, SparseCore 0:
  9.7 44.4 all-gather.1

commit v2 on v1

--- a/solution.py
+++ b/solution.py
@@ -19,6 +19,7 @@
 EXTRA = 16
 META = 128
 STEP = 256
+GROUP = 4
 PARTS = 2
 OFFSETS = (0, 1, 3, 2)
 PEERS = tuple((dx, dc) for dx in OFFSETS for dc in (0, 1))
@@ -83,20 +84,21 @@
     for d in dma:
         d.start()
     dma[0].wait()
+    dma[1].wait()
     for k in range(3):
-        dma[1 + k].wait()
+        if k == 1:
+            for d in dma[2:]:
+                d.wait()
         joined[:, k * width : (k + 1) * width] = jnp.dot(
             hidden[...], attn_v[k], preferred_element_type=F32
         ).astype(BF16)
 
     low = lax.broadcasted_iota(I32, (SEQ, 128), 1) < HEAD
     lane = lax.broadcasted_iota(I32, (2 * SEQ, 128), 1)
-    ones = jnp.ones((SEQ, 128), BF16)
     scale = math.log2(math.e) / math.sqrt(HEAD)
 
-    @pl.loop(0, passages)
-    def _(p):
-        at = pl.ds(pl.multiple_of(p * SEQ, SEQ), SEQ)
+    for p in range(passages):
+        at = slice(p * SEQ, (p + 1) * SEQ)
         length = lengths_ref[p]
         for h in range(pairs):
             q = joined[at, h * 128 : (h + 1) * 128]
@@ -107,15 +109,18 @@
             s = lax.dot_general(both, k, (((1,), (1,)), ((), ())), preferred_element_type=F32)
             s = jnp.where(lane < length, s, FILL)
             top = jnp.max(s, axis=-1, keepdims=True)
-            e = jnp.exp2((s - top) * scale).astype(BF16)
-            o = jnp.dot(e, jnp.concatenate([v, ones], axis=1), preferred_element_type=F32)
-            num = jnp.where(low, o[:SEQ, :128], o[SEQ:, :128])
-            den = jnp.where(low, o[:SEQ, 128:], o[SEQ:, 128:])
-            context[at, h * 128 : (h + 1) * 128] = (num / den).astype(BF16)
-
-    dma[4].wait()
-    mixed = hidden[...].astype(F32) + jnp.dot(context[...], out_v[...], preferred_element_type=F32)
-    first_ref[...] = normalize(mixed).astype(BF16)
+            e = jnp.exp2((s - top) * scale)
+            total = 1.0 / jnp.sum(e, axis=-1, keepdims=True)
+            o = jnp.dot(e.astype(BF16), v, preferred_element_type=F32)
+            mix = jnp.where(low, o[:SEQ] * total[:SEQ], o[SEQ:] * total[SEQ:])
+            context[at, h * 128 : (h + 1) * 128] = mix.astype(BF16)
+
+    for p in range(passages):
+        at = slice(p * SEQ, (p + 1) * SEQ)
+        mixed = hidden[at, :].astype(F32) + jnp.dot(
+            context[at, :], out_v[...], preferred_element_type=F32
+        )
+        first_ref[at, :] = normalize(mixed).astype(BF16)
 
 
 def attend(hidden, lengths, attn_w, out_w):
@@ -150,6 +155,7 @@
     rows, width = first.shape
     passages = rows // SEQ
     chunks = up_v.shape[0]
+    half = chunks // 2
     moves = [(first_hbm.at[pl.ds(offset * SEQ, rows), :], first)]
     for c in range(chunks):
         moves.append((up_hbm.at[:, pl.ds(c * FCH, FCH)], up_v.at[c]))
@@ -160,22 +166,21 @@
         d.start()
 
     def up(c):
-        dma[1 + c].wait()
         return jnp.dot(first[...], up_v[c], preferred_element_type=F32)
 
-    dma[0].wait()
-    current = up(0)
-    for c in range(chunks):
-        following = up(c + 1) if c + 1 < chunks else None
-        wide[:, c * FCH : (c + 1) * FCH] = gelu(current).astype(BF16)
-        current = following
-    dma[1 + chunks].wait()
+    for part in (0, half):
+        for d in dma[1 + part : 1 + part + half] + (dma[:1] if part == 0 else dma[1 + chunks :]):
+            d.wait()
+        current = up(part)
+        for c in range(part, part + half):
+            following = up(c + 1) if c + 1 < part + half else None
+            wide[:, c * FCH : (c + 1) * FCH] = gelu(current).astype(BF16)
+            current = following
     second = first[...].astype(F32) + jnp.dot(
         wide[...], down_v[...], preferred_element_type=F32
     )
     layer_out = normalize(second).astype(BF16)
     first[...] = layer_out
-    dma[2 + chunks].wait()
     middle = gelu(jnp.dot(layer_out, head_v[...], preferred_element_type=F32))
     acc[...] = normalize(middle) * gain_ref[...].reshape(1, width)
 
@@ -324,104 +329,96 @@
     )(recv, centroids)
 
 
-def score_kernel(base_row, tokens, vocab_hbm, earlier, res, outs, tok_v, side_v, w_v, tok_sem, side_sem, w_sem):
-    groups, rows, width = tok_v.shape
+def score_kernel(tokens, vocab_hbm, res, listed, tok_v, side_v, w_v, tok_sem, side_sem, w_sem):
+    groups = len(tokens)
+    rows = tok_v.shape[0] // groups
     passages = rows // SEQ
     shards, terms = w_v.shape[:2]
     per_device = terms // BLOCK
-    span = 2 * rows
-    tok_dma, side_dma, w_dma = [], [], []
+    tok_dma, side_dma = [], []
     for g, t in enumerate(tokens):
         tok_dma.append(
-            pltpu.make_async_copy(t.at[pl.ds(0, rows), :], tok_v.at[g], tok_sem.at[g])
+            pltpu.make_async_copy(
+                t.at[pl.ds(0, rows), :], tok_v.at[pl.ds(g * rows, rows), :], tok_sem.at[g]
+            )
         )
         side_dma.append(
             pltpu.make_async_copy(
                 t.at[pl.ds(rows, EXTRA), pl.ds(0, BLOCK)], side_v.at[g], side_sem.at[g]
             )
         )
+
+    def shard(s):
+        at = pl.ds(s * terms if isinstance(s, int) else pl.multiple_of(s * terms, terms), terms)
+        return pltpu.make_async_copy(vocab_hbm.at[at, :], w_v.at[s], w_sem.at[s])
+
+    for d in side_dma + tok_dma:
+        d.start()
     for s in range(shards):
-        w_dma.append(
-            pltpu.make_async_copy(
-                vocab_hbm.at[pl.ds(s * terms, terms), :], w_v.at[s], w_sem.at[s]
-            )
-        )
-    for d in tok_dma[:2] + w_dma[:1] + tok_dma[2:] + side_dma + w_dma[1:]:
-        d.start()
-    y, x, core = here()
+        shard(s).start()
+    y, _, _ = here()
     source = lax.broadcasted_iota(I32, (BLOCK, terms), 0)
     target = lax.div(lax.broadcasted_iota(I32, (BLOCK, terms), 1), BLOCK)
-    row = lax.broadcasted_iota(I32, (8, 1), 0)
-    for d in tok_dma + side_dma:
+    for d in side_dma:
         d.wait()
-
-    @pl.loop(0, shards)
-    def _(s):
-        pltpu.make_async_copy(
-            vocab_hbm.at[pl.ds(pl.multiple_of(s * terms, terms), terms), :], w_v.at[s], w_sem.at[s]
-        ).wait()
-        owner = y * (2 * NX) + s
-        spread = (source == target + owner * per_device).astype(F32).astype(BF16)
-        for j in range(groups // 2):
-            listed = [
-                jnp.dot(side_v[2 * j + k], spread, preferred_element_type=F32) for k in range(2)
-            ]
-            both = tok_v[2 * j : 2 * j + 2].reshape(span, width)
+    side = jnp.concatenate([side_v[g].astype(F32)[:passages] for g in range(groups)], axis=0)
+    side = side.astype(BF16)
+
+    for s in range(shards):
+        spread = (source == target + (y * shards + s) * per_device).astype(F32).astype(BF16)
+        listed[s] = jnp.dot(side, spread, preferred_element_type=F32)
+
+    for d in tok_dma:
+        d.wait()
+
+    @pl.loop(0, shards // GROUP)
+    def _(step):
+        for k in range(GROUP):
+            shard(step * GROUP + k).wait()
+        for k in range(GROUP):
+            s = step * GROUP + k
             for n in range(terms // STEP):
                 at = slice(n * STEP, (n + 1) * STEP)
                 logits = lax.dot_general(
-                    both, w_v[s, at, :], (((1,), (1,)), ((), ())), preferred_element_type=F32
+                    tok_v[...], w_v[s, at, :], (((1,), (1,)), ((), ())),
+                    preferred_element_type=F32,
                 )
-                best = jnp.max(logits.reshape(2 * passages, SEQ, STEP), axis=1)
-                if earlier is None:
-                    tile = jnp.full((8, STEP), FILL, F32)
-                else:
-                    tile = earlier[s, 8 * j : 8 * j + 8, at]
-                for g in range(2):
-                    for p in range(passages):
-                        k = g * passages + p
-                        value = jnp.where(
-                            listed[g][p : p + 1, at] > 0.5, best[k : k + 1, :], FILL
-                        )
-                        tile = jnp.where(row == g * 4 + base_row + p, value, tile)
-                res[s, 8 * j : 8 * j + 8, at] = tile
-
-    for k, (dx, dc) in enumerate(PEERS if outs else ()):
-        spot = lax.rem(x + dx, NX) * 2 + lax.rem(core + dc, 2)
-        outs[k][...] = res[spot]
-
-
-def score(part, tokens, vocab, earlier):
+                best = jnp.max(logits.reshape(groups * passages, SEQ, STEP), axis=1)
+                res[s, :, at] = jnp.where(listed[s, :, at] > 0.5, best, FILL)
+
+
+def score(tokens, vocab, earlier):
     groups = len(tokens)
     rows, width = tokens[0].shape
     rows -= EXTRA
     shards = 2 * NX
     terms = vocab.shape[0] // shards
-    passages = rows // SEQ
-    whole = jax.ShapeDtypeStruct((shards, groups * 4, terms), F32)
+    part = groups * rows // SEQ
     last = earlier is not None
 
     def kernel(*refs):
-        refs = list(refs)
-        toks, refs = refs[:groups], refs[groups:]
-        voc = refs.pop(0)
-        before = refs.pop(0) if last else None
-        if last:
-            outs, refs = refs[:shards], refs[shards:]
-            res = refs.pop(0)
-        else:
-            outs, res = None, refs.pop(0)
-        score_kernel(part * passages, toks, voc, before, res, outs, *refs)
+        toks, voc, refs = refs[:groups], refs[groups], refs[groups + 1 :]
+        if not last:
+            score_kernel(toks, voc, *refs)
+            return
+        before, outs, res = refs[0], refs[1 : 1 + shards], refs[1 + shards]
+        score_kernel(toks, voc, *refs[1 + shards :])
+        _, x, core = here()
+        for k, (dx, dc) in enumerate(PEERS):
+            spot = lax.rem(x + dx, NX) * 2 + lax.rem(core + dc, 2)
+            outs[k][:part, :] = before[spot]
+            outs[k][part:, :] = res[spot]
 
     flops = 2 * groups * rows * width * terms * shards
-    piece = jax.ShapeDtypeStruct((groups * 4, terms), F32)
+    whole = jax.ShapeDtypeStruct((shards, part, terms), F32)
+    piece = jax.ShapeDtypeStruct((PARTS * part, terms), F32)
     return pl.pallas_call(
         kernel,
         out_shape=(piece,) * shards if last else whole,
         in_specs=[hbm()] * (groups + 1) + [vmem()] * last,
         out_specs=(vmem(),) * shards if last else vmem(),
-        scratch_shapes=[pltpu.VMEM(whole.shape, F32)] * last + [
-            pltpu.VMEM((groups, rows, width), BF16),
+        scratch_shapes=[pltpu.VMEM(whole.shape, F32)] * (1 + last) + [
+            pltpu.VMEM((groups * rows, width), BF16),
             pltpu.VMEM((groups, EXTRA, BLOCK), BF16),
             pltpu.VMEM((shards, terms, width), BF16),
             pltpu.SemaphoreType.DMA((groups,)),
@@ -440,15 +437,19 @@
     pieces, (out_ref, best) = refs[: len(PEERS)], refs[len(PEERS) :]
     y, x, core = here()
     bias = bias_ref[...].astype(F32).reshape(1, -1)
+    share = pieces[0].shape[0] // PARTS
+    few = share // NY
     for k in range(0, len(PEERS), 2):
         dx = PEERS[k][0]
         for g, dy in enumerate(OFFSETS):
-            same = pieces[k][4 * g : 4 * g + 4, :]
-            other = pieces[k + 1][4 * g : 4 * g + 4, :]
+            same, other = (
+                [pieces[k + c][h * share + g * few : h * share + (g + 1) * few, :] for h in range(PARTS)]
+                for c in range(2)
+            )
             tile = jnp.where(
                 core == 0,
-                jnp.concatenate([same, other], axis=0),
-                jnp.concatenate([other, same], axis=0),
+                jnp.concatenate(same + other, axis=0),
+                jnp.concatenate(other + same, axis=0),
             )
             spot = lax.rem(y + dy, NY) * NX + lax.rem(x + dx, NX)
             best[pl.ds(pl.multiple_of(spot * 8, 8), 8), :] = tile
@@ -515,8 +516,8 @@
     )
 
 
-    scored = score(0, received[0], vocab, None)
-    sent = score(1, received[1], vocab, scored)
+    scored = score(received[0], vocab, None)
+    sent = score(received[1], vocab, scored)
     pieces = []
     for dx, dc in PEERS:
         back = sent[PEERS.index(((NX - dx) % NX, dc))]

time: 116 us -> 109 us (0.940)
  Pallas kernels: 67.9 us -> 57.8 us
  waiting for transfers between devices: 1.59 us -> 3.83 us
    pallas_call x2, Pallas kernels: 27.4 us -> 22.4 us  [score(): pl.pallas_call(kernel, out_shape=(piece,) * shards if last else whole, in...]
    pallas_call x2, Pallas kernels: 22.7 us -> 20 us  [forward(): pl.pallas_call(functools.partial(forward_kernel, part * passages), out_sh...]
    pallas_call x1, Pallas kernels: 11.2 us -> 8.6 us  [attend(): pl.pallas_call(attend_kernel, out_shape=jax.ShapeDtypeStruct((rows, width...]
    ppermute x13, waiting for transfers between devices: 0.9 us -> 3.14 us  [shift(): return lax.ppermute(value, 'term', pairs)]
  transfers between devices with their start and end apart: 15 -> 15, of which waited for: 2 -> 3; matrix products, arithmetic and copies ran while one was open for 0% -> 0% of each run, Pallas kernels for 57% -> 52%
where the time goes in v2:
time: 109 us; the launch traced here: 108 us
  Pallas kernels  57.8 us (53%)
  starting transfers between devices  30.9 us (28%)
  between operations  14.2 us (13%)
  waiting for transfers between devices  3.83 us (4%)
  local copies, waits for them, and re-layouts  1.41 us (1%)
    pallas_call x2, Pallas kernels, score(): pl.pallas_call(kernel, out_shape=(piece,) * shards if last else whole, in...  22.4 us
    pallas_call x2, Pallas kernels, forward(): pl.pallas_call(functools.partial(forward_kernel, part * passages), out_sh...  20 us
    ppermute x13, starting transfers between devices, shift(): return lax.ppermute(value, 'term', pairs)  19.1 us
    all_to_all x1, starting transfers between devices, body(): lax.all_to_all(route(cluster_ids, dense, devices), ('grp', 'term'), split...  11.7 us
    pallas_call x1, Pallas kernels, attend(): pl.pallas_call(attend_kernel, out_shape=jax.ShapeDtypeStruct((rows, width...  8.6 us
    ppermute x13, waiting for transfers between devices, shift(): return lax.ppermute(value, 'term', pairs)  3.14 us
    pallas_call x1, Pallas kernels, place(): pl.pallas_call(functools.partial(place_kernel, passages), out_shape=(jax....  3.01 us
  transfers between devices with their start and end apart: 15, of which 3 were waited for; matrix products, arithmetic and copies ran while one was open for 0% of the time, Pallas kernels for 52%

profile of v2, /device:TPU:1, one launch (start us, length us, event | category | flops | bytes accessed | tf_op | source)
XLA Modules:
  0.0 108.1 jit_solution(11815266153046328292)
XLA Ops:
  7.2 0.0 all-gather.2.cloned.1.call-start
  7.2 0.7 all-gather.2.cloned.1.call-update
  7.9 8.6 %attend.1.first_hbm = bf16[512,768]{1,0:T(8,128)(2,1)} custom-call(s32[4]{0:T(128)} %lengths_ref.5, bf16[512,768]{1,0:T(8,128)(2,1)} %hidden_hbm.1, bf16[768,2304]{1,0:T(8,128)(2,1)} %attn_hbm.1, bf16[768,768]{1,0:T(8,128)(2,1)} %out_hbm.1), custom_call_target="tpu_custom_call" | custom-call | flops 2415919104 | bytes 4718592 | tf_op jit(solution)/shard_map/attend/pallas_call | solution.py:128
  16.5 10.0 %forward.3 = (bf16[272,768]{1,0:T(8,128)(2,1)}, f32[8,768]{1,0:T(8,128)}) custom-call(s32[4]{0:T(128)} %lengths_ref.5, bf16[512,768]{1,0:T(8,128)(2,1)} %attend.1.first_hbm, s32[4,96]{1,0:T(4,128)} %lists_ref.3, f32[768]{0:T(1024)} %gain_ref.3, bf16[768,3072]{1,0:T(8,128)(2,1)} %up_hbm.3, bf16[3072,768]{1,0:T(8,128)(2,1)} %down_hbm.3, bf16[768,768]{1,0:T(8,128)(2,1)} %head_hbm.3), custom_call_target="tpu_custom_call" | custom-call | flops 1 | bytes 1 | tf_op jit(solution)/shard_map/forward/pallas_call | solution.py:210
  26.5 4.0 %collective-permute-start.5 = (bf16[272,768]{1,0:T(8,128)(2,1)}, bf16[272,768]{1,0:T(8,128)(2,1)S(1)}, u32[]{:S(2)}, u32[]{:S(2)}) collective-permute-start(bf16[272,768]{1,0:T(8,128)(2,1)} %get-tuple-element.18.refs_0_), channel_id=1, source_target_pairs={{16,0},{17,1},{18,2},{19,3},{20,4},{21,5},{22,6},{23,7},{24,8},{25... | collective-permute-start | bytes 1253384 | tf_op jit(solution)/shard_map/ppermute | solution.py:479
  30.4 0.4 collective-permute-start.4
  30.8 2.3 %collective-permute-start.3 = (bf16[272,768]{1,0:T(8,128)(2,1)}, bf16[272,768]{1,0:T(8,128)(2,1)}, u32[]{:S(2)}, u32[]{:S(2)}) collective-permute-start(bf16[272,768]{1,0:T(8,128)(2,1)} %get-tuple-element.18.refs_0_), channel_id=1, source_target_pairs={{8,0},{9,1},{10,2},{11,3},{12,4},{13,5},{14,6},{15,7},{16,8},{17,9... | collective-permute-start | bytes 1253384 | tf_op jit(solution)/shard_map/ppermute | solution.py:479
  33.1 10.1 %forward.2 = (bf16[272,768]{1,0:T(8,128)(2,1)}, f32[8,768]{1,0:T(8,128)}) custom-call(s32[4]{0:T(128)} %lengths_ref.5, bf16[512,768]{1,0:T(8,128)(2,1)} %attend.1.first_hbm, s32[4,96]{1,0:T(4,128)} %lists_ref.3, f32[768]{0:T(1024)} %gain_ref.3, bf16[768,3072]{1,0:T(8,128)(2,1)} %up_hbm.3, bf16[3072,768]{1,0:T(8,128)(2,1)} %down_hbm.3, bf16[768,768]{1,0:T(8,128)(2,1)} %head_hbm.3), custom_call_target="tpu_custom_call" | custom-call | flops 1 | bytes 1 | tf_op jit(solution)/shard_map/forward/pallas_call | solution.py:210
  43.2 0.1 collective-permute-start.2
  43.3 0.6 collective-permute-start.1
  43.9 2.0 %route.1 = f32[128,8,128]{2,1,0:T(8,128)} custom-call(s32[4]{0:T(128)} %clusters_ref.1, f32[8,768]{1,0:T(8,128)} %get-tuple-element.27.refs_0_, f32[8,768]{1,0:T(8,128)} %get-tuple-element.28.refs_1_), custom_call_target="tpu_custom_call" | custom-call | flops 1 | bytes 1 | tf_op jit(solution)/shard_map/route/pallas_call | solution.py:270
  45.9 11.7 %all-to-all-start = ((f32[128,8,128]{2,1,0:T(8,128)}), f32[128,8,128]{2,1,0:T(8,128)S(1)}, u32[]{:S(2)}, u32[]{:S(2)}) async-start(f32[128,8,128]{2,1,0:T(8,128)} %route.1), calls=%async_computation | async-start | bytes 1048576 | tf_op jit(solution)/shard_map/all_to_all | solution.py:514
  57.6 0.0 collective-permute-done.5.refs_3_
  57.6 0.0 copy-start.10
  57.6 2.9 %collective-permute-start = (bf16[272,768]{1,0:T(8,128)(2,1)}, bf16[272,768]{1,0:T(8,128)(2,1)}, u32[]{:S(2)}, u32[]{:S(2)}) collective-permute-start(bf16[272,768]{1,0:T(8,128)(2,1)} %get-tuple-element.17.refs_0_), channel_id=1, source_target_pairs={{8,0},{9,1},{10,2},{11,3},{12,4},{13,5},{14,6},{15,7},{16,8},{17,9... | collective-permute-start | bytes 1253384 | tf_op jit(solution)/shard_map/ppermute | solution.py:479
  60.6 0.0 collective-permute-done.4.refs_2_
  60.6 0.0 collective-permute-done.3.refs_1_
  60.6 0.0 copy-done.10
  60.6 10.7 %score.2.refs_5_ = f32[8,8,512]{2,1,0:T(8,128)} custom-call(bf16[272,768]{1,0:T(8,128)(2,1)} %get-tuple-element.18.refs_0_, bf16[272,768]{1,0:T(8,128)(2,1)} %collective-permute-done.3.refs_1_, bf16[272,768]{1,0:T(8,128)(2,1)} %collective-permute-done.4.refs_2_, bf16[272,768]{1,0:T(8,128)(2,1)} %copy-done.10, ...), custom_call_target="tpu_custom_call" | custom-call | flops 6442450944 | bytes 6291456 | tf_op jit(solution)/shard_map/score/pallas_call | solution.py:415
  71.3 0.0 collective-permute-done.2.refs_3_
  71.3 0.0 copy-start.8
  71.3 0.7 collective-permute-done.1.refs_2_
  72.1 1.6 %collective-permute-done.refs_1_ = bf16[272,768]{1,0:T(8,128)(2,1)} collective-permute-done((bf16[272,768]{1,0:T(8,128)(2,1)}, bf16[272,768]{1,0:T(8,128)(2,1)}, u32[]{:S(2)}, u32[]{:S(2)}) %collective-permute-start) | collective-permute-done | bytes 417824 | tf_op jit(solution)/shard_map/ppermute | solution.py:479
  73.7 0.0 copy-done.8
  73.7 0.0 copy-done.9
  73.7 11.7 %score.3 = (f32[16,512]{1,0:T(8,128)}, f32[16,512]{1,0:T(8,128)}, f32[16,512]{1,0:T(8,128)}, f32[16,512]{1,0:T(8,128)}, f32[16,512]{1,0:T(8,128)}, /*index=5*/f3...) custom-call(bf16[272,768]{1,0:T(8,128)(2,1)} %get-tuple-element.17.refs_0_, ...), custom_call_target="tpu_custom_call" | custom-call | flops 6442450944 | bytes 6291456 | tf_op jit(solution)/shard_map/score/pallas_call | solution.py:415
  85.4 1.1 %collective-permute-start.6 = (f32[16,512]{1,0:T(8,128)}, f32[16,512]{1,0:T(8,128)S(1)}, u32[]{:S(2)}, u32[]{:S(2)}) collective-permute-start(f32[16,512]{1,0:T(8,128)} %get-tuple-element.20), channel_id=1, source_target_pairs={{1,0},{0,1},{3,2},{2,3},{5,4},{4,5},{7,6},{6,7},{9,8},{8,9},{11,10... | collective-permute-start | bytes 98312 | tf_op jit(solution)/shard_map/ppermute | solution.py:479
  86.5 2.3 %collective-permute-start.7 = (f32[16,512]{1,0:T(8,128)}, f32[16,512]{1,0:T(8,128)S(1)}, u32[]{:S(2)}, u32[]{:S(2)}) collective-permute-start(f32[16,512]{1,0:T(8,128)} %get-tuple-element.21), channel_id=1, source_target_pairs={{2,0},{3,1},{4,2},{5,3},{6,4},{7,5},{0,6},{1,7},{10,8},{11,9},{12,... | collective-permute-start | bytes 98312 | tf_op jit(solution)/shard_map/ppermute | solution.py:479
  88.9 0.8 collective-permute-start.8
  89.7 0.9 collective-permute-start.9
  90.6 0.1 collective-permute-start.10
  90.6 0.0 collective-permute-done.6.refs_1_
  90.6 3.2 %collective-permute-start.11 = (f32[16,512]{1,0:T(8,128)}, f32[16,512]{1,0:T(8,128)S(1)}, u32[]{:S(2)}, u32[]{:S(2)}) collective-permute-start(f32[16,512]{1,0:T(8,128)} %get-tuple-element.25), channel_id=1, source_target_pairs={{4,0},{5,1},{6,2},{7,3},{0,4},{1,5},{2,6},{3,7},{12,8},{13,9},{14,... | collective-permute-start | bytes 98312 | tf_op jit(solution)/shard_map/ppermute | solution.py:479
  93.9 0.0 collective-permute-done.7.refs_2_
  93.9 0.4 collective-permute-start.12
  94.2 0.0 all-to-all-done.recv_ref
  94.2 0.8 copy-done
  95.1 3.0 %place.1 = (bf16[16,768]{1,0:T(8,128)(2,1)}, s32[1,128]{1,0:T(1,128)}) custom-call(f32[128,8,128]{2,1,0:T(8,128)} %copy-done, bf16[512,768]{1,0:T(8,128)(2,1)} %cent_ref.1), custom_call_target="tpu_custom_call" | custom-call | tf_op jit(solution)/shard_map/place/pallas_call | solution.py:320
  98.1 0.0 collective-permute-done.8.refs_3_
  98.1 0.0 collective-permute-done.9.refs_4_
  98.1 0.0 copy-start.4
  98.1 0.0 collective-permute-done.10.refs_5_
  98.1 0.0 copy-start.5
  98.1 0.0 collective-permute-done.11.refs_6_
  98.1 0.8 collective-permute-done.12.refs_7_
  98.9 0.0 copy-done.3
  99.0 0.6 copy-done.7
  99.5 1.8 %finish.1 = bf16[128,512]{1,0:T(8,128)(2,1)} custom-call(bf16[512]{0:T(512)(128)(2,1)} %bias_ref.1, f32[16,512]{1,0:T(8,128)} %get-tuple-element.19.refs_0_, f32[16,512]{1,0:T(8,128)} %copy-done.1, f32[16,512]{1,0:T(8,128)} %copy-done.2, f32[16,512]{1,0:T(8,128)} %copy-done.3, f32[16,512]{1,0:T(8,128)} %copy-done.4, f32[16,512]{1,0:T(8,128)} %copy-done.5, ...), custom_call_target="tpu_custom_call" | custom-call | tf_op jit(solution)/shard_map/finish/pallas_call | solution.py:462
  (13 shorter events, 0.0 us)
Async XLA Ops:
  7.2 53.4 %all-gather.2.cloned.1.call-start = ((), (), s32[]{:S(2)}) async-start(), calls=%async_computation.1 | async-start | bytes 7077888 | tf_op jit(solution)/shard_map/all_gather | solution.py:502
  26.5 31.1 %collective-permute-start.5 = (bf16[272,768]{1,0:T(8,128)(2,1)}, bf16[272,768]{1,0:T(8,128)(2,1)S(1)}, u32[]{:S(2)}, u32[]{:S(2)}) collective-permute-start(bf16[272,768]{1,0:T(8,128)(2,1)} %get-tuple-element.18.refs_0_), channel_id=1, source_target_pairs={{16,0},{17,1},{18,2},{19,3},{20,4},{21,5},{22,6},{23,7},{24,8},{25... | collective-permute-start | bytes 1253384 | tf_op jit(solution)/shard_map/ppermute | solution.py:479
  30.4 30.1 %collective-permute-start.4 = (bf16[272,768]{1,0:T(8,128)(2,1)}, bf16[272,768]{1,0:T(8,128)(2,1)}, u32[]{:S(2)}, u32[]{:S(2)}) collective-permute-start(bf16[272,768]{1,0:T(8,128)(2,1)} %get-tuple-element.18.refs_0_), channel_id=1, source_target_pairs={{24,0},{25,1},{26,2},{27,3},{28,4},{29,5},{30,6},{31,7},{0,8},{1,9... | collective-permute-start | bytes 1253384 | tf_op jit(solution)/shard_map/ppermute | solution.py:479
  30.8 29.7 %collective-permute-start.3 = (bf16[272,768]{1,0:T(8,128)(2,1)}, bf16[272,768]{1,0:T(8,128)(2,1)}, u32[]{:S(2)}, u32[]{:S(2)}) collective-permute-start(bf16[272,768]{1,0:T(8,128)(2,1)} %get-tuple-element.18.refs_0_), channel_id=1, source_target_pairs={{8,0},{9,1},{10,2},{11,3},{12,4},{13,5},{14,6},{15,7},{16,8},{17,9... | collective-permute-start | bytes 1253384 | tf_op jit(solution)/shard_map/ppermute | solution.py:479
  43.2 28.1 %collective-permute-start.2 = (bf16[272,768]{1,0:T(8,128)(2,1)}, bf16[272,768]{1,0:T(8,128)(2,1)S(1)}, u32[]{:S(2)}, u32[]{:S(2)}) collective-permute-start(bf16[272,768]{1,0:T(8,128)(2,1)} %get-tuple-element.17.refs_0_), channel_id=1, source_target_pairs={{16,0},{17,1},{18,2},{19,3},{20,4},{21,5},{22,6},{23,7},{24,8},{25... | collective-permute-start | bytes 1253384 | tf_op jit(solution)/shard_map/ppermute | solution.py:479
  43.3 28.8 %collective-permute-start.1 = (bf16[272,768]{1,0:T(8,128)(2,1)}, bf16[272,768]{1,0:T(8,128)(2,1)S(1)}, u32[]{:S(2)}, u32[]{:S(2)}) collective-permute-start(bf16[272,768]{1,0:T(8,128)(2,1)} %get-tuple-element.17.refs_0_), channel_id=1, source_target_pairs={{24,0},{25,1},{26,2},{27,3},{28,4},{29,5},{30,6},{31,7},{0,8},{1,9... | collective-permute-start | bytes 1253384 | tf_op jit(solution)/shard_map/ppermute | solution.py:479
  45.9 48.4 %all-to-all-start = ((f32[128,8,128]{2,1,0:T(8,128)}), f32[128,8,128]{2,1,0:T(8,128)S(1)}, u32[]{:S(2)}, u32[]{:S(2)}) async-start(f32[128,8,128]{2,1,0:T(8,128)} %route.1), calls=%async_computation | async-start | bytes 1048576 | tf_op jit(solution)/shard_map/all_to_all | solution.py:514
  57.6 3.0 %copy-start.10 = (bf16[272,768]{1,0:T(8,128)(2,1)}, bf16[272,768]{1,0:T(8,128)(2,1)S(1)}, u32[]{:S(2)}) copy-start(bf16[272,768]{1,0:T(8,128)(2,1)S(1)} %collective-permute-done.5.refs_3_) | copy-start | bytes 1253380
  57.6 16.0 %collective-permute-start = (bf16[272,768]{1,0:T(8,128)(2,1)}, bf16[272,768]{1,0:T(8,128)(2,1)}, u32[]{:S(2)}, u32[]{:S(2)}) collective-permute-start(bf16[272,768]{1,0:T(8,128)(2,1)} %get-tuple-element.17.refs_0_), channel_id=1, source_target_pairs={{8,0},{9,1},{10,2},{11,3},{12,4},{13,5},{14,6},{15,7},{16,8},{17,9... | collective-permute-start | bytes 1253384 | tf_op jit(solution)/shard_map/ppermute | solution.py:479
  71.3 2.3 %copy-start.8 = (bf16[272,768]{1,0:T(8,128)(2,1)}, bf16[272,768]{1,0:T(8,128)(2,1)S(1)}, u32[]{:S(2)}) copy-start(bf16[272,768]{1,0:T(8,128)(2,1)S(1)} %collective-permute-done.2.refs_3_) | copy-start | bytes 1253380
  72.1 1.6 %copy-start.9 = (bf16[272,768]{1,0:T(8,128)(2,1)}, bf16[272,768]{1,0:T(8,128)(2,1)S(1)}, u32[]{:S(2)}) copy-start(bf16[272,768]{1,0:T(8,128)(2,1)S(1)} %collective-permute-done.1.refs_2_) | copy-start | bytes 1253380
  85.4 5.3 %collective-permute-start.6 = (f32[16,512]{1,0:T(8,128)}, f32[16,512]{1,0:T(8,128)S(1)}, u32[]{:S(2)}, u32[]{:S(2)}) collective-permute-start(f32[16,512]{1,0:T(8,128)} %get-tuple-element.20), channel_id=1, source_target_pairs={{1,0},{0,1},{3,2},{2,3},{5,4},{4,5},{7,6},{6,7},{9,8},{8,9},{11,10... | collective-permute-start | bytes 98312 | tf_op jit(solution)/shard_map/ppermute | solution.py:479
  86.5 7.3 %collective-permute-start.7 = (f32[16,512]{1,0:T(8,128)}, f32[16,512]{1,0:T(8,128)S(1)}, u32[]{:S(2)}, u32[]{:S(2)}) collective-permute-start(f32[16,512]{1,0:T(8,128)} %get-tuple-element.21), channel_id=1, source_target_pairs={{2,0},{3,1},{4,2},{5,3},{6,4},{7,5},{0,6},{1,7},{10,8},{11,9},{12,... | collective-permute-start | bytes 98312 | tf_op jit(solution)/shard_map/ppermute | solution.py:479
  88.9 9.2 %collective-permute-start.8 = (f32[16,512]{1,0:T(8,128)}, f32[16,512]{1,0:T(8,128)S(1)}, u32[]{:S(2)}, u32[]{:S(2)}) collective-permute-start(f32[16,512]{1,0:T(8,128)} %get-tuple-element.22), channel_id=1, source_target_pairs={{3,0},{2,1},{5,2},{4,3},{7,4},{6,5},{1,6},{0,7},{11,8},{10,9},{13,... | collective-permute-start | bytes 98312 | tf_op jit(solution)/shard_map/ppermute | solution.py:479
  89.7 8.4 %collective-permute-start.9 = (f32[16,512]{1,0:T(8,128)}, f32[16,512]{1,0:T(8,128)S(1)}, u32[]{:S(2)}, u32[]{:S(2)}) collective-permute-start(f32[16,512]{1,0:T(8,128)} %get-tuple-element.23), channel_id=1, source_target_pairs={{6,0},{7,1},{0,2},{1,3},{2,4},{3,5},{4,6},{5,7},{14,8},{15,9},{8,1... | collective-permute-start | bytes 98312 | tf_op jit(solution)/shard_map/ppermute | solution.py:479
  90.6 7.5 %collective-permute-start.10 = (f32[16,512]{1,0:T(8,128)}, f32[16,512]{1,0:T(8,128)S(1)}, u32[]{:S(2)}, u32[]{:S(2)}) collective-permute-start(f32[16,512]{1,0:T(8,128)} %get-tuple-element.24), channel_id=1, source_target_pairs={{7,0},{6,1},{1,2},{0,3},{3,4},{2,5},{5,6},{4,7},{15,8},{14,9},{9,1... | collective-permute-start | bytes 98312 | tf_op jit(solution)/shard_map/ppermute | solution.py:479
  90.6 8.3 %copy-start.1 = (f32[16,512]{1,0:T(8,128)}, f32[16,512]{1,0:T(8,128)S(1)}, u32[]{:S(2)}) copy-start(f32[16,512]{1,0:T(8,128)S(1)} %collective-permute-done.6.refs_1_) | copy-start | bytes 98308
  90.6 7.5 %collective-permute-start.11 = (f32[16,512]{1,0:T(8,128)}, f32[16,512]{1,0:T(8,128)S(1)}, u32[]{:S(2)}, u32[]{:S(2)}) collective-permute-start(f32[16,512]{1,0:T(8,128)} %get-tuple-element.25), channel_id=1, source_target_pairs={{4,0},{5,1},{6,2},{7,3},{0,4},{1,5},{2,6},{3,7},{12,8},{13,9},{14,... | collective-permute-start | bytes 98312 | tf_op jit(solution)/shard_map/ppermute | solution.py:479
  93.9 5.1 %copy-start.2 = (f32[16,512]{1,0:T(8,128)}, f32[16,512]{1,0:T(8,128)S(1)}, u32[]{:S(2)}) copy-start(f32[16,512]{1,0:T(8,128)S(1)} %collective-permute-done.7.refs_2_) | copy-start | bytes 98308
  93.9 5.1 %collective-permute-start.12 = (f32[16,512]{1,0:T(8,128)}, f32[16,512]{1,0:T(8,128)S(1)}, u32[]{:S(2)}, u32[]{:S(2)}) collective-permute-start(f32[16,512]{1,0:T(8,128)} %get-tuple-element.26), channel_id=1, source_target_pairs={{5,0},{4,1},{7,2},{6,3},{1,4},{0,5},{3,6},{2,7},{13,8},{12,9},{15,... | collective-permute-start | bytes 98312 | tf_op jit(solution)/shard_map/ppermute | solution.py:479
  94.2 0.8 copy-start
  98.1 0.9 copy-start.3
  98.1 0.9 copy-start.4
  98.1 0.9 copy-start.5
  98.1 0.8 copy-start.6
  98.9 0.6 copy-start.7
Sparse Core Ops, SparseCore 0:
  9.7 44.4 all-gather.1

commit v3 on v2

--- a/solution.py
+++ b/solution.py
@@ -69,25 +69,95 @@
     return center * lax.rsqrt(spread + 1e-06)
 
 
-def attend_kernel(
-    lengths_ref, hidden_hbm, attn_hbm, out_hbm, first_ref,
-    hidden, attn_v, out_v, joined, context, sems,
+def feed(
+    offset, lengths_ref, lists_ref, gain_ref, send_ref, first, up_v, down_v, head_v, wide, acc, waits
+):
+    rows, width = first.shape
+    passages = rows // SEQ
+    chunks = up_v.shape[0]
+    half = chunks // 2
+
+    def up(c):
+        return jnp.dot(first[...], up_v[c], preferred_element_type=F32)
+
+    for part, ready in zip((0, half), waits):
+        for d in ready:
+            d.wait()
+        current = up(part)
+        for c in range(part, part + half):
+            following = up(c + 1) if c + 1 < part + half else None
+            wide[:, c * FCH : (c + 1) * FCH] = gelu(current).astype(BF16)
+            current = following
+    second = first[...].astype(F32) + jnp.dot(
+        wide[...], down_v[...], preferred_element_type=F32
+    )
+    layer_out = normalize(second).astype(BF16)
+    first[...] = layer_out
+    middle = gelu(jnp.dot(layer_out, head_v[...], preferred_element_type=F32))
+    acc[...] = normalize(middle) * gain_ref[...].reshape(1, width)
+
+    row = lax.broadcasted_iota(I32, (SEQ, 1), 0)
+    slots = lists_ref.shape[1]
+    block_id = lax.broadcasted_iota(I32, (BLOCK, slots), 0)
+    send_ref[rows:, :] = jnp.zeros((EXTRA, width), BF16)
+    for p in range(passages):
+        base = p * SEQ
+        send_ref[base : base + SEQ, :] = jnp.where(
+            row < lengths_ref[offset + p], acc[base : base + SEQ, :], acc[base : base + 1, :]
+        ).astype(BF16)
+        hit = (lists_ref[offset + p : offset + p + 1, :] == block_id).astype(F32).astype(BF16)
+        count = lax.dot_general(
+            jnp.ones((8, slots), BF16), hit, (((1,), (1,)), ((), ())), preferred_element_type=F32
+        )
+        send_ref[rows + p : rows + p + 1, 0:BLOCK] = count[0:1, :].astype(BF16)
+
+
+def feed_moves(up_hbm, down_hbm, head_hbm, up_v, down_v, head_v):
+    moves = [
+        (up_hbm.at[:, pl.ds(c * FCH, FCH)], up_v.at[c]) for c in range(up_v.shape[0])
+    ]
+    return moves + [(down_hbm, down_v), (head_hbm, head_v)]
+
+
+def feed_scratch(rows, width, ff):
+    return [
+        pltpu.VMEM((rows, width), BF16),
+        pltpu.VMEM((ff // FCH, width, FCH), BF16),
+        pltpu.VMEM((ff, width), BF16),
+        pltpu.VMEM((width, width), BF16),
+        pltpu.VMEM((rows, ff), BF16),
+        pltpu.VMEM((rows, width), F32),
+    ]
+
+
+def start(moves, sems):
+    dma = [pltpu.make_async_copy(s, d, sems.at[i]) for i, (s, d) in enumerate(moves)]
+    for d in dma:
+        d.start()
+    return dma
+
+
+def lead_kernel(
+    lengths_ref, hidden_hbm, lists_ref, gain_ref, attn_hbm, out_hbm, up_hbm, down_hbm, head_hbm,
+    send_ref, dense_ref, rest_ref,
+    hidden, attn_v, out_v, joined, context, first, up_v, down_v, head_v, wide, acc, sems,
 ):
     rows, width = hidden.shape
     passages = rows // SEQ
+    lead = first.shape[0] // SEQ
     pairs = width // 128
     moves = [(hidden_hbm, hidden)]
     for k in range(3):
         moves.append((attn_hbm.at[:, pl.ds(k * width, width)], attn_v.at[k]))
     moves.append((out_hbm, out_v))
-    dma = [pltpu.make_async_copy(s, d, sems.at[i]) for i, (s, d) in enumerate(moves)]
-    for d in dma:
-        d.start()
+    dma = start(
+        moves + feed_moves(up_hbm, down_hbm, head_hbm, up_v, down_v, head_v), sems
+    )
     dma[0].wait()
     dma[1].wait()
     for k in range(3):
         if k == 1:
-            for d in dma[2:]:
+            for d in dma[2:5]:
                 d.wait()
         joined[:, k * width : (k + 1) * width] = jnp.dot(
             hidden[...], attn_v[k], preferred_element_type=F32
@@ -96,7 +166,6 @@
     low = lax.broadcasted_iota(I32, (SEQ, 128), 1) < HEAD
     lane = lax.broadcasted_iota(I32, (2 * SEQ, 128), 1)
     scale = math.log2(math.e) / math.sqrt(HEAD)
-
     for p in range(passages):
         at = slice(p * SEQ, (p + 1) * SEQ)
         length = lengths_ref[p]
@@ -120,161 +189,111 @@
         mixed = hidden[at, :].astype(F32) + jnp.dot(
             context[at, :], out_v[...], preferred_element_type=F32
         )
-        first_ref[at, :] = normalize(mixed).astype(BF16)
-
-
-def attend(hidden, lengths, attn_w, out_w):
+        into, k = (first, p) if p < lead else (rest_ref, p - lead)
+        into[k * SEQ : (k + 1) * SEQ, :] = normalize(mixed).astype(BF16)
+
+    feed(
+        0, lengths_ref, lists_ref, gain_ref, send_ref, first, up_v, down_v, head_v, wide, acc,
+        (dma[5:], ()),
+    )
+    for p in range(lead):
+        dense_ref[p : p + 1, :] = first[p * SEQ : p * SEQ + 1, :].astype(F32)
+
+
+def encode_lead(hidden, lengths, block_list, gain, attn_w, out_w, up_w, down_w, head_w):
     rows, width = hidden.shape
+    part = rows // PARTS
+    ff = up_w.shape[1]
     return pl.pallas_call(
-        attend_kernel,
-        out_shape=jax.ShapeDtypeStruct((rows, width), BF16),
-        in_specs=[smem(), hbm(), hbm(), hbm()],
-        out_specs=vmem(),
+        lead_kernel,
+        out_shape=(
+            jax.ShapeDtypeStruct((part + EXTRA, width), BF16),
+            jax.ShapeDtypeStruct((8, width), F32),
+            jax.ShapeDtypeStruct((rows - part, width), BF16),
+        ),
+        in_specs=[smem(), hbm(), vmem(), vmem()] + [hbm()] * 5,
+        out_specs=(vmem(), vmem(), vmem()),
         scratch_shapes=[
             pltpu.VMEM((rows, width), BF16),
             pltpu.VMEM((3, width, width), BF16),
             pltpu.VMEM((width, width), BF16),
             pltpu.VMEM((rows, 3 * width), BF16),
             pltpu.VMEM((rows, width), BF16),
-            pltpu.SemaphoreType.DMA((5,)),
-        ],
+        ] + feed_scratch(part, width, ff) + [pltpu.SemaphoreType.DMA((7 + ff // FCH,))],
         compiler_params=pltpu.CompilerParams(vmem_limit_bytes=VMEM_BYTES),
         cost_estimate=pl.CostEstimate(
             flops=2 * rows * width * 4 * width, transcendentals=0, bytes_accessed=8 * width * width
         ),
-        name="attend",
-    )(lengths, hidden, attn_w, out_w)
-
-
-def forward_kernel(
-    offset,
-    lengths_ref, first_hbm, lists_ref, gain_ref, up_hbm, down_hbm, head_hbm,
-    send_ref, dense_ref,
+        name="lead",
+    )(lengths, hidden, block_list, gain, attn_w, out_w, up_w, down_w, head_w)
+
+
+def tail_kernel(
+    lengths_ref, clusters_ref, rest_hbm, lists_ref, gain_ref, dense_ref, up_hbm, down_hbm, head_hbm,
+    send_ref, route_ref,
     first, up_v, down_v, head_v, wide, acc, sems,
 ):
     rows, width = first.shape
-    passages = rows // SEQ
-    chunks = up_v.shape[0]
-    half = chunks // 2
-    moves = [(first_hbm.at[pl.ds(offset * SEQ, rows), :], first)]
-    for c in range(chunks):
-        moves.append((up_hbm.at[:, pl.ds(c * FCH, FCH)], up_v.at[c]))
-    moves.append((down_hbm, down_v))
-    moves.append((head_hbm, head_v))
-    dma = [pltpu.make_async_copy(s, d, sems.at[i]) for i, (s, d) in enumerate(moves)]
-    for d in dma:
-        d.start()
-
-    def up(c):
-        return jnp.dot(first[...], up_v[c], preferred_element_type=F32)
-
-    for part in (0, half):
-        for d in dma[1 + part : 1 + part + half] + (dma[:1] if part == 0 else dma[1 + chunks :]):
-            d.wait()
-        current = up(part)
-        for c in range(part, part + half):
-            following = up(c + 1) if c + 1 < part + half else None
-            wide[:, c * FCH : (c + 1) * FCH] = gelu(current).astype(BF16)
-            current = following
-    second = first[...].astype(F32) + jnp.dot(
-        wide[...], down_v[...], preferred_element_type=F32
-    )
-    layer_out = normalize(second).astype(BF16)
-    first[...] = layer_out
-    middle = gelu(jnp.dot(layer_out, head_v[...], preferred_element_type=F32))
-    acc[...] = normalize(middle) * gain_ref[...].reshape(1, width)
-
-    row = lax.broadcasted_iota(I32, (SEQ, 1), 0)
-    slots = lists_ref.shape[1]
-    block_id = lax.broadcasted_iota(I32, (BLOCK, slots), 0)
-    send_ref[rows:, :] = jnp.zeros((EXTRA, width), BF16)
-    for p in range(passages):
-        base = p * SEQ
-        send_ref[base : base + SEQ, :] = jnp.where(
-            row < lengths_ref[offset + p], acc[base : base + SEQ, :], acc[base : base + 1, :]
-        ).astype(BF16)
-        dense_ref[p : p + 1, :] = first[base : base + 1, :].astype(F32)
-        hit = (lists_ref[offset + p : offset + p + 1, :] == block_id).astype(F32).astype(BF16)
-        count = lax.dot_general(
-            jnp.ones((8, slots), BF16), hit, (((1,), (1,)), ((), ())), preferred_element_type=F32
-        )
-        send_ref[rows + p : rows + p + 1, 0:BLOCK] = count[0:1, :].astype(BF16)
-
-
-def forward(part, first, lengths, block_list, gain, up_w, down_w, head_w):
-    width = first.shape[1]
-    passages = lengths.shape[0] // PARTS
-    rows = passages * SEQ
+    lead = clusters_ref.shape[0] - rows // SEQ
+    half = up_v.shape[0] // 2
+    dma = start(
+        [(rest_hbm, first)] + feed_moves(up_hbm, down_hbm, head_hbm, up_v, down_v, head_v), sems
+    )
+    feed(
+        lead, lengths_ref, lists_ref, gain_ref, send_ref, first, up_v, down_v, head_v, wide, acc,
+        (dma[: 1 + half], dma[1 + half :]),
+    )
+    dense = [dense_ref[p : p + 1, :] for p in range(lead)]
+    dense += [first[p : p + 1, :].astype(F32) for p in range(0, rows, SEQ)]
+
+    devices = route_ref.shape[0]
+    pieces = width // META
+    row = lax.broadcasted_iota(I32, (devices, 1), 0)
+    lane = lax.broadcasted_iota(I32, (devices, META), 1)
+    term = lax.axis_index("term").astype(I32)
+    device = lax.axis_index("grp").astype(I32) * lax.axis_size("term") + term
+    parts = [jnp.zeros((devices, META), F32) for _ in range(pieces)]
+    meta = jnp.zeros((devices, META), I32)
+    for p, values in enumerate(dense):
+        cluster = clusters_ref[p]
+        owner = lax.div(cluster, CL_DEV)
+        mine = row == owner
+        for k in range(pieces):
+            parts[k] = jnp.where(mine, values[:, k * META : (k + 1) * META], parts[k])
+        word = jnp.where(lane == 0, 1, 0)
+        word = jnp.where(lane == 1, device, word)
+        word = jnp.where(lane == 2, p, word)
+        word = jnp.where(lane == 3, cluster - owner * CL_DEV, word)
+        meta = jnp.where(mine, word, meta)
+    for k in range(pieces):
+        route_ref[:, k, :] = parts[k]
+    route_ref[:, pieces, :] = meta.astype(F32)
+    route_ref[:, pieces + 1, :] = jnp.zeros((devices, META), F32)
+
+
+def encode_tail(rest, lengths, clusters, block_list, gain, dense, up_w, down_w, head_w, devices):
+    rows, width = rest.shape
     ff = up_w.shape[1]
-    chunks = ff // FCH
     return pl.pallas_call(
-        functools.partial(forward_kernel, part * passages),
+        tail_kernel,
         out_shape=(
             jax.ShapeDtypeStruct((rows + EXTRA, width), BF16),
-            jax.ShapeDtypeStruct((8, width), F32),
+            jax.ShapeDtypeStruct((devices, 8, META), F32),
         ),
-        in_specs=[smem(), hbm(), vmem(), vmem(), hbm(), hbm(), hbm()],
+        in_specs=[smem(), smem(), hbm(), vmem(), vmem(), vmem(), hbm(), hbm(), hbm()],
         out_specs=(vmem(), vmem()),
-        scratch_shapes=[
-            pltpu.VMEM((rows, width), BF16),
-            pltpu.VMEM((chunks, width, FCH), BF16),
-            pltpu.VMEM((ff, width), BF16),
-            pltpu.VMEM((width, width), BF16),
-            pltpu.VMEM((rows, ff), BF16),
-            pltpu.VMEM((rows, width), F32),
-            pltpu.SemaphoreType.DMA((3 + chunks,)),
-        ],
+        scratch_shapes=feed_scratch(rows, width, ff)
+        + [pltpu.SemaphoreType.DMA((3 + ff // FCH,))],
         compiler_params=pltpu.CompilerParams(vmem_limit_bytes=VMEM_BYTES),
         cost_estimate=pl.CostEstimate(flops=1, transcendentals=0, bytes_accessed=1),
-        name="forward",
-    )(lengths, first, block_list, gain, up_w, down_w, head_w)
+        name="tail",
+    )(lengths, clusters, rest, block_list, gain, dense, up_w, down_w, head_w)
 
 
 def here():
     term = lax.axis_index("term").astype(I32)
     chip = lax.div(term, 2)
     return lax.div(chip, NX), lax.rem(chip, NX), lax.rem(term, 2)
-
-
-def route_kernel(parts, clusters_ref, *refs):
-    dense, out_ref = refs[:parts], refs[parts]
-    devices = out_ref.shape[0]
-    pieces = dense[0].shape[1] // META
-    passages = clusters_ref.shape[0] // parts
-    row = lax.broadcasted_iota(I32, (devices, 1), 0)
-    lane = lax.broadcasted_iota(I32, (devices, META), 1)
-    term = lax.axis_index("term").astype(I32)
-    device = lax.axis_index("grp").astype(I32) * lax.axis_size("term") + term
-    rows = [jnp.zeros((devices, META), F32) for _ in range(pieces)]
-    meta = jnp.zeros((devices, META), I32)
-    for part in range(parts):
-        for p in range(passages):
-            cluster = clusters_ref[part * passages + p]
-            owner = lax.div(cluster, CL_DEV)
-            mine = row == owner
-            for k in range(pieces):
-                piece = dense[part][p : p + 1, k * META : (k + 1) * META]
-                rows[k] = jnp.where(mine, piece, rows[k])
-            word = jnp.where(lane == 0, 1, 0)
-            word = jnp.where(lane == 1, device, word)
-            word = jnp.where(lane == 2, part * passages + p, word)
-            word = jnp.where(lane == 3, cluster - owner * CL_DEV, word)
-            meta = jnp.where(mine, word, meta)
-    for k in range(pieces):
-        out_ref[:, k, :] = rows[k]
-    out_ref[:, pieces, :] = meta.astype(F32)
-    out_ref[:, pieces + 1, :] = jnp.zeros((devices, META), F32)
-
-
-def route(cluster_ids, dense, devices):
-    return pl.pallas_call(
-        functools.partial(route_kernel, len(dense)),
-        out_shape=jax.ShapeDtypeStruct((devices, 8, META), F32),
-        in_specs=[smem()] + [vmem()] * len(dense),
-        out_specs=vmem(),
-        cost_estimate=pl.CostEstimate(flops=1, transcendentals=0, bytes_accessed=1),
-        name="route",
-    )(cluster_ids, *dense)
 
 
 def place_kernel(passages, recv_ref, cent_ref, dense_ref, slot_ref):
@@ -502,28 +521,30 @@
     vocab = lax.all_gather(
         vocab_weight, "term", axis=0, tiled=True, axis_index_groups=rows_of_chips
     )
-    first = attend(hidden_states, lengths, attn_weight, out_weight)
-    dense, received = [], []
-    for part in range(PARTS):
-        payload, rows = forward(
-            part, first, lengths, block_list, head_gain, up_weight, down_weight, head_weight
-        )
-        dense.append(rows)
-        received.append([payload] + [shift(payload, d, 0, 0) for d in OFFSETS[1:]])
-
-    recv = lax.all_to_all(
-        route(cluster_ids, dense, devices), ("grp", "term"), split_axis=0, concat_axis=0, tiled=True
-    )
-
-
-    scored = score(received[0], vocab, None)
-    sent = score(received[1], vocab, scored)
+    def spread(payload):
+        return [payload] + [shift(payload, d, 0, 0) for d in OFFSETS[1:]]
+
+    payload, dense, rest = encode_lead(
+        hidden_states, lengths, block_list, head_gain,
+        attn_weight, out_weight, up_weight, down_weight, head_weight,
+    )
+    early = spread(payload)
+    payload, routed = encode_tail(
+        rest, lengths, cluster_ids, block_list, head_gain, dense,
+        up_weight, down_weight, head_weight, devices,
+    )
+    late = spread(payload)
+    recv = lax.all_to_all(routed, ("grp", "term"), split_axis=0, concat_axis=0, tiled=True)
+
+    scored = score(early, vocab, None)
+    dense_part, slot_part = place(recv, centroids, passages)
+    scored, dense_part, slot_part = lax.optimization_barrier((scored, dense_part, slot_part))
+    sent = score(late, vocab, scored)
     pieces = []
     for dx, dc in PEERS:
         back = sent[PEERS.index(((NX - dx) % NX, dc))]
         pieces.append(back if (dx, dc) == (0, 0) else shift(back, 0, dx, dc))
     sparse = finish(vocab_bias, pieces)
-    dense_part, slot_part = place(recv, centroids, passages)
     return (sparse, dense_part[None], slot_part[:, :CAP])
 
 

time: 109 us -> 124 us (1.14)
  waiting for transfers between devices: 3.83 us -> 27.3 us
  Pallas kernels: 57.8 us -> 52.3 us
  starting transfers between devices: 30.9 us -> 26 us
  local copies, waits for them, and re-layouts: 1.41 us -> 3.77 us
    all_to_all x1, waiting for transfers between devices: 0.01 us -> 12.2 us  [body(): lax.all_to_all(routed, ('grp', 'term'), split_axis=0, concat_axis=0, tile...]
    ppermute x13, waiting for transfers between devices: 3.14 us -> 14.4 us  [shift(): return lax.ppermute(value, 'term', pairs)]
    pallas_call x4 -> x2, Pallas kernels: 30.6 us -> 25.1 us  [the longest x1 13.8 us: encode_lead(): pl.pallas_call(lead_kernel, out_shape=(jax.ShapeDtypeStruct((part + EXTRA...]
    ppermute x13, starting transfers between devices: 19.1 us -> 15.1 us  [shift(): return lax.ppermute(value, 'term', pairs)]
    unnamed x22 -> x28, local copies, waits for them, and re-layouts: 1.41 us -> 3.77 us
  transfers between devices with their start and end apart: 15 -> 15, of which waited for: 3 -> 6; matrix products, arithmetic and copies ran while one was open for 0% -> 0% of each run, Pallas kernels for 52% -> 31%
where the time goes in v3:
time: 124 us
  Pallas kernels  52.3 us (42%)
  waiting for transfers between devices  27.3 us (22%)
  starting transfers between devices  26 us (21%)
  between operations  14.2 us (11%)
  local copies, waits for them, and re-layouts  3.77 us (3%)
    pallas_call x2, Pallas kernels, score(): pl.pallas_call(kernel, out_shape=(piece,) * shards if last else whole, in...  22.4 us
    ppermute x13, starting transfers between devices, shift(): return lax.ppermute(value, 'term', pairs)  15.1 us
    ppermute x13, waiting for transfers between devices, shift(): return lax.ppermute(value, 'term', pairs)  14.4 us
    pallas_call x1, Pallas kernels, encode_lead(): pl.pallas_call(lead_kernel, out_shape=(jax.ShapeDtypeStruct((part + EXTRA...  13.8 us
    all_to_all x1, waiting for transfers between devices, body(): lax.all_to_all(routed, ('grp', 'term'), split_axis=0, concat_axis=0, tile...  12.2 us
    pallas_call x1, Pallas kernels, encode_tail(): pl.pallas_call(tail_kernel, out_shape=(jax.ShapeDtypeStruct((rows + EXTRA...  11.3 us
    all_to_all x1, starting transfers between devices, body(): lax.all_to_all(routed, ('grp', 'term'), split_axis=0, concat_axis=0, tile...  10.9 us
    unnamed x28, local copies, waits for them, and re-layouts  3.77 us
  transfers between devices with their start and end apart: 15, of which 6 were waited for; matrix products, arithmetic and copies ran while one was open for 0% of the time, Pallas kernels for 31%

profile of v3, /device:TPU:1, one launch (start us, length us, event | category | flops | bytes accessed | tf_op | source)
XLA Modules:
  0.0 123.6 jit_solution(3279875372156586512)
XLA Ops:
  7.2 0.0 all-gather.2.cloned.1.call-start
  7.2 0.7 all-gather.2.cloned.1.call-update
  7.9 13.8 %lead.1 = (bf16[272,768]{1,0:T(8,128)(2,1)}, f32[8,768]{1,0:T(8,128)}, bf16[256,768]{1,0:T(8,128)(2,1)}) custom-call(s32[4]{0:T(128)} %lengths_ref.3, bf16[512,768]{1,0:T(8,128)(2,1)} %hidden_hbm.1, s32[4,96]{1,0:T(4,128)} %lists_ref.3, f32[768]{0:T(1024)} %gain_ref.3, bf16[768,2304]{1,0:T(8,128)(2,1)} %attn_hbm.1, bf16[768,768]{1,0:T(8,128)(2,1)} %out_hbm.1, ...), custom_call_target="tpu_custom_call" | custom-call | flops 2415919104 | bytes 4718592 | tf_op jit(solution)/shard_map/lead/pallas_call | solution.py:207
  21.7 0.0 copy-start.8
  21.7 11.3 %tail.1 = (bf16[272,768]{1,0:T(8,128)(2,1)}, f32[128,8,128]{2,1,0:T(8,128)}) custom-call(s32[4]{0:T(128)} %lengths_ref.3, s32[4]{0:T(128)} %clusters_ref.1, bf16[256,768]{1,0:T(8,128)(2,1)} %get-tuple-element.21.rest_hbm, s32[4,96]{1,0:T(4,128)} %lists_ref.3, f32[768]{0:T(1024)} %gain_ref.3, f32[8,768]{1,0:T(8,128)} %get-tuple-element.22.dense_ref, ...), custom_call_target="tpu_custom_call" | custom-call | flops 1 | bytes 1 | tf_op jit(solution)/shard_map/tail/pallas_call | solution.py:277
  33.1 10.9 %all-to-all-start = ((f32[128,8,128]{2,1,0:T(8,128)}), f32[128,8,128]{2,1,0:T(8,128)S(1)}, u32[]{:S(2)}, u32[]{:S(2)}) async-start(f32[128,8,128]{2,1,0:T(8,128)} %get-tuple-element.25), calls=%async_computation | async-start | bytes 1048576 | tf_op jit(solution)/shard_map/all_to_all | solution.py:537
  44.0 0.0 copy-done.8
  44.0 3.0 %collective-permute-start.5 = (bf16[272,768]{1,0:T(8,128)(2,1)S(1)}, bf16[272,768]{1,0:T(8,128)(2,1)S(1)}, u32[]{:S(2)}, u32[]{:S(2)}) collective-permute-start(bf16[272,768]{1,0:T(8,128)(2,1)S(1)} %copy-done.8), channel_id=1, source_target_pairs={{16,0},{17,1},{18,2},{19,3},{20,4},{21,5},{22,6},{23,7},{24,8},{25... | collective-permute-start | bytes 1253384 | tf_op jit(solution)/shard_map/ppermute | solution.py:498
  47.0 0.3 collective-permute-start.4
  47.3 2.3 %collective-permute-start.3 = (bf16[272,768]{1,0:T(8,128)(2,1)S(1)}, bf16[272,768]{1,0:T(8,128)(2,1)S(1)}, u32[]{:S(2)}, u32[]{:S(2)}) collective-permute-start(bf16[272,768]{1,0:T(8,128)(2,1)S(1)} %copy-done.8), channel_id=1, source_target_pairs={{8,0},{9,1},{10,2},{11,3},{12,4},{13,5},{14,6},{15,7},{16,8},{17,9... | collective-permute-start | bytes 1253384 | tf_op jit(solution)/shard_map/ppermute | solution.py:498
  49.6 0.0 collective-permute-start.2
  49.6 0.6 collective-permute-start.1
  50.2 12.2 %all-to-all-done.recv_ref = f32[128,8,128]{2,1,0:T(8,128)S(1)} async-done(((f32[128,8,128]{2,1,0:T(8,128)}), f32[128,8,128]{2,1,0:T(8,128)S(1)}, u32[]{:S(2)}, u32[]{:S(2)}) %all-to-all-start) | async-done | bytes 524320 | tf_op jit(solution)/shard_map/all_to_all | solution.py:537
  62.5 0.8 copy-done
  63.3 3.0 %place.1 = (bf16[16,768]{1,0:T(8,128)(2,1)}, s32[1,128]{1,0:T(1,128)}) custom-call(f32[128,8,128]{2,1,0:T(8,128)} %copy-done, bf16[512,768]{1,0:T(8,128)(2,1)} %cent_ref.1), custom_call_target="tpu_custom_call" | custom-call | tf_op jit(solution)/shard_map/place/pallas_call | solution.py:339
  66.3 0.0 collective-permute-done.5.refs_3_
  66.3 0.6 collective-permute-start
  66.9 4.9 %collective-permute-done.4.refs_2_ = bf16[272,768]{1,0:T(8,128)(2,1)S(1)} collective-permute-done((bf16[272,768]{1,0:T(8,128)(2,1)S(1)}, bf16[272,768]{1,0:T(8,128)(2,1)S(1)}, u32[]{:S(2)}, u32[]{:S(2)}) %collective-permute-start.4) | collective-permute-done | bytes 417824 | tf_op jit(solution)/shard_map/ppermute | solution.py:498
  71.8 0.0 collective-permute-done.3.refs_1_
  71.8 0.8 copy-done.12
  72.6 0.8 copy-done.13
  73.4 0.0 copy-done.11
  73.4 10.7 %score.2.refs_5_ = f32[8,8,512]{2,1,0:T(8,128)} custom-call(bf16[272,768]{1,0:T(8,128)(2,1)} %get-tuple-element.24.refs_0_, bf16[272,768]{1,0:T(8,128)(2,1)} %copy-done.13, bf16[272,768]{1,0:T(8,128)(2,1)} %copy-done.12, bf16[272,768]{1,0:T(8,128)(2,1)} %copy-done.11, bf16[4096,768]{1,0:T(8,128)(2,1)} %all-gather.2.cloned.1.call-done.refs_4_), custom_call_target="tpu_custom_call" | custom-call | flops 6442450944 | bytes 6291456 | tf_op jit(solution)/shard_map/score/pallas_call | solution.py:434
  84.1 0.0 collective-permute-done.2.refs_3_
  84.1 0.0 copy-start.9
  84.1 4.9 %collective-permute-done.1.refs_2_ = bf16[272,768]{1,0:T(8,128)(2,1)S(1)} collective-permute-done((bf16[272,768]{1,0:T(8,128)(2,1)}, bf16[272,768]{1,0:T(8,128)(2,1)S(1)}, u32[]{:S(2)}, u32[]{:S(2)}) %collective-permute-start.1) | collective-permute-done | bytes 417824 | tf_op jit(solution)/shard_map/ppermute | solution.py:498
  89.0 0.0 collective-permute-done.refs_1_
  89.0 0.0 copy-done.9
  89.1 0.8 copy-done.10
  89.8 11.7 %score.3 = (f32[16,512]{1,0:T(8,128)}, f32[16,512]{1,0:T(8,128)}, f32[16,512]{1,0:T(8,128)}, f32[16,512]{1,0:T(8,128)}, f32[16,512]{1,0:T(8,128)}, /*index=5*/f3...) custom-call(bf16[272,768]{1,0:T(8,128)(2,1)} %get-tuple-element.23.refs_0_, ...), custom_call_target="tpu_custom_call" | custom-call | flops 6442450944 | bytes 6291456 | tf_op jit(solution)/shard_map/score/pallas_call | solution.py:434
  101.5 0.5 collective-permute-start.6
  102.0 2.4 %collective-permute-start.7 = (f32[16,512]{1,0:T(8,128)}, f32[16,512]{1,0:T(8,128)S(1)}, u32[]{:S(2)}, u32[]{:S(2)}) collective-permute-start(f32[16,512]{1,0:T(8,128)} %get-tuple-element.31), channel_id=1, source_target_pairs={{2,0},{3,1},{4,2},{5,3},{6,4},{7,5},{0,6},{1,7},{10,8},{11,9},{12,... | collective-permute-start | bytes 98312 | tf_op jit(solution)/shard_map/ppermute | solution.py:498
  104.4 0.7 collective-permute-start.8
  105.1 1.0 collective-permute-start.9
  106.1 0.1 collective-permute-start.10
  106.1 0.0 collective-permute-done.6.refs_1_
  106.2 3.1 %collective-permute-start.11 = (f32[16,512]{1,0:T(8,128)}, f32[16,512]{1,0:T(8,128)S(1)}, u32[]{:S(2)}, u32[]{:S(2)}) collective-permute-start(f32[16,512]{1,0:T(8,128)} %get-tuple-element.35), channel_id=1, source_target_pairs={{4,0},{5,1},{6,2},{7,3},{0,4},{1,5},{2,6},{3,7},{12,8},{13,9},{14,... | collective-permute-start | bytes 98312 | tf_op jit(solution)/shard_map/ppermute | solution.py:498
  109.3 0.0 collective-permute-done.7.refs_2_
  109.3 0.5 collective-permute-start.12
  109.8 0.0 collective-permute-done.8.refs_3_
  109.8 0.0 collective-permute-done.9.refs_4_
  109.8 1.2 collective-permute-done.10.refs_5_
  111.0 0.9 collective-permute-done.11.refs_6_
  111.9 2.5 %collective-permute-done.12.refs_7_ = f32[16,512]{1,0:T(8,128)S(1)} collective-permute-done((f32[16,512]{1,0:T(8,128)}, f32[16,512]{1,0:T(8,128)S(1)}, u32[]{:S(2)}, u32[]{:S(2)}) %collective-permute-start.12) | collective-permute-done | bytes 32800 | tf_op jit(solution)/shard_map/ppermute | solution.py:498
  114.4 0.0 copy-done.1
  114.4 0.0 copy-done.3
  114.4 0.6 copy-done.7
  115.0 1.8 %finish.1 = bf16[128,512]{1,0:T(8,128)(2,1)} custom-call(bf16[512]{0:T(512)(128)(2,1)} %bias_ref.1, f32[16,512]{1,0:T(8,128)} %get-tuple-element.29.refs_0_, f32[16,512]{1,0:T(8,128)} %copy-done.1, f32[16,512]{1,0:T(8,128)} %copy-done.2, f32[16,512]{1,0:T(8,128)} %copy-done.3, f32[16,512]{1,0:T(8,128)} %copy-done.4, f32[16,512]{1,0:T(8,128)} %copy-done.5, ...), custom_call_target="tpu_custom_call" | custom-call | tf_op jit(solution)/shard_map/finish/pallas_call | solution.py:481
  (17 shorter events, 0.0 us)
Async XLA Ops:
  7.2 66.2 %all-gather.2.cloned.1.call-start = ((), (), s32[]{:S(2)}) async-start(), calls=%async_computation.1 | async-start | bytes 7077888 | tf_op jit(solution)/shard_map/all_gather | solution.py:521
  21.7 22.3 %copy-start.8 = (bf16[272,768]{1,0:T(8,128)(2,1)S(1)}, bf16[272,768]{1,0:T(8,128)(2,1)}, u32[]{:S(2)}) copy-start(bf16[272,768]{1,0:T(8,128)(2,1)} %get-tuple-element.24.refs_0_) | copy-start | bytes 1253380
  33.1 29.4 %all-to-all-start = ((f32[128,8,128]{2,1,0:T(8,128)}), f32[128,8,128]{2,1,0:T(8,128)S(1)}, u32[]{:S(2)}, u32[]{:S(2)}) async-start(f32[128,8,128]{2,1,0:T(8,128)} %get-tuple-element.25), calls=%async_computation | async-start | bytes 1048576 | tf_op jit(solution)/shard_map/all_to_all | solution.py:537
  44.0 22.3 %collective-permute-start.5 = (bf16[272,768]{1,0:T(8,128)(2,1)S(1)}, bf16[272,768]{1,0:T(8,128)(2,1)S(1)}, u32[]{:S(2)}, u32[]{:S(2)}) collective-permute-start(bf16[272,768]{1,0:T(8,128)(2,1)S(1)} %copy-done.8), channel_id=1, source_target_pairs={{16,0},{17,1},{18,2},{19,3},{20,4},{21,5},{22,6},{23,7},{24,8},{25... | collective-permute-start | bytes 1253384 | tf_op jit(solution)/shard_map/ppermute | solution.py:498
  47.0 24.8 %collective-permute-start.4 = (bf16[272,768]{1,0:T(8,128)(2,1)S(1)}, bf16[272,768]{1,0:T(8,128)(2,1)S(1)}, u32[]{:S(2)}, u32[]{:S(2)}) collective-permute-start(bf16[272,768]{1,0:T(8,128)(2,1)S(1)} %copy-done.8), channel_id=1, source_target_pairs={{24,0},{25,1},{26,2},{27,3},{28,4},{29,5},{30,6},{31,7},{0,8},{1,9... | collective-permute-start | bytes 1253384 | tf_op jit(solution)/shard_map/ppermute | solution.py:498
  47.3 24.5 %collective-permute-start.3 = (bf16[272,768]{1,0:T(8,128)(2,1)S(1)}, bf16[272,768]{1,0:T(8,128)(2,1)S(1)}, u32[]{:S(2)}, u32[]{:S(2)}) collective-permute-start(bf16[272,768]{1,0:T(8,128)(2,1)S(1)} %copy-done.8), channel_id=1, source_target_pairs={{8,0},{9,1},{10,2},{11,3},{12,4},{13,5},{14,6},{15,7},{16,8},{17,9... | collective-permute-start | bytes 1253384 | tf_op jit(solution)/shard_map/ppermute | solution.py:498
  49.6 34.5 %collective-permute-start.2 = (bf16[272,768]{1,0:T(8,128)(2,1)}, bf16[272,768]{1,0:T(8,128)(2,1)S(1)}, u32[]{:S(2)}, u32[]{:S(2)}) collective-permute-start(bf16[272,768]{1,0:T(8,128)(2,1)} %get-tuple-element.23.refs_0_), channel_id=1, source_target_pairs={{16,0},{17,1},{18,2},{19,3},{20,4},{21,5},{22,6},{23,7},{24,8},{25... | collective-permute-start | bytes 1253384 | tf_op jit(solution)/shard_map/ppermute | solution.py:498
  49.6 39.4 %collective-permute-start.1 = (bf16[272,768]{1,0:T(8,128)(2,1)}, bf16[272,768]{1,0:T(8,128)(2,1)S(1)}, u32[]{:S(2)}, u32[]{:S(2)}) collective-permute-start(bf16[272,768]{1,0:T(8,128)(2,1)} %get-tuple-element.23.refs_0_), channel_id=1, source_target_pairs={{24,0},{25,1},{26,2},{27,3},{28,4},{29,5},{30,6},{31,7},{0,8},{1,9... | collective-permute-start | bytes 1253384 | tf_op jit(solution)/shard_map/ppermute | solution.py:498
  62.5 0.8 copy-start
  66.3 7.1 %copy-start.11 = (bf16[272,768]{1,0:T(8,128)(2,1)}, bf16[272,768]{1,0:T(8,128)(2,1)S(1)}, u32[]{:S(2)}) copy-start(bf16[272,768]{1,0:T(8,128)(2,1)S(1)} %collective-permute-done.5.refs_3_) | copy-start | bytes 1253380
  66.3 22.7 %collective-permute-start = (bf16[272,768]{1,0:T(8,128)(2,1)}, bf16[272,768]{1,0:T(8,128)(2,1)}, u32[]{:S(2)}, u32[]{:S(2)}) collective-permute-start(bf16[272,768]{1,0:T(8,128)(2,1)} %get-tuple-element.23.refs_0_), channel_id=1, source_target_pairs={{8,0},{9,1},{10,2},{11,3},{12,4},{13,5},{14,6},{15,7},{16,8},{17,9... | collective-permute-start | bytes 1253384 | tf_op jit(solution)/shard_map/ppermute | solution.py:498
  71.8 0.8 copy-start.12
  72.6 0.8 copy-start.13
  84.1 4.9 %copy-start.9 = (bf16[272,768]{1,0:T(8,128)(2,1)}, bf16[272,768]{1,0:T(8,128)(2,1)S(1)}, u32[]{:S(2)}) copy-start(bf16[272,768]{1,0:T(8,128)(2,1)S(1)} %collective-permute-done.2.refs_3_) | copy-start | bytes 1253380
  89.0 0.8 copy-start.10
  101.5 4.6 %collective-permute-start.6 = (f32[16,512]{1,0:T(8,128)}, f32[16,512]{1,0:T(8,128)S(1)}, u32[]{:S(2)}, u32[]{:S(2)}) collective-permute-start(f32[16,512]{1,0:T(8,128)} %get-tuple-element.30), channel_id=1, source_target_pairs={{1,0},{0,1},{3,2},{2,3},{5,4},{4,5},{7,6},{6,7},{9,8},{8,9},{11,10... | collective-permute-start | bytes 98312 | tf_op jit(solution)/shard_map/ppermute | solution.py:498
  102.0 7.3 %collective-permute-start.7 = (f32[16,512]{1,0:T(8,128)}, f32[16,512]{1,0:T(8,128)S(1)}, u32[]{:S(2)}, u32[]{:S(2)}) collective-permute-start(f32[16,512]{1,0:T(8,128)} %get-tuple-element.31), channel_id=1, source_target_pairs={{2,0},{3,1},{4,2},{5,3},{6,4},{7,5},{0,6},{1,7},{10,8},{11,9},{12,... | collective-permute-start | bytes 98312 | tf_op jit(solution)/shard_map/ppermute | solution.py:498
  104.4 5.4 %collective-permute-start.8 = (f32[16,512]{1,0:T(8,128)}, f32[16,512]{1,0:T(8,128)S(1)}, u32[]{:S(2)}, u32[]{:S(2)}) collective-permute-start(f32[16,512]{1,0:T(8,128)} %get-tuple-element.32), channel_id=1, source_target_pairs={{3,0},{2,1},{5,2},{4,3},{7,4},{6,5},{1,6},{0,7},{11,8},{10,9},{13,... | collective-permute-start | bytes 98312 | tf_op jit(solution)/shard_map/ppermute | solution.py:498
  105.1 4.7 %collective-permute-start.9 = (f32[16,512]{1,0:T(8,128)}, f32[16,512]{1,0:T(8,128)S(1)}, u32[]{:S(2)}, u32[]{:S(2)}) collective-permute-start(f32[16,512]{1,0:T(8,128)} %get-tuple-element.33), channel_id=1, source_target_pairs={{6,0},{7,1},{0,2},{1,3},{2,4},{3,5},{4,6},{5,7},{14,8},{15,9},{8,1... | collective-permute-start | bytes 98312 | tf_op jit(solution)/shard_map/ppermute | solution.py:498
  106.1 4.9 %collective-permute-start.10 = (f32[16,512]{1,0:T(8,128)}, f32[16,512]{1,0:T(8,128)S(1)}, u32[]{:S(2)}, u32[]{:S(2)}) collective-permute-start(f32[16,512]{1,0:T(8,128)} %get-tuple-element.34), channel_id=1, source_target_pairs={{7,0},{6,1},{1,2},{0,3},{3,4},{2,5},{5,6},{4,7},{15,8},{14,9},{9,1... | collective-permute-start | bytes 98312 | tf_op jit(solution)/shard_map/ppermute | solution.py:498
  106.2 8.2 %copy-start.1 = (f32[16,512]{1,0:T(8,128)}, f32[16,512]{1,0:T(8,128)S(1)}, u32[]{:S(2)}) copy-start(f32[16,512]{1,0:T(8,128)S(1)} %collective-permute-done.6.refs_1_) | copy-start | bytes 98308
  106.2 5.7 %collective-permute-start.11 = (f32[16,512]{1,0:T(8,128)}, f32[16,512]{1,0:T(8,128)S(1)}, u32[]{:S(2)}, u32[]{:S(2)}) collective-permute-start(f32[16,512]{1,0:T(8,128)} %get-tuple-element.35), channel_id=1, source_target_pairs={{4,0},{5,1},{6,2},{7,3},{0,4},{1,5},{2,6},{3,7},{12,8},{13,9},{14,... | collective-permute-start | bytes 98312 | tf_op jit(solution)/shard_map/ppermute | solution.py:498
  109.3 5.1 %copy-start.2 = (f32[16,512]{1,0:T(8,128)}, f32[16,512]{1,0:T(8,128)S(1)}, u32[]{:S(2)}) copy-start(f32[16,512]{1,0:T(8,128)S(1)} %collective-permute-done.7.refs_2_) | copy-start | bytes 98308
  109.3 5.1 %collective-permute-start.12 = (f32[16,512]{1,0:T(8,128)}, f32[16,512]{1,0:T(8,128)S(1)}, u32[]{:S(2)}, u32[]{:S(2)}) collective-permute-start(f32[16,512]{1,0:T(8,128)} %get-tuple-element.36), channel_id=1, source_target_pairs={{5,0},{4,1},{7,2},{6,3},{1,4},{0,5},{3,6},{2,7},{13,8},{12,9},{15,... | collective-permute-start | bytes 98312 | tf_op jit(solution)/shard_map/ppermute | solution.py:498
  109.8 4.6 %copy-start.3 = (f32[16,512]{1,0:T(8,128)}, f32[16,512]{1,0:T(8,128)S(1)}, u32[]{:S(2)}) copy-start(f32[16,512]{1,0:T(8,128)S(1)} %collective-permute-done.8.refs_3_) | copy-start | bytes 98308
  109.8 4.6 %copy-start.4 = (f32[16,512]{1,0:T(8,128)}, f32[16,512]{1,0:T(8,128)S(1)}, u32[]{:S(2)}) copy-start(f32[16,512]{1,0:T(8,128)S(1)} %collective-permute-done.9.refs_4_) | copy-start | bytes 98308
  111.0 3.4 %copy-start.5 = (f32[16,512]{1,0:T(8,128)}, f32[16,512]{1,0:T(8,128)S(1)}, u32[]{:S(2)}) copy-start(f32[16,512]{1,0:T(8,128)S(1)} %collective-permute-done.10.refs_5_) | copy-start | bytes 98308
  111.9 2.5 %copy-start.6 = (f32[16,512]{1,0:T(8,128)}, f32[16,512]{1,0:T(8,128)S(1)}, u32[]{:S(2)}) copy-start(f32[16,512]{1,0:T(8,128)S(1)} %collective-permute-done.11.refs_6_) | copy-start | bytes 98308
  114.4 0.6 copy-start.7
Sparse Core Ops, SparseCore 0:
  9.7 49.8 all-gather.1

commit v4 on v3

--- a/solution.py
+++ b/solution.py
@@ -425,12 +425,13 @@
         _, x, core = here()
         for k, (dx, dc) in enumerate(PEERS):
             spot = lax.rem(x + dx, NX) * 2 + lax.rem(core + dc, 2)
-            outs[k][:part, :] = before[spot]
-            outs[k][part:, :] = res[spot]
+            outs[k][:done, :] = before[spot]
+            outs[k][done:, :] = res[spot]
 
     flops = 2 * groups * rows * width * terms * shards
     whole = jax.ShapeDtypeStruct((shards, part, terms), F32)
-    piece = jax.ShapeDtypeStruct((PARTS * part, terms), F32)
+    done = earlier.shape[1] if last else 0
+    piece = jax.ShapeDtypeStruct((done + part, terms), F32)
     return pl.pallas_call(
         kernel,
         out_shape=(piece,) * shards if last else whole,
@@ -536,15 +537,14 @@
     late = spread(payload)
     recv = lax.all_to_all(routed, ("grp", "term"), split_axis=0, concat_axis=0, tiled=True)
 
-    scored = score(early, vocab, None)
-    dense_part, slot_part = place(recv, centroids, passages)
-    scored, dense_part, slot_part = lax.optimization_barrier((scored, dense_part, slot_part))
-    sent = score(late, vocab, scored)
+    scored = score(early + late[:1], vocab, None)
+    sent = score(late[1:], vocab, scored)
     pieces = []
     for dx, dc in PEERS:
         back = sent[PEERS.index(((NX - dx) % NX, dc))]
         pieces.append(back if (dx, dc) == (0, 0) else shift(back, 0, dx, dc))
     sparse = finish(vocab_bias, pieces)
+    dense_part, slot_part = place(recv, centroids, passages)
     return (sparse, dense_part[None], slot_part[:, :CAP])
 
 

time: 124 us -> 103 us (0.83)
  waiting for transfers between devices: 27.3 us -> 3.17 us
  starting transfers between devices: 26 us -> 32.3 us
  local copies, waits for them, and re-layouts: 3.77 us -> 1.41 us
    ppermute x13, waiting for transfers between devices: 14.4 us -> 1.84 us  [shift(): return lax.ppermute(value, 'term', pairs)]
    all_to_all x1, waiting for transfers between devices: 12.2 us -> 0.01 us  [body(): lax.all_to_all(routed, ('grp', 'term'), split_axis=0, concat_axis=0, tile...]
    ppermute x13, starting transfers between devices: 15.1 us -> 21.3 us  [shift(): return lax.ppermute(value, 'term', pairs)]
    unnamed x28 -> x22, local copies, waits for them, and re-layouts: 3.77 us -> 1.41 us
  transfers between devices with their start and end apart: 15 -> 15, of which waited for: 6 -> 2; matrix products, arithmetic and copies ran while one was open for 0% -> 0% of each run, Pallas kernels for 31% -> 49%
where the time goes in v4:
time: 103 us
  Pallas kernels  51.8 us (50%)
  starting transfers between devices  32.3 us (31%)
  between operations  14.2 us (14%)
  waiting for transfers between devices  3.17 us (3%)
  local copies, waits for them, and re-layouts  1.41 us (1%)
    pallas_call x2, Pallas kernels, score(): pl.pallas_call(kernel, out_shape=(piece,) * shards if last else whole, in...  22.6 us
    ppermute x13, starting transfers between devices, shift(): return lax.ppermute(value, 'term', pairs)  21.3 us
    pallas_call x1, Pallas kernels, encode_lead(): pl.pallas_call(lead_kernel, out_shape=(jax.ShapeDtypeStruct((part + EXTRA...  13.8 us
    all_to_all x1, starting transfers between devices, body(): lax.all_to_all(routed, ('grp', 'term'), split_axis=0, concat_axis=0, tile...  10.9 us
    pallas_call x1, Pallas kernels, encode_tail(): pl.pallas_call(tail_kernel, out_shape=(jax.ShapeDtypeStruct((rows + EXTRA...  10.6 us
    pallas_call x1, Pallas kernels, place(): pl.pallas_call(functools.partial(place_kernel, passages), out_shape=(jax....  3.01 us
  transfers between devices with their start and end apart: 15, of which 2 were waited for; matrix products, arithmetic and copies ran while one was open for 0% of the time, Pallas kernels for 49%

profile of v4, /device:TPU:1, one launch (start us, length us, event | category | flops | bytes accessed | tf_op | source)
XLA Modules:
  0.0 102.8 jit_solution(576364110759139511)
XLA Ops:
  7.2 0.0 all-gather.2.cloned.1.call-start
  7.2 0.7 all-gather.2.cloned.1.call-update
  7.9 13.8 %lead.1 = (bf16[272,768]{1,0:T(8,128)(2,1)}, f32[8,768]{1,0:T(8,128)}, bf16[256,768]{1,0:T(8,128)(2,1)}) custom-call(s32[4]{0:T(128)} %lengths_ref.3, bf16[512,768]{1,0:T(8,128)(2,1)} %hidden_hbm.1, s32[4,96]{1,0:T(4,128)} %lists_ref.3, f32[768]{0:T(1024)} %gain_ref.3, bf16[768,2304]{1,0:T(8,128)(2,1)} %attn_hbm.1, bf16[768,768]{1,0:T(8,128)(2,1)} %out_hbm.1, ...), custom_call_target="tpu_custom_call" | custom-call | flops 2415919104 | bytes 4718592 | tf_op jit(solution)/shard_map/lead/pallas_call | solution.py:207
  21.7 3.6 %collective-permute-start.3 = (bf16[272,768]{1,0:T(8,128)(2,1)}, bf16[272,768]{1,0:T(8,128)(2,1)S(1)}, u32[]{:S(2)}, u32[]{:S(2)}) collective-permute-start(bf16[272,768]{1,0:T(8,128)(2,1)} %get-tuple-element.21.refs_0_), channel_id=1, source_target_pairs={{8,0},{9,1},{10,2},{11,3},{12,4},{13,5},{14,6},{15,7},{16,8},{17,9... | collective-permute-start | bytes 1253384 | tf_op jit(solution)/shard_map/ppermute | solution.py:499
  25.4 0.0 collective-permute-start.4
  25.4 1.6 %collective-permute-start.5 = (bf16[272,768]{1,0:T(8,128)(2,1)}, bf16[272,768]{1,0:T(8,128)(2,1)}, u32[]{:S(2)}, u32[]{:S(2)}) collective-permute-start(bf16[272,768]{1,0:T(8,128)(2,1)} %get-tuple-element.21.refs_0_), channel_id=1, source_target_pairs={{16,0},{17,1},{18,2},{19,3},{20,4},{21,5},{22,6},{23,7},{24,8},{25... | collective-permute-start | bytes 1253384 | tf_op jit(solution)/shard_map/ppermute | solution.py:499
  27.0 10.6 %tail.1 = (bf16[272,768]{1,0:T(8,128)(2,1)}, f32[128,8,128]{2,1,0:T(8,128)}) custom-call(s32[4]{0:T(128)} %lengths_ref.3, s32[4]{0:T(128)} %clusters_ref.1, bf16[256,768]{1,0:T(8,128)(2,1)} %get-tuple-element.18.rest_hbm, s32[4,96]{1,0:T(4,128)} %lists_ref.3, f32[768]{0:T(1024)} %gain_ref.3, f32[8,768]{1,0:T(8,128)} %get-tuple-element.19.dense_ref, ...), custom_call_target="tpu_custom_call" | custom-call | flops 1 | bytes 1 | tf_op jit(solution)/shard_map/tail/pallas_call | solution.py:277
  37.6 1.1 %collective-permute-start = (bf16[272,768]{1,0:T(8,128)(2,1)}, bf16[272,768]{1,0:T(8,128)(2,1)S(1)}, u32[]{:S(2)}, u32[]{:S(2)}) collective-permute-start(bf16[272,768]{1,0:T(8,128)(2,1)} %get-tuple-element.20.refs_4_), channel_id=1, source_target_pairs={{8,0},{9,1},{10,2},{11,3},{12,4},{13,5},{14,6},{15,7},{16,8},{17,9... | collective-permute-start | bytes 1253384 | tf_op jit(solution)/shard_map/ppermute | solution.py:499
  38.7 0.8 collective-permute-start.1
  39.4 10.9 %all-to-all-start = ((f32[128,8,128]{2,1,0:T(8,128)}), f32[128,8,128]{2,1,0:T(8,128)S(1)}, u32[]{:S(2)}, u32[]{:S(2)}) async-start(f32[128,8,128]{2,1,0:T(8,128)} %get-tuple-element.30), calls=%async_computation | async-start | bytes 1048576 | tf_op jit(solution)/shard_map/all_to_all | solution.py:538
  50.4 0.0 collective-permute-done.3.refs_1_
  50.4 0.0 copy-start.10
  50.4 3.2 %collective-permute-start.2 = (bf16[272,768]{1,0:T(8,128)(2,1)}, bf16[272,768]{1,0:T(8,128)(2,1)}, u32[]{:S(2)}, u32[]{:S(2)}) collective-permute-start(bf16[272,768]{1,0:T(8,128)(2,1)} %get-tuple-element.20.refs_4_), channel_id=1, source_target_pairs={{16,0},{17,1},{18,2},{19,3},{20,4},{21,5},{22,6},{23,7},{24,8},{25... | collective-permute-start | bytes 1253384 | tf_op jit(solution)/shard_map/ppermute | solution.py:499
  53.6 0.0 collective-permute-done.4.refs_2_
  53.6 0.0 collective-permute-done.5.refs_3_
  53.6 0.6 all-gather.2.cloned.1.call-done.refs_5_.refs_3_
  54.2 0.0 copy-done.10
  54.2 12.6 %score.2.refs_4_ = f32[8,10,512]{2,1,0:T(8,128)} custom-call(bf16[272,768]{1,0:T(8,128)(2,1)} %get-tuple-element.21.refs_0_, bf16[272,768]{1,0:T(8,128)(2,1)} %copy-done.10, bf16[272,768]{1,0:T(8,128)(2,1)} %collective-permute-done.4.refs_2_, bf16[272,768]{1,0:T(8,128)(2,1)} %collective-permute-done.5.refs_3_, bf16[272,768]{1,0:T(8,128)(2,1)} %get-tuple-element.20.refs_4_, ...), custom_call_target="tpu_custom_call" | custom-call | flops 8053063680 | bytes 6291456 | tf_op jit(solution)/shard_map/score/pallas_call | solution.py:435
  66.8 0.0 collective-permute-done.refs_0_
  66.8 0.0 copy-start.8
  66.8 0.0 collective-permute-done.1.refs_1_
  66.9 1.8 %collective-permute-done.2.refs_2_ = bf16[272,768]{1,0:T(8,128)(2,1)} collective-permute-done((bf16[272,768]{1,0:T(8,128)(2,1)}, bf16[272,768]{1,0:T(8,128)(2,1)}, u32[]{:S(2)}, u32[]{:S(2)}) %collective-permute-start.2) | collective-permute-done | bytes 417824 | tf_op jit(solution)/shard_map/ppermute | solution.py:499
  68.7 0.0 copy-done.8
  68.7 10.0 %score.3 = (f32[16,512]{1,0:T(8,128)}, f32[16,512]{1,0:T(8,128)}, f32[16,512]{1,0:T(8,128)}, f32[16,512]{1,0:T(8,128)}, f32[16,512]{1,0:T(8,128)}, /*index=5*/f3...) custom-call(bf16[272,768]{1,0:T(8,128)(2,1)} %copy-done.8, bf16[272,768]{1,0:T(8,128)(2,1)} %copy-done.9, ...), custom_call_target="tpu_custom_call" | custom-call | flops 4831838208 | bytes 6291456 | tf_op jit(solution)/shard_map/score/pallas_call | solution.py:435
  78.7 4.2 %collective-permute-start.10 = (f32[16,512]{1,0:T(8,128)}, f32[16,512]{1,0:T(8,128)S(1)}, u32[]{:S(2)}, u32[]{:S(2)}) collective-permute-start(f32[16,512]{1,0:T(8,128)} %get-tuple-element.27), channel_id=1, source_target_pairs={{7,0},{6,1},{1,2},{0,3},{3,4},{2,5},{5,6},{4,7},{15,8},{14,9},{9,1... | collective-permute-start | bytes 98312 | tf_op jit(solution)/shard_map/ppermute | solution.py:499
  82.9 2.4 %collective-permute-start.11 = (f32[16,512]{1,0:T(8,128)}, f32[16,512]{1,0:T(8,128)S(1)}, u32[]{:S(2)}, u32[]{:S(2)}) collective-permute-start(f32[16,512]{1,0:T(8,128)} %get-tuple-element.28), channel_id=1, source_target_pairs={{4,0},{5,1},{6,2},{7,3},{0,4},{1,5},{2,6},{3,7},{12,8},{13,9},{14,... | collective-permute-start | bytes 98312 | tf_op jit(solution)/shard_map/ppermute | solution.py:499
  85.4 0.0 collective-permute-start.12
  85.4 0.9 collective-permute-start.6
  86.3 1.5 %collective-permute-start.7 = (f32[16,512]{1,0:T(8,128)}, f32[16,512]{1,0:T(8,128)S(1)}, u32[]{:S(2)}, u32[]{:S(2)}) collective-permute-start(f32[16,512]{1,0:T(8,128)} %get-tuple-element.24), channel_id=1, source_target_pairs={{2,0},{3,1},{4,2},{5,3},{6,4},{7,5},{0,6},{1,7},{10,8},{11,9},{12,... | collective-permute-start | bytes 98312 | tf_op jit(solution)/shard_map/ppermute | solution.py:499
  87.7 0.0 collective-permute-done.10.refs_5_
  87.8 1.4 %collective-permute-start.8 = (f32[16,512]{1,0:T(8,128)}, f32[16,512]{1,0:T(8,128)S(1)}, u32[]{:S(2)}, u32[]{:S(2)}) collective-permute-start(f32[16,512]{1,0:T(8,128)} %get-tuple-element.25), channel_id=1, source_target_pairs={{3,0},{2,1},{5,2},{4,3},{7,4},{6,5},{1,6},{0,7},{11,8},{10,9},{13,... | collective-permute-start | bytes 98312 | tf_op jit(solution)/shard_map/ppermute | solution.py:499
  89.2 0.0 collective-permute-done.11.refs_6_
  89.2 0.5 collective-permute-start.9
  89.7 0.0 all-to-all-done.recv_ref
  89.7 0.8 copy-done
  90.5 3.0 %place.1 = (bf16[16,768]{1,0:T(8,128)(2,1)}, s32[1,128]{1,0:T(1,128)}) custom-call(f32[128,8,128]{2,1,0:T(8,128)} %copy-done, bf16[512,768]{1,0:T(8,128)(2,1)} %cent_ref.1), custom_call_target="tpu_custom_call" | custom-call | tf_op jit(solution)/shard_map/place/pallas_call | solution.py:339
  93.5 0.0 collective-permute-done.12.refs_7_
  93.5 0.0 collective-permute-done.6.refs_1_
  93.5 0.0 collective-permute-done.7.refs_2_
  93.5 0.0 copy-start.5
  93.6 0.0 collective-permute-done.8.refs_3_
  93.6 0.0 collective-permute-done.9.refs_4_
  93.6 0.5 copy-done.3
  94.1 0.0 copy-done.4
  94.1 0.0 copy-done.5
  94.2 0.0 copy-done.6
  94.2 0.0 copy-done.7
  94.2 1.8 %finish.1 = bf16[128,512]{1,0:T(8,128)(2,1)} custom-call(bf16[512]{0:T(512)(128)(2,1)} %bias_ref.1, f32[16,512]{1,0:T(8,128)} %get-tuple-element.22.refs_0_, f32[16,512]{1,0:T(8,128)} %copy-done.4, f32[16,512]{1,0:T(8,128)} %copy-done.5, f32[16,512]{1,0:T(8,128)} %copy-done.6, f32[16,512]{1,0:T(8,128)} %copy-done.7, f32[16,512]{1,0:T(8,128)} %copy-done.1, ...), custom_call_target="tpu_custom_call" | custom-call | tf_op jit(solution)/shard_map/finish/pallas_call | solution.py:482
  (11 shorter events, 0.0 us)
Async XLA Ops:
  7.2 47.1 %all-gather.2.cloned.1.call-start = ((), (), s32[]{:S(2)}) async-start(), calls=%async_computation.1 | async-start | bytes 7077888 | tf_op jit(solution)/shard_map/all_gather | solution.py:522
  21.7 28.6 %collective-permute-start.3 = (bf16[272,768]{1,0:T(8,128)(2,1)}, bf16[272,768]{1,0:T(8,128)(2,1)S(1)}, u32[]{:S(2)}, u32[]{:S(2)}) collective-permute-start(bf16[272,768]{1,0:T(8,128)(2,1)} %get-tuple-element.21.refs_0_), channel_id=1, source_target_pairs={{8,0},{9,1},{10,2},{11,3},{12,4},{13,5},{14,6},{15,7},{16,8},{17,9... | collective-permute-start | bytes 1253384 | tf_op jit(solution)/shard_map/ppermute | solution.py:499
  25.4 28.2 %collective-permute-start.4 = (bf16[272,768]{1,0:T(8,128)(2,1)}, bf16[272,768]{1,0:T(8,128)(2,1)}, u32[]{:S(2)}, u32[]{:S(2)}) collective-permute-start(bf16[272,768]{1,0:T(8,128)(2,1)} %get-tuple-element.21.refs_0_), channel_id=1, source_target_pairs={{24,0},{25,1},{26,2},{27,3},{28,4},{29,5},{30,6},{31,7},{0,8},{1,9... | collective-permute-start | bytes 1253384 | tf_op jit(solution)/shard_map/ppermute | solution.py:499
  25.4 28.2 %collective-permute-start.5 = (bf16[272,768]{1,0:T(8,128)(2,1)}, bf16[272,768]{1,0:T(8,128)(2,1)}, u32[]{:S(2)}, u32[]{:S(2)}) collective-permute-start(bf16[272,768]{1,0:T(8,128)(2,1)} %get-tuple-element.21.refs_0_), channel_id=1, source_target_pairs={{16,0},{17,1},{18,2},{19,3},{20,4},{21,5},{22,6},{23,7},{24,8},{25... | collective-permute-start | bytes 1253384 | tf_op jit(solution)/shard_map/ppermute | solution.py:499
  37.6 29.2 %collective-permute-start = (bf16[272,768]{1,0:T(8,128)(2,1)}, bf16[272,768]{1,0:T(8,128)(2,1)S(1)}, u32[]{:S(2)}, u32[]{:S(2)}) collective-permute-start(bf16[272,768]{1,0:T(8,128)(2,1)} %get-tuple-element.20.refs_4_), channel_id=1, source_target_pairs={{8,0},{9,1},{10,2},{11,3},{12,4},{13,5},{14,6},{15,7},{16,8},{17,9... | collective-permute-start | bytes 1253384 | tf_op jit(solution)/shard_map/ppermute | solution.py:499
  38.7 28.2 %collective-permute-start.1 = (bf16[272,768]{1,0:T(8,128)(2,1)}, bf16[272,768]{1,0:T(8,128)(2,1)S(1)}, u32[]{:S(2)}, u32[]{:S(2)}) collective-permute-start(bf16[272,768]{1,0:T(8,128)(2,1)} %get-tuple-element.20.refs_4_), channel_id=1, source_target_pairs={{24,0},{25,1},{26,2},{27,3},{28,4},{29,5},{30,6},{31,7},{0,8},{1,9... | collective-permute-start | bytes 1253384 | tf_op jit(solution)/shard_map/ppermute | solution.py:499
  39.4 50.2 %all-to-all-start = ((f32[128,8,128]{2,1,0:T(8,128)}), f32[128,8,128]{2,1,0:T(8,128)S(1)}, u32[]{:S(2)}, u32[]{:S(2)}) async-start(f32[128,8,128]{2,1,0:T(8,128)} %get-tuple-element.30), calls=%async_computation | async-start | bytes 1048576 | tf_op jit(solution)/shard_map/all_to_all | solution.py:538
  50.4 3.9 %copy-start.10 = (bf16[272,768]{1,0:T(8,128)(2,1)}, bf16[272,768]{1,0:T(8,128)(2,1)S(1)}, u32[]{:S(2)}) copy-start(bf16[272,768]{1,0:T(8,128)(2,1)S(1)} %collective-permute-done.3.refs_1_) | copy-start | bytes 1253380
  50.4 18.3 %collective-permute-start.2 = (bf16[272,768]{1,0:T(8,128)(2,1)}, bf16[272,768]{1,0:T(8,128)(2,1)}, u32[]{:S(2)}, u32[]{:S(2)}) collective-permute-start(bf16[272,768]{1,0:T(8,128)(2,1)} %get-tuple-element.20.refs_4_), channel_id=1, source_target_pairs={{16,0},{17,1},{18,2},{19,3},{20,4},{21,5},{22,6},{23,7},{24,8},{25... | collective-permute-start | bytes 1253384 | tf_op jit(solution)/shard_map/ppermute | solution.py:499
  66.8 1.8 %copy-start.8 = (bf16[272,768]{1,0:T(8,128)(2,1)}, bf16[272,768]{1,0:T(8,128)(2,1)S(1)}, u32[]{:S(2)}) copy-start(bf16[272,768]{1,0:T(8,128)(2,1)S(1)} %collective-permute-done.refs_0_) | copy-start | bytes 1253380
  66.9 1.8 %copy-start.9 = (bf16[272,768]{1,0:T(8,128)(2,1)}, bf16[272,768]{1,0:T(8,128)(2,1)S(1)}, u32[]{:S(2)}) copy-start(bf16[272,768]{1,0:T(8,128)(2,1)S(1)} %collective-permute-done.1.refs_1_) | copy-start | bytes 1253380
  78.7 9.1 %collective-permute-start.10 = (f32[16,512]{1,0:T(8,128)}, f32[16,512]{1,0:T(8,128)S(1)}, u32[]{:S(2)}, u32[]{:S(2)}) collective-permute-start(f32[16,512]{1,0:T(8,128)} %get-tuple-element.27), channel_id=1, source_target_pairs={{7,0},{6,1},{1,2},{0,3},{3,4},{2,5},{5,6},{4,7},{15,8},{14,9},{9,1... | collective-permute-start | bytes 98312 | tf_op jit(solution)/shard_map/ppermute | solution.py:499
  82.9 6.3 %collective-permute-start.11 = (f32[16,512]{1,0:T(8,128)}, f32[16,512]{1,0:T(8,128)S(1)}, u32[]{:S(2)}, u32[]{:S(2)}) collective-permute-start(f32[16,512]{1,0:T(8,128)} %get-tuple-element.28), channel_id=1, source_target_pairs={{4,0},{5,1},{6,2},{7,3},{0,4},{1,5},{2,6},{3,7},{12,8},{13,9},{14,... | collective-permute-start | bytes 98312 | tf_op jit(solution)/shard_map/ppermute | solution.py:499
  85.4 8.1 %collective-permute-start.12 = (f32[16,512]{1,0:T(8,128)}, f32[16,512]{1,0:T(8,128)S(1)}, u32[]{:S(2)}, u32[]{:S(2)}) collective-permute-start(f32[16,512]{1,0:T(8,128)} %get-tuple-element.29), channel_id=1, source_target_pairs={{5,0},{4,1},{7,2},{6,3},{1,4},{0,5},{3,6},{2,7},{13,8},{12,9},{15,... | collective-permute-start | bytes 98312 | tf_op jit(solution)/shard_map/ppermute | solution.py:499
  85.4 8.1 %collective-permute-start.6 = (f32[16,512]{1,0:T(8,128)}, f32[16,512]{1,0:T(8,128)S(1)}, u32[]{:S(2)}, u32[]{:S(2)}) collective-permute-start(f32[16,512]{1,0:T(8,128)} %get-tuple-element.23), channel_id=1, source_target_pairs={{1,0},{0,1},{3,2},{2,3},{5,4},{4,5},{7,6},{6,7},{9,8},{8,9},{11,10... | collective-permute-start | bytes 98312 | tf_op jit(solution)/shard_map/ppermute | solution.py:499
  86.3 7.2 %collective-permute-start.7 = (f32[16,512]{1,0:T(8,128)}, f32[16,512]{1,0:T(8,128)S(1)}, u32[]{:S(2)}, u32[]{:S(2)}) collective-permute-start(f32[16,512]{1,0:T(8,128)} %get-tuple-element.24), channel_id=1, source_target_pairs={{2,0},{3,1},{4,2},{5,3},{6,4},{7,5},{0,6},{1,7},{10,8},{11,9},{12,... | collective-permute-start | bytes 98312 | tf_op jit(solution)/shard_map/ppermute | solution.py:499
  87.8 5.8 %copy-start.1 = (f32[16,512]{1,0:T(8,128)}, f32[16,512]{1,0:T(8,128)S(1)}, u32[]{:S(2)}) copy-start(f32[16,512]{1,0:T(8,128)S(1)} %collective-permute-done.10.refs_5_) | copy-start | bytes 98308
  87.8 5.8 %collective-permute-start.8 = (f32[16,512]{1,0:T(8,128)}, f32[16,512]{1,0:T(8,128)S(1)}, u32[]{:S(2)}, u32[]{:S(2)}) collective-permute-start(f32[16,512]{1,0:T(8,128)} %get-tuple-element.25), channel_id=1, source_target_pairs={{3,0},{2,1},{5,2},{4,3},{7,4},{6,5},{1,6},{0,7},{11,8},{10,9},{13,... | collective-permute-start | bytes 98312 | tf_op jit(solution)/shard_map/ppermute | solution.py:499
  89.2 4.4 %copy-start.2 = (f32[16,512]{1,0:T(8,128)}, f32[16,512]{1,0:T(8,128)S(1)}, u32[]{:S(2)}) copy-start(f32[16,512]{1,0:T(8,128)S(1)} %collective-permute-done.11.refs_6_) | copy-start | bytes 98308
  89.2 4.4 %collective-permute-start.9 = (f32[16,512]{1,0:T(8,128)}, f32[16,512]{1,0:T(8,128)S(1)}, u32[]{:S(2)}, u32[]{:S(2)}) collective-permute-start(f32[16,512]{1,0:T(8,128)} %get-tuple-element.26), channel_id=1, source_target_pairs={{6,0},{7,1},{0,2},{1,3},{2,4},{3,5},{4,6},{5,7},{14,8},{15,9},{8,1... | collective-permute-start | bytes 98312 | tf_op jit(solution)/shard_map/ppermute | solution.py:499
  89.7 0.8 copy-start
  93.5 0.6 copy-start.3
  93.5 0.6 copy-start.4
  93.5 0.6 copy-start.5
  93.6 0.6 copy-start.6
  93.6 0.6 copy-start.7
Sparse Core Ops, SparseCore 0:
  9.7 44.4 all-gather.1

commit v5 on v4

--- a/solution.py
+++ b/solution.py
@@ -22,6 +22,7 @@
 GROUP = 4
 PARTS = 2
 OFFSETS = (0, 1, 3, 2)
+ORDER_Y = (0, 2, 1, 3)
 PEERS = tuple((dx, dc) for dx in OFFSETS for dc in (0, 1))
 FILL = -1e30
 F32 = jnp.float32
@@ -461,7 +462,7 @@
     few = share // NY
     for k in range(0, len(PEERS), 2):
         dx = PEERS[k][0]
-        for g, dy in enumerate(OFFSETS):
+        for g, dy in enumerate(ORDER_Y):
             same, other = (
                 [pieces[k + c][h * share + g * few : h * share + (g + 1) * few, :] for h in range(PARTS)]
                 for c in range(2)
@@ -523,7 +524,7 @@
         vocab_weight, "term", axis=0, tiled=True, axis_index_groups=rows_of_chips
     )
     def spread(payload):
-        return [payload] + [shift(payload, d, 0, 0) for d in OFFSETS[1:]]
+        return [payload] + [shift(payload, d, 0, 0) for d in ORDER_Y[1:]]
 
     payload, dense, rest = encode_lead(
         hidden_states, lengths, block_list, head_gain,

time: 103 us -> 101 us (0.981)
  starting transfers between devices: 32.3 us -> 29.2 us
    ppermute x13, starting transfers between devices: 21.3 us -> 18.3 us  [shift(): return lax.ppermute(value, 'term', pairs)]
  transfers between devices with their start and end apart: 15 -> 15, of which waited for: 2 -> 2; matrix products, arithmetic and copies ran while one was open for 0% -> 0% of each run, Pallas kernels for 49% -> 50%
where the time goes in v5:
time: 101 us
  Pallas kernels  51.8 us (51%)
  starting transfers between devices  29.2 us (29%)
  between operations  14.2 us (14%)
  waiting for transfers between devices  4.18 us (4%)
  local copies, waits for them, and re-layouts  1.41 us (1%)
    pallas_call x2, Pallas kernels, score(): pl.pallas_call(kernel, out_shape=(piece,) * shards if last else whole, in...  22.6 us
    ppermute x13, starting transfers between devices, shift(): return lax.ppermute(value, 'term', pairs)  18.3 us
    pallas_call x1, Pallas kernels, encode_lead(): pl.pallas_call(lead_kernel, out_shape=(jax.ShapeDtypeStruct((part + EXTRA...  13.8 us
    all_to_all x1, starting transfers between devices, body(): lax.all_to_all(routed, ('grp', 'term'), split_axis=0, concat_axis=0, tile...  10.8 us
    pallas_call x1, Pallas kernels, encode_tail(): pl.pallas_call(tail_kernel, out_shape=(jax.ShapeDtypeStruct((rows + EXTRA...  10.6 us
    pallas_call x1, Pallas kernels, place(): pl.pallas_call(functools.partial(place_kernel, passages), out_shape=(jax....  3.01 us
    ppermute x13, waiting for transfers between devices, shift(): return lax.ppermute(value, 'term', pairs)  2.28 us
  transfers between devices with their start and end apart: 15, of which 2 were waited for; matrix products, arithmetic and copies ran while one was open for 0% of the time, Pallas kernels for 50%

profile of v5, /device:TPU:1, one launch (start us, length us, event | category | flops | bytes accessed | tf_op | source)
XLA Modules:
  0.0 100.7 jit_solution(17967652509677637361)
XLA Ops:
  7.2 0.0 all-gather.2.cloned.1.call-start
  7.2 0.7 all-gather.2.cloned.1.call-update
  7.9 13.8 %lead.1 = (bf16[272,768]{1,0:T(8,128)(2,1)}, f32[8,768]{1,0:T(8,128)}, bf16[256,768]{1,0:T(8,128)(2,1)}) custom-call(s32[4]{0:T(128)} %lengths_ref.3, bf16[512,768]{1,0:T(8,128)(2,1)} %hidden_hbm.1, s32[4,96]{1,0:T(4,128)} %lists_ref.3, f32[768]{0:T(1024)} %gain_ref.3, bf16[768,2304]{1,0:T(8,128)(2,1)} %attn_hbm.1, bf16[768,768]{1,0:T(8,128)(2,1)} %out_hbm.1, ...), custom_call_target="tpu_custom_call" | custom-call | flops 2415919104 | bytes 4718592 | tf_op jit(solution)/shard_map/lead/pallas_call | solution.py:208
  21.7 3.8 %collective-permute-start.3 = (bf16[272,768]{1,0:T(8,128)(2,1)}, bf16[272,768]{1,0:T(8,128)(2,1)S(1)}, u32[]{:S(2)}, u32[]{:S(2)}) collective-permute-start(bf16[272,768]{1,0:T(8,128)(2,1)} %get-tuple-element.21.refs_0_), channel_id=1, source_target_pairs={{16,0},{17,1},{18,2},{19,3},{20,4},{21,5},{22,6},{23,7},{24,8},{25... | collective-permute-start | bytes 1253384 | tf_op jit(solution)/shard_map/ppermute | solution.py:500
  25.5 0.8 collective-permute-start.4
  26.3 0.7 collective-permute-start.5
  27.0 10.6 %tail.1 = (bf16[272,768]{1,0:T(8,128)(2,1)}, f32[128,8,128]{2,1,0:T(8,128)}) custom-call(s32[4]{0:T(128)} %lengths_ref.3, s32[4]{0:T(128)} %clusters_ref.1, bf16[256,768]{1,0:T(8,128)(2,1)} %get-tuple-element.18.rest_hbm, s32[4,96]{1,0:T(4,128)} %lists_ref.3, f32[768]{0:T(1024)} %gain_ref.3, f32[8,768]{1,0:T(8,128)} %get-tuple-element.19.dense_ref, ...), custom_call_target="tpu_custom_call" | custom-call | flops 1 | bytes 1 | tf_op jit(solution)/shard_map/tail/pallas_call | solution.py:278
  37.6 0.7 collective-permute-start
  38.3 2.2 %collective-permute-start.1 = (bf16[272,768]{1,0:T(8,128)(2,1)}, bf16[272,768]{1,0:T(8,128)(2,1)S(1)}, u32[]{:S(2)}, u32[]{:S(2)}) collective-permute-start(bf16[272,768]{1,0:T(8,128)(2,1)} %get-tuple-element.20.refs_4_), channel_id=1, source_target_pairs={{8,0},{9,1},{10,2},{11,3},{12,4},{13,5},{14,6},{15,7},{16,8},{17,9... | collective-permute-start | bytes 1253384 | tf_op jit(solution)/shard_map/ppermute | solution.py:500
  40.5 10.8 %all-to-all-start = ((f32[128,8,128]{2,1,0:T(8,128)}), f32[128,8,128]{2,1,0:T(8,128)S(1)}, u32[]{:S(2)}, u32[]{:S(2)}) async-start(f32[128,8,128]{2,1,0:T(8,128)} %get-tuple-element.30), calls=%async_computation | async-start | bytes 1048576 | tf_op jit(solution)/shard_map/all_to_all | solution.py:539
  51.3 0.0 collective-permute-done.3.refs_1_
  51.3 0.0 copy-start.10
  51.3 1.7 %collective-permute-start.2 = (bf16[272,768]{1,0:T(8,128)(2,1)}, bf16[272,768]{1,0:T(8,128)(2,1)}, u32[]{:S(2)}, u32[]{:S(2)}) collective-permute-start(bf16[272,768]{1,0:T(8,128)(2,1)} %get-tuple-element.20.refs_4_), channel_id=1, source_target_pairs={{24,0},{25,1},{26,2},{27,3},{28,4},{29,5},{30,6},{31,7},{0,8},{1,9... | collective-permute-start | bytes 1253384 | tf_op jit(solution)/shard_map/ppermute | solution.py:500
  53.0 0.0 collective-permute-done.4.refs_2_
  53.0 0.0 collective-permute-done.5.refs_3_
  53.0 1.2 %all-gather.2.cloned.1.call-done.refs_5_.refs_3_ = bf16[4096,768]{1,0:T(8,128)(2,1)} async-done(((bf16[512,768]{1,0:T(8,128)(2,1)}), bf16[4096,768]{1,0:T(8,128)(2,1)}) %all-gather.2.cloned.1.call-update) | async-done | bytes 6291472 | tf_op jit(solution)/shard_map/all_gather | solution.py:523
  54.2 0.0 copy-done.10
  54.2 12.6 %score.2.refs_4_ = f32[8,10,512]{2,1,0:T(8,128)} custom-call(bf16[272,768]{1,0:T(8,128)(2,1)} %get-tuple-element.21.refs_0_, bf16[272,768]{1,0:T(8,128)(2,1)} %copy-done.10, bf16[272,768]{1,0:T(8,128)(2,1)} %collective-permute-done.4.refs_2_, bf16[272,768]{1,0:T(8,128)(2,1)} %collective-permute-done.5.refs_3_, bf16[272,768]{1,0:T(8,128)(2,1)} %get-tuple-element.20.refs_4_, ...), custom_call_target="tpu_custom_call" | custom-call | flops 8053063680 | bytes 6291456 | tf_op jit(solution)/shard_map/score/pallas_call | solution.py:436
  66.8 0.0 collective-permute-done.refs_0_
  66.8 0.0 copy-start.8
  66.8 0.0 collective-permute-done.1.refs_1_
  66.9 0.0 copy-start.9
  66.9 2.2 %collective-permute-done.2.refs_2_ = bf16[272,768]{1,0:T(8,128)(2,1)} collective-permute-done((bf16[272,768]{1,0:T(8,128)(2,1)}, bf16[272,768]{1,0:T(8,128)(2,1)}, u32[]{:S(2)}, u32[]{:S(2)}) %collective-permute-start.2) | collective-permute-done | bytes 417824 | tf_op jit(solution)/shard_map/ppermute | solution.py:500
  69.1 10.0 %score.3 = (f32[16,512]{1,0:T(8,128)}, f32[16,512]{1,0:T(8,128)}, f32[16,512]{1,0:T(8,128)}, f32[16,512]{1,0:T(8,128)}, f32[16,512]{1,0:T(8,128)}, /*index=5*/f3...) custom-call(bf16[272,768]{1,0:T(8,128)(2,1)} %copy-done.8, bf16[272,768]{1,0:T(8,128)(2,1)} %copy-done.9, ...), custom_call_target="tpu_custom_call" | custom-call | flops 4831838208 | bytes 6291456 | tf_op jit(solution)/shard_map/score/pallas_call | solution.py:436
  79.1 1.8 %collective-permute-start.10 = (f32[16,512]{1,0:T(8,128)}, f32[16,512]{1,0:T(8,128)S(1)}, u32[]{:S(2)}, u32[]{:S(2)}) collective-permute-start(f32[16,512]{1,0:T(8,128)} %get-tuple-element.27), channel_id=1, source_target_pairs={{7,0},{6,1},{1,2},{0,3},{3,4},{2,5},{5,6},{4,7},{15,8},{14,9},{9,1... | collective-permute-start | bytes 98312 | tf_op jit(solution)/shard_map/ppermute | solution.py:500
  81.0 2.3 %collective-permute-start.11 = (f32[16,512]{1,0:T(8,128)}, f32[16,512]{1,0:T(8,128)S(1)}, u32[]{:S(2)}, u32[]{:S(2)}) collective-permute-start(f32[16,512]{1,0:T(8,128)} %get-tuple-element.28), channel_id=1, source_target_pairs={{4,0},{5,1},{6,2},{7,3},{0,4},{1,5},{2,6},{3,7},{12,8},{13,9},{14,... | collective-permute-start | bytes 98312 | tf_op jit(solution)/shard_map/ppermute | solution.py:500
  83.3 0.7 collective-permute-start.12
  84.0 0.3 collective-permute-start.6
  84.3 1.6 %collective-permute-start.7 = (f32[16,512]{1,0:T(8,128)}, f32[16,512]{1,0:T(8,128)S(1)}, u32[]{:S(2)}, u32[]{:S(2)}) collective-permute-start(f32[16,512]{1,0:T(8,128)} %get-tuple-element.24), channel_id=1, source_target_pairs={{2,0},{3,1},{4,2},{5,3},{6,4},{7,5},{0,6},{1,7},{10,8},{11,9},{12,... | collective-permute-start | bytes 98312 | tf_op jit(solution)/shard_map/ppermute | solution.py:500
  86.0 0.0 collective-permute-done.10.refs_5_
  86.0 1.3 %collective-permute-start.8 = (f32[16,512]{1,0:T(8,128)}, f32[16,512]{1,0:T(8,128)S(1)}, u32[]{:S(2)}, u32[]{:S(2)}) collective-permute-start(f32[16,512]{1,0:T(8,128)} %get-tuple-element.25), channel_id=1, source_target_pairs={{3,0},{2,1},{5,2},{4,3},{7,4},{6,5},{1,6},{0,7},{11,8},{10,9},{13,... | collective-permute-start | bytes 98312 | tf_op jit(solution)/shard_map/ppermute | solution.py:500
  87.3 0.0 collective-permute-done.11.refs_6_
  87.3 0.3 collective-permute-start.9
  87.6 0.0 all-to-all-done.recv_ref
  87.6 0.8 copy-done
  88.4 3.0 %place.1 = (bf16[16,768]{1,0:T(8,128)(2,1)}, s32[1,128]{1,0:T(1,128)}) custom-call(f32[128,8,128]{2,1,0:T(8,128)} %copy-done, bf16[512,768]{1,0:T(8,128)(2,1)} %cent_ref.1), custom_call_target="tpu_custom_call" | custom-call | tf_op jit(solution)/shard_map/place/pallas_call | solution.py:340
  91.4 0.0 collective-permute-done.12.refs_7_
  91.5 0.0 collective-permute-done.6.refs_1_
  91.5 0.0 copy-start.4
  91.5 0.0 collective-permute-done.7.refs_2_
  91.5 0.0 collective-permute-done.8.refs_3_
  91.5 0.0 collective-permute-done.9.refs_4_
  91.5 0.5 copy-done.3
  92.1 0.0 copy-done.4
  92.1 0.0 copy-done.5
  92.1 0.0 copy-done.6
  92.1 0.0 copy-done.7
  92.1 1.8 %finish.1 = bf16[128,512]{1,0:T(8,128)(2,1)} custom-call(bf16[512]{0:T(512)(128)(2,1)} %bias_ref.1, f32[16,512]{1,0:T(8,128)} %get-tuple-element.22.refs_0_, f32[16,512]{1,0:T(8,128)} %copy-done.4, f32[16,512]{1,0:T(8,128)} %copy-done.5, f32[16,512]{1,0:T(8,128)} %copy-done.6, f32[16,512]{1,0:T(8,128)} %copy-done.7, f32[16,512]{1,0:T(8,128)} %copy-done.1, ...), custom_call_target="tpu_custom_call" | custom-call | tf_op jit(solution)/shard_map/finish/pallas_call | solution.py:483
  (11 shorter events, 0.0 us)
Async XLA Ops:
  7.2 47.1 %all-gather.2.cloned.1.call-start = ((), (), s32[]{:S(2)}) async-start(), calls=%async_computation.1 | async-start | bytes 7077888 | tf_op jit(solution)/shard_map/all_gather | solution.py:523
  21.7 29.6 %collective-permute-start.3 = (bf16[272,768]{1,0:T(8,128)(2,1)}, bf16[272,768]{1,0:T(8,128)(2,1)S(1)}, u32[]{:S(2)}, u32[]{:S(2)}) collective-permute-start(bf16[272,768]{1,0:T(8,128)(2,1)} %get-tuple-element.21.refs_0_), channel_id=1, source_target_pairs={{16,0},{17,1},{18,2},{19,3},{20,4},{21,5},{22,6},{23,7},{24,8},{25... | collective-permute-start | bytes 1253384 | tf_op jit(solution)/shard_map/ppermute | solution.py:500
  25.5 27.5 %collective-permute-start.4 = (bf16[272,768]{1,0:T(8,128)(2,1)}, bf16[272,768]{1,0:T(8,128)(2,1)}, u32[]{:S(2)}, u32[]{:S(2)}) collective-permute-start(bf16[272,768]{1,0:T(8,128)(2,1)} %get-tuple-element.21.refs_0_), channel_id=1, source_target_pairs={{8,0},{9,1},{10,2},{11,3},{12,4},{13,5},{14,6},{15,7},{16,8},{17,9... | collective-permute-start | bytes 1253384 | tf_op jit(solution)/shard_map/ppermute | solution.py:500
  26.3 26.7 %collective-permute-start.5 = (bf16[272,768]{1,0:T(8,128)(2,1)}, bf16[272,768]{1,0:T(8,128)(2,1)}, u32[]{:S(2)}, u32[]{:S(2)}) collective-permute-start(bf16[272,768]{1,0:T(8,128)(2,1)} %get-tuple-element.21.refs_0_), channel_id=1, source_target_pairs={{24,0},{25,1},{26,2},{27,3},{28,4},{29,5},{30,6},{31,7},{0,8},{1,9... | collective-permute-start | bytes 1253384 | tf_op jit(solution)/shard_map/ppermute | solution.py:500
  37.6 29.2 %collective-permute-start = (bf16[272,768]{1,0:T(8,128)(2,1)}, bf16[272,768]{1,0:T(8,128)(2,1)S(1)}, u32[]{:S(2)}, u32[]{:S(2)}) collective-permute-start(bf16[272,768]{1,0:T(8,128)(2,1)} %get-tuple-element.20.refs_4_), channel_id=1, source_target_pairs={{16,0},{17,1},{18,2},{19,3},{20,4},{21,5},{22,6},{23,7},{24,8},{25... | collective-permute-start | bytes 1253384 | tf_op jit(solution)/shard_map/ppermute | solution.py:500
  38.3 28.6 %collective-permute-start.1 = (bf16[272,768]{1,0:T(8,128)(2,1)}, bf16[272,768]{1,0:T(8,128)(2,1)S(1)}, u32[]{:S(2)}, u32[]{:S(2)}) collective-permute-start(bf16[272,768]{1,0:T(8,128)(2,1)} %get-tuple-element.20.refs_4_), channel_id=1, source_target_pairs={{8,0},{9,1},{10,2},{11,3},{12,4},{13,5},{14,6},{15,7},{16,8},{17,9... | collective-permute-start | bytes 1253384 | tf_op jit(solution)/shard_map/ppermute | solution.py:500
  40.5 47.1 %all-to-all-start = ((f32[128,8,128]{2,1,0:T(8,128)}), f32[128,8,128]{2,1,0:T(8,128)S(1)}, u32[]{:S(2)}, u32[]{:S(2)}) async-start(f32[128,8,128]{2,1,0:T(8,128)} %get-tuple-element.30), calls=%async_computation | async-start | bytes 1048576 | tf_op jit(solution)/shard_map/all_to_all | solution.py:539
  51.3 2.9 %copy-start.10 = (bf16[272,768]{1,0:T(8,128)(2,1)}, bf16[272,768]{1,0:T(8,128)(2,1)S(1)}, u32[]{:S(2)}) copy-start(bf16[272,768]{1,0:T(8,128)(2,1)S(1)} %collective-permute-done.3.refs_1_) | copy-start | bytes 1253380
  51.3 17.8 %collective-permute-start.2 = (bf16[272,768]{1,0:T(8,128)(2,1)}, bf16[272,768]{1,0:T(8,128)(2,1)}, u32[]{:S(2)}, u32[]{:S(2)}) collective-permute-start(bf16[272,768]{1,0:T(8,128)(2,1)} %get-tuple-element.20.refs_4_), channel_id=1, source_target_pairs={{24,0},{25,1},{26,2},{27,3},{28,4},{29,5},{30,6},{31,7},{0,8},{1,9... | collective-permute-start | bytes 1253384 | tf_op jit(solution)/shard_map/ppermute | solution.py:500
  66.8 2.3 %copy-start.8 = (bf16[272,768]{1,0:T(8,128)(2,1)}, bf16[272,768]{1,0:T(8,128)(2,1)S(1)}, u32[]{:S(2)}) copy-start(bf16[272,768]{1,0:T(8,128)(2,1)S(1)} %collective-permute-done.refs_0_) | copy-start | bytes 1253380
  66.9 2.3 %copy-start.9 = (bf16[272,768]{1,0:T(8,128)(2,1)}, bf16[272,768]{1,0:T(8,128)(2,1)S(1)}, u32[]{:S(2)}) copy-start(bf16[272,768]{1,0:T(8,128)(2,1)S(1)} %collective-permute-done.1.refs_1_) | copy-start | bytes 1253380
  79.1 6.8 %collective-permute-start.10 = (f32[16,512]{1,0:T(8,128)}, f32[16,512]{1,0:T(8,128)S(1)}, u32[]{:S(2)}, u32[]{:S(2)}) collective-permute-start(f32[16,512]{1,0:T(8,128)} %get-tuple-element.27), channel_id=1, source_target_pairs={{7,0},{6,1},{1,2},{0,3},{3,4},{2,5},{5,6},{4,7},{15,8},{14,9},{9,1... | collective-permute-start | bytes 98312 | tf_op jit(solution)/shard_map/ppermute | solution.py:500
  81.0 6.3 %collective-permute-start.11 = (f32[16,512]{1,0:T(8,128)}, f32[16,512]{1,0:T(8,128)S(1)}, u32[]{:S(2)}, u32[]{:S(2)}) collective-permute-start(f32[16,512]{1,0:T(8,128)} %get-tuple-element.28), channel_id=1, source_target_pairs={{4,0},{5,1},{6,2},{7,3},{0,4},{1,5},{2,6},{3,7},{12,8},{13,9},{14,... | collective-permute-start | bytes 98312 | tf_op jit(solution)/shard_map/ppermute | solution.py:500
  83.3 8.1 %collective-permute-start.12 = (f32[16,512]{1,0:T(8,128)}, f32[16,512]{1,0:T(8,128)S(1)}, u32[]{:S(2)}, u32[]{:S(2)}) collective-permute-start(f32[16,512]{1,0:T(8,128)} %get-tuple-element.29), channel_id=1, source_target_pairs={{5,0},{4,1},{7,2},{6,3},{1,4},{0,5},{3,6},{2,7},{13,8},{12,9},{15,... | collective-permute-start | bytes 98312 | tf_op jit(solution)/shard_map/ppermute | solution.py:500
  84.0 7.4 %collective-permute-start.6 = (f32[16,512]{1,0:T(8,128)}, f32[16,512]{1,0:T(8,128)S(1)}, u32[]{:S(2)}, u32[]{:S(2)}) collective-permute-start(f32[16,512]{1,0:T(8,128)} %get-tuple-element.23), channel_id=1, source_target_pairs={{1,0},{0,1},{3,2},{2,3},{5,4},{4,5},{7,6},{6,7},{9,8},{8,9},{11,10... | collective-permute-start | bytes 98312 | tf_op jit(solution)/shard_map/ppermute | solution.py:500
  84.3 7.1 %collective-permute-start.7 = (f32[16,512]{1,0:T(8,128)}, f32[16,512]{1,0:T(8,128)S(1)}, u32[]{:S(2)}, u32[]{:S(2)}) collective-permute-start(f32[16,512]{1,0:T(8,128)} %get-tuple-element.24), channel_id=1, source_target_pairs={{2,0},{3,1},{4,2},{5,3},{6,4},{7,5},{0,6},{1,7},{10,8},{11,9},{12,... | collective-permute-start | bytes 98312 | tf_op jit(solution)/shard_map/ppermute | solution.py:500
  86.0 5.6 %copy-start.1 = (f32[16,512]{1,0:T(8,128)}, f32[16,512]{1,0:T(8,128)S(1)}, u32[]{:S(2)}) copy-start(f32[16,512]{1,0:T(8,128)S(1)} %collective-permute-done.10.refs_5_) | copy-start | bytes 98308
  86.0 5.5 %collective-permute-start.8 = (f32[16,512]{1,0:T(8,128)}, f32[16,512]{1,0:T(8,128)S(1)}, u32[]{:S(2)}, u32[]{:S(2)}) collective-permute-start(f32[16,512]{1,0:T(8,128)} %get-tuple-element.25), channel_id=1, source_target_pairs={{3,0},{2,1},{5,2},{4,3},{7,4},{6,5},{1,6},{0,7},{11,8},{10,9},{13,... | collective-permute-start | bytes 98312 | tf_op jit(solution)/shard_map/ppermute | solution.py:500
  87.3 4.3 %copy-start.2 = (f32[16,512]{1,0:T(8,128)}, f32[16,512]{1,0:T(8,128)S(1)}, u32[]{:S(2)}) copy-start(f32[16,512]{1,0:T(8,128)S(1)} %collective-permute-done.11.refs_6_) | copy-start | bytes 98308
  87.3 4.2 %collective-permute-start.9 = (f32[16,512]{1,0:T(8,128)}, f32[16,512]{1,0:T(8,128)S(1)}, u32[]{:S(2)}, u32[]{:S(2)}) collective-permute-start(f32[16,512]{1,0:T(8,128)} %get-tuple-element.26), channel_id=1, source_target_pairs={{6,0},{7,1},{0,2},{1,3},{2,4},{3,5},{4,6},{5,7},{14,8},{15,9},{8,1... | collective-permute-start | bytes 98312 | tf_op jit(solution)/shard_map/ppermute | solution.py:500
  87.6 0.8 copy-start
  91.4 0.6 copy-start.3
  91.5 0.6 copy-start.4
  91.5 0.6 copy-start.5
  91.5 0.6 copy-start.6
  91.5 0.6 copy-start.7
Sparse Core Ops, SparseCore 0:
  9.7 44.4 all-gather.1
